TPU v7x, 32 devices: a whole 2x2x4 slice. The times are simulated.
32 devices in a mesh: row: 4 (over y, x), col: 8 (over z, core).
Axes of the slice: x: 2, y: 2, z: 4, core: 2. Of those that a mesh axis runs over, the one named last changes fastest.
Arguments:
- tokens: bfloat16 [8192, 1024], P(('col', 'row')), may hold values from -6 to 6
- first_gain: float32 [1024], replicated, may hold values from 0.5 to 1.5
- query_weight: bfloat16 [1024, 1024], P('col', 'row'), may hold values from -0.1875 to 0.1875
- latent_weight: bfloat16 [1024, 512], P('col', 'row'), may hold values from -0.1875 to 0.1875
- key_weight: bfloat16 [256, 1024], P('col', 'row'), may hold values from -0.375 to 0.375
- value_weight: bfloat16 [256, 1024], P('col', 'row'), may hold values from -0.375 to 0.375
- output_weight: bfloat16 [1024, 1024], P('row', 'col'), may hold values from -3 to 3
- second_gain: float32 [1024], replicated, may hold values from 0.5 to 1.5
- gate_weight: bfloat16 [1024, 2816], P('col', 'row'), may hold values from -0.1875 to 0.1875
- up_weight: bfloat16 [1024, 2816], P('col', 'row'), may hold values from -0.1875 to 0.1875
- down_weight: bfloat16 [2816, 1024], P('row', 'col'), may hold values from -0.109375 to 0.109375
- block_order: int32 [8], replicated, may hold values from 0 to 7, as said below
- cotangent: bfloat16 [8192, 1024], P(('col', 'row')), may hold values from -6 to 6
Outputs:
- layer_output: float32 [8192, 1024], P(('col', 'row'))
- input_gradient: float32 [8192, 1024], P(('col', 'row'))
- first_gain_gradient: float32 [1024], replicated
- query_gradient: float32 [1024, 1024], P('col', 'row')
- latent_gradient: float32 [1024, 512], P('col', 'row')
- key_gradient: float32 [256, 1024], P('col', 'row')
- value_gradient: float32 [256, 1024], P('col', 'row')
- output_gradient: float32 [1024, 1024], P('row', 'col')
- second_gain_gradient: float32 [1024], replicated
- gate_gradient: float32 [1024, 2816], P('col', 'row')
- up_gradient: float32 [1024, 2816], P('col', 'row')
- down_gradient: float32 [2816, 1024], P('row', 'col')
Inputs may be any that keep to these rules, and one draw needn't show every extreme that they name: Each value appears once; block c holds part block_order[c] % 8 of the prompt of group block_order[c] // 8; the 8 blocks of one group are the aligned run of blocks k * 8 to (k + 1) * 8 - 1 for some k.
All inputs are finite; a program needn't handle non-finite values.
Results may differ from a plain program's by a relative error of at most 0.024.
Values may be sent and summed in bfloat16 or wider, within the bound.
No kernel may reach another device: no remote copies, remote signals or barrier semaphores. Data moves between devices by JAX's collectives and lax.ppermute only.
A program may use at most 256 MiB of HBM per device.

v0:
```python
import jax
import jax.numpy as jnp
from jax import lax
from jax.sharding import PartitionSpec as P

HEAD_DIM = 64
LATENT_HEADS = 2
LATENT = 256
PROMPT = 4096
CONT = 512


epsilon = 1e-05
masked_value = -1e30


def swapped(block, axis, distance):
    count = lax.axis_size(axis)
    route = []
    for low in range(count):
        high = low | 1 << distance
        if high != low and high < count:
            route += [(low, high), (high, low)]
    return lax.ppermute(block, axis, route)


def matmul(left, right):
    return jnp.dot(left, right, preferred_element_type=jnp.float32)


def times_transposed(left, right):
    return lax.dot_general(
        left, right, (((1,), (1,)), ((), ())), preferred_element_type=jnp.float32
    )


def transposed_times(left, right):
    return lax.dot_general(
        left, right, (((0,), (0,)), ((), ())), preferred_element_type=jnp.float32
    )


def norm_forward(rows, gain):
    scale = lax.rsqrt(jnp.mean(rows * rows, axis=-1, keepdims=True) + epsilon)
    return (rows * scale * gain, scale)


def norm_backward(rows, scale, gain, grad_out):
    normal = rows * scale
    gain_term = jnp.sum(grad_out * normal, axis=0)
    inner = grad_out * gain
    grad_rows = scale * (inner - normal * jnp.mean(inner * normal, axis=-1, keepdims=True))
    return (grad_rows, gain_term)


def gather_tokens(rows):
    return lax.all_gather(rows, "row", axis=0, tiled=True)


def gather_grads(rows):
    return lax.all_gather(rows, "row", axis=0, tiled=True)


def sum_rows(part):
    return lax.psum_scatter(
        part.astype(jnp.bfloat16), "row", scatter_dimension=0, tiled=True
    ).astype(jnp.float32)


def sum_inputs(part):
    return lax.psum_scatter(
        part.astype(jnp.bfloat16), "row", scatter_dimension=0, tiled=True
    ).astype(jnp.float32)


def expand_heads(latent_all, weight):
    block = latent_all.shape[0]
    shaped = latent_all.reshape(block, LATENT_HEADS, LATENT)
    table = weight.reshape(LATENT, -1, LATENT_HEADS, HEAD_DIM)
    return jnp.einsum("tgl,lagd->tagd", shaped, table, preferred_element_type=jnp.float32).reshape(
        block, -1
    )


def collapse_heads(grad, weight):
    block = grad.shape[0]
    shaped = grad.reshape(block, -1, LATENT_HEADS, HEAD_DIM)
    table = weight.reshape(LATENT, -1, LATENT_HEADS, HEAD_DIM)
    return jnp.einsum("tagd,lagd->tgl", shaped, table, preferred_element_type=jnp.float32).reshape(
        block, LATENT_HEADS * LATENT
    )


def weight_term(latent_all, grad):
    block = latent_all.shape[0]
    shaped = latent_all.reshape(block, LATENT_HEADS, LATENT)
    grads = grad.reshape(block, -1, LATENT_HEADS, HEAD_DIM)
    return jnp.einsum("tgl,tagd->lagd", shaped, grads, preferred_element_type=jnp.float32).reshape(
        LATENT, -1
    )


def key_layout(block_order, block, portion):
    portions = PROMPT // portion
    ident = block_order[lax.axis_index("col")]
    group = ident // portions
    place = ident % portions
    slots = jnp.arange(block_order.shape[0], dtype=jnp.int32)
    sources = [
        jnp.sum(jnp.where(block_order == group * portions + part, slots, 0))
        for part in range(portions)
    ]
    rows = jnp.arange(block, dtype=jnp.int32)[:, None]
    cols = jnp.arange(portion, dtype=jnp.int32)[None, :]
    following = rows >= portion
    masks = [
        following | (part * portion + cols <= place * portion + rows) for part in range(portions)
    ]
    later = rows - portion
    masks.append(following & (later // CONT == cols // CONT) & (cols <= later))
    return (sources, masks)


def key_blocks(prompt_rows, own_rows, sources, base, portion, heads_here):
    blocks = [
        lax.dynamic_slice_in_dim(prompt_rows, (source - base) * portion, portion, 0).reshape(
            portion, heads_here, HEAD_DIM
        )
        for source in sources
    ]
    blocks.append(own_rows[portion:].reshape(portion, heads_here, HEAD_DIM))
    return blocks


def block_scores(queries, keys, mask):
    raw = jnp.einsum(
        "qhd,khd->hqk", queries, keys, preferred_element_type=jnp.float32
    ) * HEAD_DIM ** (-0.5)
    return jnp.where(mask[None], raw, masked_value)


def attend(queries, key_list, value_list, masks):
    first = block_scores(queries, key_list[0], masks[0])
    top = jnp.max(first, axis=-1, keepdims=True)
    total = jnp.sum(jnp.exp(first - top), axis=-1, keepdims=True)
    for keys, mask in zip(key_list[1:], masks[1:]):
        scores = block_scores(queries, keys, mask)
        merged = jnp.maximum(top, jnp.max(scores, axis=-1, keepdims=True))
        total = total * jnp.exp(top - merged) + jnp.sum(
            jnp.exp(scores - merged), axis=-1, keepdims=True
        )
        top = merged
    log_total = top + jnp.log(total)
    result = jnp.zeros(queries.shape, jnp.float32)
    for keys, values, mask in zip(key_list, value_list, masks):
        probs = jnp.exp(block_scores(queries, keys, mask) - log_total).astype(jnp.bfloat16)
        result = result + jnp.einsum(
            "hqk,khd->qhd", probs, values, preferred_element_type=jnp.float32
        )
    return (result, log_total)


def attend_back(queries, key_list, value_list, masks, log_total, result, out_grad):
    inner = jnp.transpose(jnp.sum(out_grad.astype(jnp.float32) * result, axis=-1))[:, :, None]
    scale = HEAD_DIM ** (-0.5)
    query_grad = jnp.zeros(queries.shape, jnp.float32)
    key_grads = []
    value_grads = []
    for keys, values, mask in zip(key_list, value_list, masks):
        probs = jnp.exp(block_scores(queries, keys, mask) - log_total)
        dprobs = jnp.einsum("qhd,khd->hqk", out_grad, values, preferred_element_type=jnp.float32)
        score_grad = (probs * (dprobs - inner)).astype(jnp.bfloat16)
        query_grad = (
            query_grad
            + jnp.einsum("hqk,khd->qhd", score_grad, keys, preferred_element_type=jnp.float32)
            * scale
        )
        key_grads.append(
            jnp.einsum("hqk,qhd->khd", score_grad, queries, preferred_element_type=jnp.float32)
            * scale
        )
        value_grads.append(
            jnp.einsum(
                "hqk,qhd->khd",
                probs.astype(jnp.bfloat16),
                out_grad,
                preferred_element_type=jnp.float32,
            )
        )
    return (query_grad, key_grads, value_grads)


def bit_of(value, bit):
    return value // (1 << bit) % 2


def forward(tokens, first_gain, second_gain, weights, block_order):
    full = (
        lax.all_gather(weights[0], "col", axis=0, tiled=True),
        lax.all_gather(weights[1], "col", axis=0, tiled=True),
        lax.all_gather(weights[2], "col", axis=0, tiled=True),
        lax.all_gather(weights[3], "col", axis=0, tiled=True),
        lax.all_gather(weights[4], "col", axis=1, tiled=True),
        lax.all_gather(weights[5], "col", axis=0, tiled=True),
        lax.all_gather(weights[6], "col", axis=0, tiled=True),
        lax.all_gather(weights[7], "col", axis=1, tiled=True),
    )
    query_full, latent_full, key_full, value_full, output_full, gate_full, up_full, down_full = full
    rows = tokens.astype(jnp.float32)
    normed, first_scale = norm_forward(rows, first_gain)
    normed_block = gather_tokens(normed.astype(jnp.bfloat16))
    block = normed_block.shape[0]
    portion = block // 2
    portions = PROMPT // portion
    heads_here = query_full.shape[1] // HEAD_DIM
    queries = matmul(normed_block, query_full).astype(jnp.bfloat16)
    latent_part = matmul(normed_block, latent_full).astype(jnp.bfloat16)
    latent_all = lax.all_gather(latent_part, "row", axis=1, tiled=True)
    keys = expand_heads(latent_all, key_full).astype(jnp.bfloat16)
    values = expand_heads(latent_all, value_full).astype(jnp.bfloat16)
    column = lax.axis_index("col")
    held = jnp.stack([keys[:portion], values[:portion]], axis=0)
    for bit in range(portions.bit_length() - 1):
        other = swapped(held, "col", bit)
        upper = bit_of(column, bit) == 1
        held = jnp.where(
            upper, jnp.concatenate([other, held], axis=1), jnp.concatenate([held, other], axis=1)
        )
    prompt_keys = held[0]
    prompt_values = held[1]
    base = column // portions * portions
    sources, masks = key_layout(block_order, block, portion)
    key_list = key_blocks(prompt_keys, keys, sources, base, portion, heads_here)
    value_list = key_blocks(prompt_values, values, sources, base, portion, heads_here)
    query_heads = queries.reshape(block, heads_here, HEAD_DIM)
    result, log_total = attend(query_heads, key_list, value_list, masks)
    attended = result.reshape(block, heads_here * HEAD_DIM).astype(jnp.bfloat16)
    hidden = rows + sum_rows(matmul(attended, output_full))
    normed2, second_scale = norm_forward(hidden, second_gain)
    normed2_block = gather_tokens(normed2.astype(jnp.bfloat16))
    gate = matmul(normed2_block, gate_full)
    up = matmul(normed2_block, up_full)
    act = (jax.nn.silu(gate) * up).astype(jnp.bfloat16)
    layer = hidden + sum_rows(matmul(act, down_full))
    saved = (
        full,
        rows,
        first_scale,
        normed_block,
        query_heads,
        latent_all,
        keys,
        values,
        prompt_keys,
        prompt_values,
        base,
        log_total,
        result,
        attended,
        hidden,
        second_scale,
        normed2_block,
        gate,
        up,
        act,
    )
    return (layer, saved)


def per_device(
    tokens,
    first_gain,
    query_weight,
    latent_weight,
    key_weight,
    value_weight,
    output_weight,
    second_gain,
    gate_weight,
    up_weight,
    down_weight,
    block_order,
    cotangent,
):
    weights = (
        query_weight,
        latent_weight,
        key_weight,
        value_weight,
        output_weight,
        gate_weight,
        up_weight,
        down_weight,
    )
    layer, saved = forward(tokens, first_gain, second_gain, weights, block_order)
    saved = forward(tokens, first_gain, second_gain, weights, block_order)[1]
    (
        full,
        rows,
        first_scale,
        normed_block,
        query_heads,
        latent_all,
        keys,
        values,
        prompt_keys,
        prompt_values,
        base,
        log_total,
        result,
        attended,
        hidden,
        second_scale,
        normed2_block,
        gate,
        up,
        act,
    ) = saved
    query_full, latent_full, key_full, value_full, output_full, gate_full, up_full, down_full = full
    block = normed_block.shape[0]
    portion = block // 2
    portions = PROMPT // portion
    heads_here = query_full.shape[1] // HEAD_DIM
    width = heads_here * HEAD_DIM
    gradient = cotangent.astype(jnp.float32)
    cot_block = gather_grads(cotangent)
    act_grad = times_transposed(cot_block, down_full)
    down_term = transposed_times(act, cot_block)
    sigma = jax.nn.sigmoid(gate)
    gate_grad = (act_grad * up * sigma * (1.0 + gate * (1.0 - sigma))).astype(jnp.bfloat16)
    up_grad = (act_grad * gate * sigma).astype(jnp.bfloat16)
    normed2_grad = sum_inputs(
        times_transposed(gate_grad, gate_full) + times_transposed(up_grad, up_full)
    )
    gate_term = transposed_times(normed2_block, gate_grad)
    up_term = transposed_times(normed2_block, up_grad)
    norm2_grad, second_gain_term = norm_backward(hidden, second_scale, second_gain, normed2_grad)
    hidden_grad = gradient + norm2_grad
    branch_block = gather_grads(hidden_grad.astype(jnp.bfloat16))
    attended_grad = times_transposed(branch_block, output_full).astype(jnp.bfloat16)
    output_term = transposed_times(attended, branch_block)
    sources, masks = key_layout(block_order, block, portion)
    key_list = key_blocks(prompt_keys, keys, sources, base, portion, heads_here)
    value_list = key_blocks(prompt_values, values, sources, base, portion, heads_here)
    out_grad = attended_grad.reshape(block, heads_here, HEAD_DIM)
    query_grad, key_grads, value_grads = attend_back(
        query_heads, key_list, value_list, masks, log_total, result, out_grad
    )
    column = lax.axis_index("col")
    buffer = jnp.zeros((2, portions * portion, width), jnp.float32)
    for index, source in enumerate(sources):
        pair = jnp.stack(
            [key_grads[index].reshape(portion, width), value_grads[index].reshape(portion, width)],
            axis=0,
        )
        buffer = lax.dynamic_update_slice_in_dim(buffer, pair, (source - base) * portion, 1)
    for bit in reversed(range(portions.bit_length() - 1)):
        half = buffer.shape[1] // 2
        lower = buffer[:, :half]
        higher = buffer[:, half:]
        upper = bit_of(column, bit) == 1
        keep = jnp.where(upper, higher, lower)
        outgoing = jnp.where(upper, lower, higher)
        buffer = keep + swapped(outgoing.astype(jnp.bfloat16), "col", bit).astype(outgoing.dtype)
    prompt_key_grad = buffer[0]
    prompt_value_grad = buffer[1]
    key_grad = jnp.concatenate(
        [prompt_key_grad, key_grads[-1].reshape(portion, width)], axis=0
    ).astype(jnp.bfloat16)
    value_grad = jnp.concatenate(
        [prompt_value_grad, value_grads[-1].reshape(portion, width)], axis=0
    ).astype(jnp.bfloat16)
    query_low = query_grad.reshape(block, width).astype(jnp.bfloat16)
    latent_terms = collapse_heads(key_grad, key_full) + collapse_heads(value_grad, value_full)
    key_term = weight_term(latent_all, key_grad)
    value_term = weight_term(latent_all, value_grad)
    latent_grad = lax.psum_scatter(
        latent_terms.astype(jnp.bfloat16), "row", scatter_dimension=1, tiled=True
    )
    normed_grad = sum_inputs(
        times_transposed(query_low, query_full) + times_transposed(latent_grad, latent_full)
    )
    query_term = transposed_times(normed_block, query_low)
    latent_term = transposed_times(normed_block, latent_grad)
    norm1_grad, first_gain_term = norm_backward(rows, first_scale, first_gain, normed_grad)
    input_gradient = hidden_grad + norm1_grad
    terms = (
        query_term,
        latent_term,
        key_term,
        value_term,
        output_term,
        gate_term,
        up_term,
        down_term,
    )
    summed = (
        lax.psum_scatter(
            terms[0].astype(jnp.bfloat16), "col", scatter_dimension=0, tiled=True
        ).astype(jnp.float32),
        lax.psum_scatter(
            terms[1].astype(jnp.bfloat16), "col", scatter_dimension=0, tiled=True
        ).astype(jnp.float32),
        lax.psum_scatter(
            terms[2].astype(jnp.bfloat16), "col", scatter_dimension=0, tiled=True
        ).astype(jnp.float32),
        lax.psum_scatter(
            terms[3].astype(jnp.bfloat16), "col", scatter_dimension=0, tiled=True
        ).astype(jnp.float32),
        lax.psum_scatter(
            terms[4].astype(jnp.bfloat16), "col", scatter_dimension=1, tiled=True
        ).astype(jnp.float32),
        lax.psum_scatter(
            terms[5].astype(jnp.bfloat16), "col", scatter_dimension=0, tiled=True
        ).astype(jnp.float32),
        lax.psum_scatter(
            terms[6].astype(jnp.bfloat16), "col", scatter_dimension=0, tiled=True
        ).astype(jnp.float32),
        lax.psum_scatter(
            terms[7].astype(jnp.bfloat16), "col", scatter_dimension=1, tiled=True
        ).astype(jnp.float32),
    )
    first_total, second_total = lax.psum((first_gain_term, second_gain_term), ("row", "col"))
    return (
        layer,
        input_gradient,
        first_total,
        summed[0],
        summed[1],
        summed[2],
        summed[3],
        summed[4],
        second_total,
        summed[5],
        summed[6],
        summed[7],
    )


def solution(mesh):
    placed = (
        P(("col", "row"), None),
        P(),
        P("col", "row"),
        P("col", "row"),
        P("col", "row"),
        P("col", "row"),
        P("row", "col"),
        P(),
        P("col", "row"),
        P("col", "row"),
        P("row", "col"),
        P(),
        P(("col", "row"), None),
    )
    return jax.shard_map(
        per_device,
        mesh=mesh,
        in_specs=placed,
        out_specs=(
            P(("col", "row"), None),
            P(("col", "row"), None),
            P(),
            P("col", "row"),
            P("col", "row"),
            P("col", "row"),
            P("col", "row"),
            P("row", "col"),
            P(),
            P("col", "row"),
            P("col", "row"),
            P("row", "col"),
        ),
        check_vma=False,
    )
```

profile of v0, /device:TPU:0, one launch (start us, length us, event | category | flops | bytes accessed | tf_op | source)
XLA Modules:
  0.0 1193.7 jit_solution(16807473162914532227)
XLA Ops:
  12.0 16.1 %all_gather.51 = bf16[1024,128]{1,0:T(8,128)(2,1)S(1)} all-gather(bf16[128,128]{1,0:T(8,128)(2,1)} %param.16), channel_id=1, replica_groups=mesh['row'=4,'col'=8] {'col'}, dimensions={0}, use_global_device_ids=true | all-gather | bytes 294912 | tf_op jit(solution)/shard_map/all_gather | solution.py:200
  28.1 21.9 %all-gather.9.cloned.1.call-done = bf16[1024,1024]{1,0:T(8,128)(2,1)} async-done(((bf16[256,1024]{1,0:T(8,128)(2,1)}), bf16[1024,1024]{1,0:T(8,128)(2,1)}) %all-gather.9.cloned.1.call-update) | async-done | bytes 2097168 | tf_op jit(solution)/shard_map/all_gather | solution.py:57
  53.0 14.3 %all_gather.53 = bf16[256,256]{1,0:T(8,128)(2,1)S(1)} all-gather(bf16[32,256]{1,0:T(8,128)(2,1)} %param.17), channel_id=1, replica_groups=mesh['row'=4,'col'=8] {'col'}, dimensions={0}, use_global_device_ids=true | all-gather | bytes 147456 | tf_op jit(solution)/shard_map/all_gather | solution.py:201
  67.4 14.2 %all_gather.54 = bf16[256,256]{1,0:T(8,128)(2,1)S(1)} all-gather(bf16[32,256]{1,0:T(8,128)(2,1)} %param.18), channel_id=1, replica_groups=mesh['row'=4,'col'=8] {'col'}, dimensions={0}, use_global_device_ids=true | all-gather | bytes 147456 | tf_op jit(solution)/shard_map/all_gather | solution.py:202
  96.6 32.0 %all_gather.55 = bf16[1024,256]{1,0:T(8,128)(2,1)} all-gather(bf16[128,256]{1,0:T(8,128)(2,1)S(1)} %copy-done.101), channel_id=1, replica_groups=mesh['row'=4,'col'=8] {'col'}, dimensions={0}, use_global_device_ids=true | all-gather | bytes 589824 | tf_op jit(solution)/shard_map/all_gather | solution.py:199
  138.9 95.8 %all_gather.56 = bf16[256,1024]{1,0:T(8,128)(2,1)S(1)} all-gather(bf16[256,128]{1,0:T(8,128)(2,1)S(1)} %copy-done.102), channel_id=1, replica_groups=mesh['row'=4,'col'=8] {'col'}, dimensions={1}, use_global_device_ids=true | all-gather | bytes 589824 | tf_op jit(solution)/shard_map/all_gather | solution.py:203
  354.8 33.4 %reduce-scatter.26.cloned.1.call-done = bf16[256,1024]{1,0:T(8,128)(2,1)} async-done(((bf16[1024,1024]{1,0:T(8,128)(2,1)}), bf16[256,1024]{1,0:T(8,128)(2,1)}) %reduce-scatter.26.cloned.1.call-update) | async-done | bytes 524304 | tf_op jit(solution)/shard_map/reduce_scatter | solution.py:65
  394.2 32.5 %all-gather.13.cloned.1.call-done = bf16[1024,1024]{1,0:T(8,128)(2,1)} async-done(((bf16[256,1024]{1,0:T(8,128)(2,1)}), bf16[1024,1024]{1,0:T(8,128)(2,1)}) %all-gather.13.cloned.1.call-update) | async-done | bytes 2097168 | tf_op jit(solution)/shard_map/all_gather | solution.py:57
  431.9 22.7 %all-gather.15.cloned.1.call-done = bf16[1024,704]{0,1:T(8,128)(2,1)} async-done(((bf16[128,704]{0,1:T(8,128)(2,1)}), bf16[1024,704]{0,1:T(8,128)(2,1)}) %all-gather.15.cloned.1.call-update) | async-done | bytes 1441808 | tf_op jit(solution)/shard_map/all_gather | solution.py:204
  459.9 21.3 %all-gather.19.cloned.1.call-done = bf16[704,1024]{1,0:T(8,128)(2,1)} async-done(((bf16[704,128]{1,0:T(8,128)(2,1)}), bf16[704,1024]{1,0:T(8,128)(2,1)}) %all-gather.19.cloned.1.call-update) | async-done | bytes 1441808 | tf_op jit(solution)/shard_map/all_gather | solution.py:206
  481.2 35.5 %all-gather.21.cloned.1.call-done = bf16[1024,1024]{1,0:T(8,128)(2,1)} async-done(((bf16[256,1024]{1,0:T(8,128)(2,1)}), bf16[1024,1024]{1,0:T(8,128)(2,1)}) %all-gather.21.cloned.1.call-update) | async-done | bytes 2097168 | tf_op jit(solution)/shard_map/all_gather | solution.py:61
  530.1 35.3 %reduce-scatter.30.cloned.1.call-done = bf16[256,1024]{1,0:T(8,128)(2,1)} async-done(((bf16[1024,1024]{1,0:T(8,128)(2,1)}), bf16[256,1024]{1,0:T(8,128)(2,1)}) %reduce-scatter.30.cloned.1.call-update) | async-done | bytes 524304 | tf_op jit(solution)/shard_map/reduce_scatter | solution.py:71
  570.8 35.1 %all-gather.23.cloned.1.call-done = bf16[1024,1024]{1,0:T(8,128)(2,1)} async-done(((bf16[256,1024]{1,0:T(8,128)(2,1)}), bf16[1024,1024]{1,0:T(8,128)(2,1)}) %all-gather.23.cloned.1.call-update) | async-done | bytes 2097168 | tf_op jit(solution)/shard_map/all_gather | solution.py:61
  689.0 90.6 %collective-permute-done.3 = bf16[2,2048,256]{1,2,0:T(8,128)(2,1)S(1)} collective-permute-done((bf16[2,2048,256]{1,2,0:T(8,128)(2,1)S(1)}, bf16[2,2048,256]{1,2,0:T(8,128)(2,1)S(1)}, u32[]{:S(2)}, u32[]{:S(2)}) %collective-permute-start.3) | collective-permute-done | bytes 2097184 | tf_op jit(solution)/shard_map/ppermute | solution.py:24
  789.7 17.7 %collective-permute-done.4 = bf16[2,1024,256]{1,2,0:T(8,128)(2,1)S(1)} collective-permute-done((bf16[2,1024,256]{1,2,0:T(8,128)(2,1)S(1)}, bf16[2,1024,256]{1,2,0:T(8,128)(2,1)S(1)}, u32[]{:S(2)}, u32[]{:S(2)}) %collective-permute-start.4) | collective-permute-done | bytes 1048608 | tf_op jit(solution)/shard_map/ppermute | solution.py:24
  880.4 32.7 %reduce-scatter.48.cloned.1.call-done = bf16[128,704]{1,0:T(8,128)(2,1)} async-done(((bf16[1024,704]{1,0:T(8,128)(2,1)}), bf16[128,704]{1,0:T(8,128)(2,1)}) %reduce-scatter.48.cloned.1.call-update) | async-done | bytes 180240
  914.9 32.8 %reduce-scatter.46.cloned.1.call-done = bf16[128,704]{1,0:T(8,128)(2,1)} async-done(((bf16[1024,704]{1,0:T(8,128)(2,1)}), bf16[128,704]{1,0:T(8,128)(2,1)}) %reduce-scatter.46.cloned.1.call-update) | async-done | bytes 180240
  949.6 30.1 %reduce-scatter.44.cloned.1.call-done = bf16[128,256]{1,0:T(8,128)(2,1)} async-done(((bf16[1024,256]{1,0:T(8,128)(2,1)}), bf16[128,256]{1,0:T(8,128)(2,1)}) %reduce-scatter.44.cloned.1.call-update) | async-done | bytes 65552
  981.3 30.0 %reduce-scatter.36.cloned.1.call-done = bf16[128,256]{1,0:T(8,128)(2,1)} async-done(((bf16[1024,256]{1,0:T(8,128)(2,1)}), bf16[128,256]{1,0:T(8,128)(2,1)}) %reduce-scatter.36.cloned.1.call-update) | async-done | bytes 65552 | tf_op jit(solution)/shard_map/reduce_scatter | solution.py:398
  1012.8 29.5 %reduce-scatter.42.cloned.1.call-done = bf16[32,256]{1,0:T(8,128)(2,1)} async-done(((bf16[256,256]{1,0:T(8,128)(2,1)}), bf16[32,256]{1,0:T(8,128)(2,1)}) %reduce-scatter.42.cloned.1.call-update) | async-done | bytes 16400
  1043.9 29.2 %reduce-scatter.40.cloned.1.call-done = bf16[32,256]{1,0:T(8,128)(2,1)} async-done(((bf16[256,256]{1,0:T(8,128)(2,1)}), bf16[32,256]{1,0:T(8,128)(2,1)}) %reduce-scatter.40.cloned.1.call-update) | async-done | bytes 16400
  1074.6 30.3 %reduce-scatter.38.cloned.1.call-done = bf16[128,128]{1,0:T(8,128)(2,1)} async-done(((bf16[1024,128]{1,0:T(8,128)(2,1)}), bf16[128,128]{1,0:T(8,128)(2,1)}) %reduce-scatter.38.cloned.1.call-update) | async-done | bytes 32784 | tf_op jit(solution)/shard_map/reduce_scatter | solution.py:401
  1106.3 35.0 %reduce-scatter.34.cloned.1.call-done = bf16[256,1024]{1,0:T(8,128)(2,1)} async-done(((bf16[1024,1024]{1,0:T(8,128)(2,1)}), bf16[256,1024]{1,0:T(8,128)(2,1)}) %reduce-scatter.34.cloned.1.call-update) | async-done | bytes 524304 | tf_op jit(solution)/shard_map/reduce_scatter | solution.py:71
  1142.8 40.1 %all-reduce = (f32[1024]{0:T(1024)}, f32[1024]{0:T(1024)}) all-reduce(f32[1024]{0:T(1024)S(1)} %get-tuple-element.38, f32[1024]{0:T(1024)S(1)} %copy-done.108), channel_id=1, replica_groups=mesh['row'=4,'col'=8] {'row','col'}, use_global_device_ids=true, to_apply=%region_37.38 | all-reduce | flops 2048 | bytes 16384 | tf_op jit(solution)/shard_map/psum | solution.py:423
  (523 shorter events, 359.6 us)
Async XLA Ops:
  8.0 42.0 %all-gather.9.cloned.1.call-start = ((), (), s32[]{:S(2)}) async-start(), calls=%async_computation.13 | async-start | bytes 2621440 | tf_op jit(solution)/shard_map/all_gather | solution.py:57
  11.9 69.9 %all-gather.11.cloned.1.call-start = ((), (), s32[]{:S(2)}) async-start(), calls=%async_computation.14 | async-start | bytes 1310720 | tf_op jit(solution)/shard_map/all_gather | solution.py:218
  53.0 335.2 %reduce-scatter.26.cloned.1.call-start = ((), (), s32[]{:S(2)}) async-start(), calls=%async_computation.15 | async-start | bytes 2621440 | tf_op jit(solution)/shard_map/reduce_scatter | solution.py:65
  91.1 37.5 %collective-permute-start.1 = (bf16[2,1024,256]{1,2,0:T(8,128)(2,1)}, bf16[2,1024,256]{1,2,0:T(8,128)(2,1)}, u32[]{:S(2)}, u32[]{:S(2)}) collective-permute-start(bf16[2,1024,256]{1,2,0:T(8,128)(2,1)} %maximum_select_fusion.2), channel_id=1, source_target_pairs={{0,2},{2,0},{1,3},{3,1},{4,6},{6,4},{5,7},{7,5},{8,10},{10,8},{9,1... | collective-permute-start | bytes 3145736 | tf_op jit(solution)/shard_map/ppermute | solution.py:24
  133.0 110.4 %collective-permute-start.2 = (bf16[2,2048,256]{1,2,0:T(8,128)(2,1)}, bf16[2,2048,256]{1,2,0:T(8,128)(2,1)}, u32[]{:S(2)}, u32[]{:S(2)}) collective-permute-start(bf16[2,2048,256]{1,2,0:T(8,128)(2,1)} %maximum_select_fusion.1), channel_id=1, source_target_pairs={{0,4},{4,0},{1,5},{5,1},{2,6},{6,2},{3,7},{7,3},{8,12},{12,8},{9,1... | collective-permute-start | bytes 6291464 | tf_op jit(solution)/shard_map/ppermute | solution.py:24
  354.2 40.0 %all-gather.17.cloned.1.call-start = ((), (), s32[]{:S(2)}) async-start(), calls=%async_computation.18 | async-start | bytes 1622016 | tf_op jit(solution)/shard_map/all_gather | solution.py:205
  354.7 72.0 %all-gather.13.cloned.1.call-start = ((), (), s32[]{:S(2)}) async-start(), calls=%async_computation.16 | async-start | bytes 2621440 | tf_op jit(solution)/shard_map/all_gather | solution.py:57
  391.5 63.1 %all-gather.15.cloned.1.call-start = ((), (), s32[]{:S(2)}) async-start(), calls=%async_computation.17 | async-start | bytes 1622016 | tf_op jit(solution)/shard_map/all_gather | solution.py:204
  392.1 89.1 %all-gather.19.cloned.1.call-start = ((), (), s32[]{:S(2)}) async-start(), calls=%async_computation.19 | async-start | bytes 1622016 | tf_op jit(solution)/shard_map/all_gather | solution.py:206
  392.9 123.9 %all-gather.21.cloned.1.call-start = ((), (), s32[]{:S(2)}) async-start(), calls=%async_computation.21 | async-start | bytes 2621440 | tf_op jit(solution)/shard_map/all_gather | solution.py:61
  393.6 171.8 %reduce-scatter.30.cloned.1.call-start = ((), (), s32[]{:S(2)}) async-start(), calls=%async_computation.22 | async-start | bytes 2621440 | tf_op jit(solution)/shard_map/reduce_scatter | solution.py:71
  530.1 75.8 %all-gather.23.cloned.1.call-start = ((), (), s32[]{:S(2)}) async-start(), calls=%async_computation.23 | async-start | bytes 2621440 | tf_op jit(solution)/shard_map/all_gather | solution.py:61
  570.5 285.9 %reduce-scatter.32.cloned.1.call-start = ((), (), s32[]{:S(2)}) async-start(), calls=%async_computation.24 | async-start | bytes 1310720 | tf_op jit(solution)/shard_map/reduce_scatter | solution.py:377
  686.6 93.1 %collective-permute-start.3 = (bf16[2,2048,256]{1,2,0:T(8,128)(2,1)S(1)}, bf16[2,2048,256]{1,2,0:T(8,128)(2,1)S(1)}, u32[]{:S(2)}, u32[]{:S(2)}) collective-permute-start(bf16[2,2048,256]{1,2,0:T(8,128)(2,1)S(1)} %select_convert_fusion), channel_id=1, source_target_pairs={{0,4},{4,0},{1,5},{5,1},{2,6},{6,2},{3,7},{7,3},{8,12},{12,8},{9,1... | collective-permute-start | bytes 6291464 | tf_op jit(solution)/shard_map/ppermute | solution.py:24
  813.1 65.4 %reduce-scatter.50.cloned.1.call-start = ((), (), s32[]{:S(2)}) async-start(), calls=%async_computation.33 | async-start | bytes 1769472
  818.6 94.4 %reduce-scatter.48.cloned.1.call-start = ((), (), s32[]{:S(2)}) async-start(), calls=%async_computation.32 | async-start | bytes 1769472
  823.3 124.4 %reduce-scatter.46.cloned.1.call-start = ((), (), s32[]{:S(2)}) async-start(), calls=%async_computation.31 | async-start | bytes 1769472
  828.8 150.9 %reduce-scatter.44.cloned.1.call-start = ((), (), s32[]{:S(2)}) async-start(), calls=%async_computation.30 | async-start | bytes 589824
  845.0 166.3 %reduce-scatter.36.cloned.1.call-start = ((), (), s32[]{:S(2)}) async-start(), calls=%async_computation.26 | async-start | bytes 589824 | tf_op jit(solution)/shard_map/reduce_scatter | solution.py:398
  851.2 191.1 %reduce-scatter.42.cloned.1.call-start = ((), (), s32[]{:S(2)}) async-start(), calls=%async_computation.29 | async-start | bytes 147456
  853.8 219.3 %reduce-scatter.40.cloned.1.call-start = ((), (), s32[]{:S(2)}) async-start(), calls=%async_computation.28 | async-start | bytes 147456
  856.4 248.5 %reduce-scatter.38.cloned.1.call-start = ((), (), s32[]{:S(2)}) async-start(), calls=%async_computation.27 | async-start | bytes 294912 | tf_op jit(solution)/shard_map/reduce_scatter | solution.py:401
  858.9 282.3 %reduce-scatter.34.cloned.1.call-start = ((), (), s32[]{:S(2)}) async-start(), calls=%async_computation.25 | async-start | bytes 2621440 | tf_op jit(solution)/shard_map/reduce_scatter | solution.py:71
  862.9 319.9 %reduce-scatter.28.cloned.1.call-start = ((), (), s32[]{:S(2)}) async-start(), calls=%async_computation.20 | async-start | bytes 2621440 | tf_op jit(solution)/shard_map/reduce_scatter | solution.py:65
  (148 other events, 6837.2 us)
Sparse Core Ops, SparseCore 0:
  12.0 37.8 all-gather.8
  53.1 26.3 all-gather.10
  354.3 33.8 reduce-scatter.25
  530.2 35.1 reduce-scatter.29
  570.7 35.1 all-gather.22
Sparse Core Ops, SparseCore 1:
  356.2 25.0 all-gather.16
  391.6 35.0 all-gather.12
  428.2 26.4 all-gather.14
  456.2 24.9 all-gather.18
  483.1 33.6 all-gather.20
  813.2 28.8 reduce-scatter.31
  844.2 34.2 reduce-scatter.49
  880.7 32.3 reduce-scatter.47
  915.3 32.4 reduce-scatter.45
  950.0 29.6 reduce-scatter.43
  981.8 29.4 reduce-scatter.35
  1013.6 28.7 reduce-scatter.41
  1044.4 28.6 reduce-scatter.39
  1075.9 28.9 reduce-scatter.37
  1107.9 33.3 reduce-scatter.33
  1144.2 35.3 reduce-scatter.27
where the time goes:
time: 1200 us; the launch traced here: 1190 us
  waiting for transfers between devices  610 us (51%)
  matrix products  233 us (19%)
  blocking collectives  213 us (18%)
  other arithmetic  76.4 us (6%)
  local copies, waits for them, and re-layouts  27.8 us (2%)
  between operations  26 us (2%)
    unnamed x27, waiting for transfers between devices  167 us
    ppermute x6, waiting for transfers between devices, swapped(): return lax.ppermute(block, axis, route)  110 us
    all_gather x1, blocking collectives, forward(): lax.all_gather(weights[4], 'col', axis=1, tiled=True)  95.8 us
    all_gather x2, waiting for transfers between devices, gather_grads(): return lax.all_gather(rows, 'row', axis=0, tiled=True)  70.6 us
    reduce_scatter x2, waiting for transfers between devices, sum_inputs(): lax.psum_scatter(part.astype(jnp.bfloat16), 'row', scatter_dimension=0, t...  70.2 us
    all_gather x2, waiting for transfers between devices, gather_tokens(): return lax.all_gather(rows, 'row', axis=0, tiled=True)  54.4 us
    psum x1, blocking collectives, per_device(): lax.psum((first_gain_term, second_gain_term), ('row', 'col'))  40.1 us
    dot_general x9, matrix products, attend_back(): jnp.einsum('qhd,khd->hqk', out_grad, values, preferred_element_type=jnp.f...  38.7 us
  transfers between devices with their start and end apart: 27, of which 20 were waited for; matrix products, arithmetic and copies ran while one was open for 8% of the time, Pallas kernels for 0%

commit v1 on v0

v1 whole, which is shorter than its diff:
```python
import functools

import jax
import jax.numpy as jnp
from jax import lax
from jax.experimental import pallas as pl
from jax.experimental.pallas import tpu as pltpu
from jax.sharding import PartitionSpec as P

HEAD_DIM = 64
LATENT_HEADS = 2
LATENT = 256
PROMPT = 4096
CONT = 512
KEY_TILE = 512
ROW_TILE = 256

epsilon = 1e-05
masked_value = -1e30
BF16 = jnp.bfloat16
F32 = jnp.float32


def dot(left, right, left_dim, right_dim):
    return lax.dot_general(
        left, right, (((left_dim,), (right_dim,)), ((), ())), preferred_element_type=F32
    )


def norm_forward(rows, gain):
    scale = lax.rsqrt(jnp.mean(rows * rows, axis=-1, keepdims=True) + epsilon)
    return (rows * scale * gain, scale)


def norm_backward(rows, scale, gain, grad_out):
    normal = rows * scale
    gain_term = jnp.sum(grad_out * normal, axis=0)
    inner = grad_out * gain
    grad_rows = scale * (inner - normal * jnp.mean(inner * normal, axis=-1, keepdims=True))
    return (grad_rows, gain_term)


def exchange(block, mask):
    return lax.ppermute(block, "row", [(i, i ^ mask) for i in range(lax.axis_size("row"))])


def gather_pieces(rows):
    half = rows.shape[0] // 2
    low, high = rows[:half], rows[half:]
    low_x = exchange(low, 1)
    high_y = exchange(high, 2)
    low_y = exchange(jnp.concatenate([low, low_x], axis=0), 2)
    high_x = exchange(jnp.concatenate([high, high_y], axis=0), 1)
    return [
        (low, high),
        (low_x, high_x[:half]),
        (low_y[:half], high_y),
        (low_y[half:], high_x[half:]),
    ]


def gather_near(rows):
    if lax.axis_size("row") != 4:
        return lax.all_gather(rows, "row", axis=0, tiled=True)
    return jnp.concatenate([part for piece in gather_pieces(rows) for part in piece], axis=0)


def gather_true(rows):
    if lax.axis_size("row") != 4:
        return lax.all_gather(rows, "row", axis=0, tiled=True)
    count = rows.shape[0]
    here = lax.axis_index("row")
    whole = jnp.zeros((4 * count,) + rows.shape[1:], rows.dtype)
    for j, piece in enumerate(gather_pieces(rows)):
        whole = lax.dynamic_update_slice_in_dim(
            whole, jnp.concatenate(piece, axis=0), (here ^ j) * count, 0
        )
    return whole


def scatter_pieces(pieces):
    half = pieces[0].shape[0] // 2
    low = [piece[:half] for piece in pieces]
    high = [piece[half:] for piece in pieces]
    low_in = exchange(jnp.concatenate([low[2], low[3]], axis=0), 2)
    high_in = exchange(jnp.concatenate([high[1], high[3]], axis=0), 1)
    low_on = (low[1].astype(F32) + low_in[half:].astype(F32)).astype(BF16)
    high_on = (high[2].astype(F32) + high_in[half:].astype(F32)).astype(BF16)
    low_last = exchange(low_on, 1)
    high_last = exchange(high_on, 2)
    low_sum = low[0].astype(F32) + low_in[:half].astype(F32) + low_last.astype(F32)
    high_sum = high[0].astype(F32) + high_in[:half].astype(F32) + high_last.astype(F32)
    return jnp.concatenate([low_sum, high_sum], axis=0)


def scatter_near(part):
    part = part.astype(BF16)
    if lax.axis_size("row") != 4:
        return lax.psum_scatter(part, "row", scatter_dimension=0, tiled=True).astype(F32)
    count = part.shape[0] // 4
    return scatter_pieces([part[j * count : (j + 1) * count] for j in range(4)])


def scatter_true(part):
    part = part.astype(BF16)
    if lax.axis_size("row") != 4:
        return lax.psum_scatter(part, "row", scatter_dimension=0, tiled=True).astype(F32)
    count = part.shape[0] // 4
    here = lax.axis_index("row")
    return scatter_pieces(
        [lax.dynamic_slice_in_dim(part, (here ^ j) * count, count, 0) for j in range(4)]
    )


def gather_features(part):
    if lax.axis_size("row") != 4:
        return lax.all_gather(part, "row", axis=1, tiled=True)
    count = part.shape[0]
    whole = gather_true(part)
    return jnp.concatenate([whole[j * count : (j + 1) * count] for j in range(4)], axis=1)


def scatter_features(part):
    part = part.astype(BF16)
    size = lax.axis_size("row")
    if size != 4:
        return lax.psum_scatter(part, "row", scatter_dimension=1, tiled=True)
    width = part.shape[1] // size
    stacked = jnp.concatenate([part[:, j * width : (j + 1) * width] for j in range(size)], axis=0)
    return scatter_true(stacked).astype(BF16)


def all_sum(value):
    for axis in ("row", "col"):
        size = lax.axis_size(axis)
        if size & (size - 1):
            value = lax.psum(value, axis)
            continue
        bit = 1
        while bit < size:
            value = value + lax.ppermute(value, axis, [(i, i ^ bit) for i in range(size)])
            bit *= 2
    return value


def masked_heads(tile, heads):
    lanes = lax.broadcasted_iota(jnp.int32, tile.shape, 1) // HEAD_DIM
    return [jnp.where(lanes == h, tile, jnp.zeros_like(tile)) for h in range(heads)]


def one_head(ref, h, rows):
    pair = pl.ds((h // 2) * 2 * HEAD_DIM, 2 * HEAD_DIM)
    own = ref[h * HEAD_DIM : (h + 1) * HEAD_DIM, rows]
    none = jnp.zeros_like(own)
    return pair, jnp.concatenate([own, none] if h % 2 == 0 else [none, own], axis=0)


def visit_tiles(meta, step, prompt_tiles, portion, rows, body):
    place = meta[prompt_tiles]
    first_rows = portion // ROW_TILE

    def visit(index, carry):
        is_prompt = index < first_rows
        row0 = index * ROW_TILE
        position = place * portion + row0
        later = row0 - portion
        key0 = step * KEY_TILE
        on_prompt = step < prompt_tiles
        prompt_full = is_prompt & on_prompt & (key0 + KEY_TILE - 1 <= position)
        prompt_part = is_prompt & on_prompt & (key0 <= position + ROW_TILE - 1)
        full = prompt_full | (jnp.logical_not(is_prompt) & on_prompt)
        own_part = (
            jnp.logical_not(is_prompt)
            & jnp.logical_not(on_prompt)
            & (later // CONT == step - prompt_tiles)
        )
        partly = (prompt_part & jnp.logical_not(prompt_full)) | own_part
        ahead = jnp.where(is_prompt, position - key0, later % CONT)

        @pl.when(full)
        def _():
            body(index, None)

        @pl.when(partly)
        def _():
            body(index, ahead)

        return carry

    lax.fori_loop(0, rows // ROW_TILE, visit, 0)


def hide(scores, ahead):
    if ahead is None:
        return scores
    key = lax.broadcasted_iota(jnp.int32, scores.shape, 0)
    query = lax.broadcasted_iota(jnp.int32, scores.shape, 1)
    return jnp.where(key <= query + ahead, scores, masked_value)


def attend_kernel(
    meta, q_t, key_in, value_in, key_own, value_own, out, out_low, lse, keys, values_t, acc, top, total,
    *, heads, prompt_tiles, portion, rows,
):
    step = pl.program_id(0)

    @pl.when(step == 0)
    def _():
        acc[...] = jnp.zeros_like(acc)
        top[...] = jnp.full_like(top, masked_value)
        total[...] = jnp.zeros_like(total)

    @pl.when(step < prompt_tiles)
    def _():
        keys[...] = key_in[...]
        values_t[...] = value_in[...].T

    @pl.when(step >= prompt_tiles)
    def _():
        keys[...] = key_own[...]
        values_t[...] = value_own[...].T

    def body(index, ahead):
        at = pl.ds(pl.multiple_of(index * ROW_TILE, ROW_TILE), ROW_TILE)
        for h in range(heads):
            pair, query = one_head(q_t, h, at)
            scores = hide(dot(keys[:, pair], query, 1, 0), ahead)
            before = top[h : h + 1, at]
            now = jnp.maximum(before, jnp.max(scores, axis=0, keepdims=True))
            probs = jnp.exp(scores - now)
            decay = jnp.exp(before - now)
            top[h : h + 1, at] = now
            total[h : h + 1, at] = decay * total[h : h + 1, at] + jnp.sum(
                probs, axis=0, keepdims=True
            )
            mine = slice(h * HEAD_DIM, (h + 1) * HEAD_DIM)
            acc[mine, at] = decay * acc[mine, at] + dot(values_t[mine, :], probs.astype(BF16), 1, 0)

    visit_tiles(meta, step, prompt_tiles, portion, rows, body)

    @pl.when(step == pl.num_programs(0) - 1)
    def _():
        lse[...] = top[...] + jnp.log(jnp.maximum(total[...], 1e-37))
        for h in range(heads):
            mine = slice(h * HEAD_DIM, (h + 1) * HEAD_DIM)
            result = acc[mine, :] / total[h : h + 1, :]
            out[mine, :] = result
            out_low[mine, :] = result.astype(BF16)


def attend_back_kernel(
    meta, q_t, grad_t, q, grad, lse, inner, key_in, value_in, key_own, value_own,
    query_grad, prompt_grad, own_grad,
    keys, keys_t, values, queries_apart, grads_apart, query_acc, key_acc, value_acc,
    *, heads, prompt_tiles, portion, rows,
):
    step = pl.program_id(0)
    wide = heads * ROW_TILE

    @pl.when(step == 0)
    def _():
        query_acc[...] = jnp.zeros_like(query_acc)

        def spread(index, carry):
            at = pl.ds(pl.multiple_of(index * ROW_TILE, ROW_TILE), ROW_TILE)
            far = pl.ds(pl.multiple_of(index * wide, wide), wide)
            queries_apart[far, :] = jnp.concatenate(masked_heads(q[at, :], heads), axis=0)
            grads_apart[far, :] = jnp.concatenate(masked_heads(grad[at, :], heads), axis=0)
            return carry

        lax.fori_loop(0, rows // ROW_TILE, spread, 0)

    key_acc[...] = jnp.zeros_like(key_acc)
    value_acc[...] = jnp.zeros_like(value_acc)

    @pl.when(step < prompt_tiles)
    def _():
        keys[...] = key_in[...]
        keys_t[...] = key_in[...].T
        values[...] = value_in[...]

    @pl.when(step >= prompt_tiles)
    def _():
        keys[...] = key_own[...]
        keys_t[...] = key_own[...].T
        values[...] = value_own[...]

    def body(index, ahead):
        at = pl.ds(pl.multiple_of(index * ROW_TILE, ROW_TILE), ROW_TILE)
        far = pl.ds(pl.multiple_of(index * wide, wide), wide)
        all_probs = []
        all_grads = []
        for h in range(heads):
            pair, query = one_head(q_t, h, at)
            _, out_grad = one_head(grad_t, h, at)
            scores = hide(dot(keys[:, pair], query, 1, 0), ahead)
            probs = jnp.exp(scores - lse[h : h + 1, at])
            dprobs = dot(values[:, pair], out_grad, 1, 0)
            score_grad = (probs * (dprobs - inner[h : h + 1, at])).astype(BF16)
            mine = slice(h * HEAD_DIM, (h + 1) * HEAD_DIM)
            query_acc[mine, at] += dot(keys_t[mine, :], score_grad, 1, 0)
            all_probs.append(probs.astype(BF16))
            all_grads.append(score_grad)
        value_acc[...] += dot(jnp.concatenate(all_probs, axis=1), grads_apart[far, :], 1, 0)
        key_acc[...] += dot(jnp.concatenate(all_grads, axis=1), queries_apart[far, :], 1, 0)

    visit_tiles(meta, step, prompt_tiles, portion, rows, body)

    width = heads * HEAD_DIM

    @pl.when(step < prompt_tiles)
    def _():
        prompt_grad[:, :width] = key_acc[...].astype(BF16)
        prompt_grad[:, width:] = value_acc[...].astype(BF16)

    @pl.when(step >= prompt_tiles)
    def _():
        own_grad[:, :width] = key_acc[...].astype(BF16)
        own_grad[:, width:] = value_acc[...].astype(BF16)

    @pl.when(step == pl.num_programs(0) - 1)
    def _():
        query_grad[...] = (query_acc[...] * HEAD_DIM**-0.5).astype(BF16)


def whole_spec(shape):
    return pl.BlockSpec(shape, lambda step, meta: (0, 0))


def attention_specs(width, prompt_tiles):
    def prompt_map(column):
        return lambda step, meta: (meta[jnp.minimum(step, prompt_tiles - 1)], column)

    def own_map(column):
        return lambda step, meta: (jnp.maximum(step - prompt_tiles, 0), column)

    tile = (KEY_TILE, width)
    return [
        pl.BlockSpec(tile, prompt_map(0)),
        pl.BlockSpec(tile, prompt_map(1)),
        pl.BlockSpec(tile, own_map(0)),
        pl.BlockSpec(tile, own_map(1)),
    ]


def attend(meta, q_t, prompt, own):
    width, rows = q_t.shape
    heads = width // HEAD_DIM
    portion = own.shape[0]
    prompt_tiles = PROMPT // KEY_TILE
    steps = prompt_tiles + portion // KEY_TILE
    keys = (prompt.shape[0] + portion) * rows * heads * 3 // 4
    return pl.pallas_call(
        functools.partial(
            attend_kernel, heads=heads, prompt_tiles=prompt_tiles, portion=portion, rows=rows
        ),
        grid_spec=pltpu.PrefetchScalarGridSpec(
            num_scalar_prefetch=1,
            grid=(steps,),
            in_specs=[whole_spec((width, rows))] + attention_specs(width, prompt_tiles),
            out_specs=[
                whole_spec((width, rows)),
                whole_spec((width, rows)),
                whole_spec((8, rows)),
            ],
            scratch_shapes=[
                pltpu.VMEM((KEY_TILE, width), BF16),
                pltpu.VMEM((width, KEY_TILE), BF16),
                pltpu.VMEM((width, rows), F32),
                pltpu.VMEM((8, rows), F32),
                pltpu.VMEM((8, rows), F32),
            ],
        ),
        out_shape=[
            jax.ShapeDtypeStruct((width, rows), F32),
            jax.ShapeDtypeStruct((width, rows), BF16),
            jax.ShapeDtypeStruct((8, rows), F32),
        ],
        compiler_params=pltpu.CompilerParams(dimension_semantics=("arbitrary",)),
        cost_estimate=pl.CostEstimate(
            flops=keys * HEAD_DIM * 16, transcendentals=keys, bytes_accessed=8 << 20
        ),
        name="attend",
    )(meta, q_t, prompt, prompt, own, own)


def attend_back(meta, q_t, grad_t, q, grad, lse, inner, prompt, own):
    width, rows = q_t.shape
    heads = width // HEAD_DIM
    portion = own.shape[0]
    prompt_tiles = PROMPT // KEY_TILE
    steps = prompt_tiles + portion // KEY_TILE
    keys = (prompt.shape[0] + portion) * rows * heads * 3 // 4
    tall = heads * rows
    return pl.pallas_call(
        functools.partial(
            attend_back_kernel, heads=heads, prompt_tiles=prompt_tiles, portion=portion, rows=rows
        ),
        grid_spec=pltpu.PrefetchScalarGridSpec(
            num_scalar_prefetch=1,
            grid=(steps,),
            in_specs=[
                whole_spec((width, rows)),
                whole_spec((width, rows)),
                whole_spec((rows, width)),
                whole_spec((rows, width)),
                whole_spec((8, rows)),
                whole_spec((8, rows)),
            ]
            + attention_specs(width, prompt_tiles),
            out_specs=[
                whole_spec((width, rows)),
                pl.BlockSpec(
                    (KEY_TILE, 2 * width),
                    lambda step, meta: (meta[jnp.minimum(step, prompt_tiles - 1)], 0),
                ),
                pl.BlockSpec(
                    (KEY_TILE, 2 * width),
                    lambda step, meta: (jnp.maximum(step - prompt_tiles, 0), 0),
                ),
            ],
            scratch_shapes=[
                pltpu.VMEM((KEY_TILE, width), BF16),
                pltpu.VMEM((width, KEY_TILE), BF16),
                pltpu.VMEM((KEY_TILE, width), BF16),
                pltpu.VMEM((tall, width), BF16),
                pltpu.VMEM((tall, width), BF16),
                pltpu.VMEM((width, rows), F32),
                pltpu.VMEM((KEY_TILE, width), F32),
                pltpu.VMEM((KEY_TILE, width), F32),
            ],
        ),
        out_shape=[
            jax.ShapeDtypeStruct((width, rows), BF16),
            jax.ShapeDtypeStruct((PROMPT, 2 * width), BF16),
            jax.ShapeDtypeStruct((portion, 2 * width), BF16),
        ],
        compiler_params=pltpu.CompilerParams(dimension_semantics=("arbitrary",)),
        cost_estimate=pl.CostEstimate(
            flops=keys * HEAD_DIM * 40, transcendentals=keys, bytes_accessed=14 << 20
        ),
        name="attend_back",
    )(meta, q_t, grad_t, q, grad, lse, inner, prompt, prompt, own, own)


def key_layout(block_order, portion):
    portions = PROMPT // portion
    column = lax.axis_index("col")
    base = column // portions * portions
    ident = block_order[column]
    group = ident // portions
    place = ident % portions
    slots = jnp.arange(block_order.shape[0], dtype=jnp.int32)
    parts = group * portions + jnp.arange(portions, dtype=jnp.int32)
    sources = jnp.sum(jnp.where(block_order[None, :] == parts[:, None], slots[None, :], 0), axis=1)
    split = portion // KEY_TILE
    tiles = (sources - base)[:, None] * split + jnp.arange(split, dtype=jnp.int32)[None, :]
    return jnp.concatenate([tiles.reshape(-1), place[None]]).astype(jnp.int32)


def bit_of(value, bit):
    return value // (1 << bit) % 2


def swapped(block, axis, distance):
    size = lax.axis_size(axis)
    return lax.ppermute(block, axis, [(i, i ^ 1 << distance) for i in range(size)])


def gather_prompt(held):
    portion = held.shape[0]
    portions = PROMPT // portion
    if portions == lax.axis_size("col"):
        return lax.all_gather(held, "col", axis=0, tiled=True)
    column = lax.axis_index("col")
    for bit in range(portions.bit_length() - 1):
        other = swapped(held, "col", bit)
        upper = bit_of(column, bit) == 1
        held = jnp.where(
            upper, jnp.concatenate([other, held], axis=0), jnp.concatenate([held, other], axis=0)
        )
    return held


def scatter_prompt(buffer, portion):
    portions = PROMPT // portion
    if portions == lax.axis_size("col"):
        return lax.psum_scatter(buffer, "col", scatter_dimension=0, tiled=True)
    column = lax.axis_index("col")
    for bit in reversed(range(portions.bit_length() - 1)):
        half = buffer.shape[0] // 2
        upper = bit_of(column, bit) == 1
        keep = jnp.where(upper, buffer[half:], buffer[:half])
        outgoing = jnp.where(upper, buffer[:half], buffer[half:])
        got = swapped(outgoing, "col", bit)
        buffer = (keep.astype(F32) + got.astype(F32)).astype(BF16)
    return buffer


def padded(block, width):
    return jnp.pad(block, ((0, 0), (0, width - block.shape[1])))


def to_strips(block, rows):
    count = block.shape[0]
    strips = [block[:, i : i + 128] for i in range(0, block.shape[1], 128)]
    tall = jnp.concatenate(strips, axis=0)
    return jnp.concatenate(
        [tall[i : i + rows] for i in range(0, tall.shape[0], rows)], axis=1
    ) if tall.shape[0] != rows else tall


def head_mask(width):
    group = lax.broadcasted_iota(jnp.int32, (LATENT_HEADS * LATENT, 2 * width), 0) // LATENT
    head = lax.broadcasted_iota(jnp.int32, (LATENT_HEADS * LATENT, 2 * width), 1) // HEAD_DIM
    return group == head % LATENT_HEADS


def per_device(
    tokens, first_gain, query_weight, latent_weight, key_weight, value_weight, output_weight,
    second_gain, gate_weight, up_weight, down_weight, block_order, cotangent,
):
    columns = lax.axis_size("col")
    share = query_weight.shape[0]
    width = query_weight.shape[1]
    features = latent_weight.shape[1]
    hidden_units = gate_weight.shape[1]
    units = -(-hidden_units // 128) * 128

    early = jnp.concatenate(
        [query_weight, latent_weight, output_weight.T], axis=1
    )
    pair_weight = jnp.concatenate([key_weight, value_weight], axis=1)
    late = jnp.concatenate(
        [padded(gate_weight, units), padded(up_weight, units), padded(down_weight.T, units)], axis=1
    )
    pair_rows = pair_weight.shape[0]
    strips = 2 * width // 128
    pair_flat = jnp.concatenate(
        [pair_weight[:, i * 128 : (i + 1) * 128] for i in range(strips)], axis=0
    )
    if pair_flat.shape[0] == share:
        early_all = lax.all_gather(
            jnp.concatenate([early, pair_flat], axis=1), "col", axis=0, tiled=True
        )
        flat_all = early_all[:, early.shape[1] :].reshape(columns, strips, pair_rows, 128)
    else:
        early_all = lax.all_gather(early, "col", axis=0, tiled=True)
        flat_all = lax.all_gather(pair_flat, "col", axis=0, tiled=True).reshape(
            columns, strips, pair_rows, 128
        )
    pair_full = jnp.concatenate(
        [flat_all[:, i].reshape(columns * pair_rows, 128) for i in range(strips)], axis=1
    )
    query_full = early_all[:, :width]
    latent_full = early_all[:, width : width + features]
    output_full = early_all[:, width + features : 2 * width + features]

    rows = tokens.astype(F32)
    normed, first_scale = norm_forward(rows, first_gain)
    normed_block = gather_true(normed.astype(BF16))
    block = normed_block.shape[0]
    portion = block // 2
    mask = head_mask(width)
    spread = jnp.where(mask, jnp.concatenate([pair_full] * LATENT_HEADS, axis=0), jnp.zeros((), BF16))
    latent_part = dot(normed_block, latent_full, 1, 0).astype(BF16)
    latent_all = gather_features(latent_part)
    pairs = dot(latent_all, spread, 1, 0).astype(BF16)
    own = pairs[portion:]
    prompt = gather_prompt(pairs[:portion])
    scale = HEAD_DIM**-0.5
    queries_t = (dot(query_full, normed_block, 0, 1).astype(BF16) * scale).astype(BF16)
    queries = (dot(normed_block, query_full, 1, 0).astype(BF16) * scale).astype(BF16)
    meta = key_layout(block_order, portion)
    late, prompt_first = lax.optimization_barrier((late, prompt[:8]))
    late_all = lax.all_gather(late, "col", axis=0, tiled=True)
    wide_full = late_all[:, : 2 * units]
    down_full = late_all[:, 2 * units :]
    cot_block = gather_near(cotangent)
    result_t, attended_t, lse = attend(meta, queries_t, prompt, own)
    branch = dot(attended_t, output_full, 0, 1)
    hidden = rows + scatter_true(branch)

    normed2, second_scale = norm_forward(hidden, second_gain)
    normed2_block = gather_near(normed2.astype(BF16))
    both = dot(normed2_block, wide_full, 1, 0)
    gate = both[:, :units]
    up = both[:, units:]
    sigma = jax.nn.sigmoid(gate)
    act = (gate * sigma * up).astype(BF16)
    act_grad = dot(cot_block, down_full, 1, 0)
    gate_grad = (act_grad * up * sigma * (1.0 + gate * (1.0 - sigma))).astype(BF16)
    up_grad = (act_grad * gate * sigma).astype(BF16)
    both_grad = jnp.concatenate([gate_grad, up_grad], axis=1)
    normed2_grad = scatter_near(dot(both_grad, wide_full, 1, 1))
    layer = hidden + scatter_near(dot(act, down_full, 1, 1))
    late_terms = jnp.concatenate(
        [
            dot(normed2_block, both_grad, 0, 0).astype(BF16),
            dot(cot_block, act, 0, 0).astype(BF16),
        ],
        axis=1,
    )
    late_sums = lax.psum_scatter(late_terms, "col", scatter_dimension=0, tiled=True).astype(F32)
    norm2_grad, second_gain_term = norm_backward(hidden, second_scale, second_gain, normed2_grad)
    hidden_grad = cotangent.astype(F32) + norm2_grad

    branch_block = gather_true(hidden_grad.astype(BF16))
    attended_grad = dot(branch_block, output_full, 1, 0).astype(BF16)
    attended_grad_t = dot(output_full, branch_block, 0, 1).astype(BF16)
    inner = jnp.sum(
        (attended_grad_t.astype(F32) * result_t).reshape(-1, HEAD_DIM, block), axis=1
    )
    inner = jnp.pad(inner, ((0, 8 - inner.shape[0]), (0, 0)))
    query_grad_t, prompt_grad, own_grad = attend_back(
        meta, queries_t, attended_grad_t, queries, attended_grad, lse, inner, prompt, own
    )
    output_term = dot(branch_block, attended_t, 0, 1).astype(BF16)
    query_term = dot(normed_block, query_grad_t, 0, 1).astype(BF16)
    pair_grad = jnp.concatenate([scatter_prompt(prompt_grad, portion), own_grad], axis=0)
    latent_grad = scatter_features(dot(pair_grad, spread, 1, 1))
    pair_big = dot(latent_all, pair_grad, 0, 0)
    pair_term = jnp.where(mask[:LATENT], pair_big[:LATENT], pair_big[LATENT:]).astype(BF16)
    normed_grad = scatter_true(
        dot(query_grad_t, query_full, 0, 1) + dot(latent_grad, latent_full, 1, 1)
    )
    latent_term = dot(normed_block, latent_grad, 0, 0).astype(BF16)
    pair_terms = pair_term.reshape(columns, pair_rows, strips, 128)
    pair_terms = jnp.concatenate([pair_terms[:, :, i] for i in range(strips)], axis=1)
    pair_terms = pair_terms.reshape(columns * strips * pair_rows, 128)
    early_terms = jnp.concatenate([query_term, latent_term, output_term], axis=1)
    if pair_flat.shape[0] == share:
        early_sums = lax.psum_scatter(
            jnp.concatenate([early_terms, pair_terms], axis=1),
            "col", scatter_dimension=0, tiled=True,
        ).astype(F32)
        pair_sums = early_sums[:, early_terms.shape[1] :]
    else:
        early_sums = lax.psum_scatter(
            early_terms, "col", scatter_dimension=0, tiled=True
        ).astype(F32)
        pair_sums = lax.psum_scatter(
            pair_terms, "col", scatter_dimension=0, tiled=True
        ).astype(F32)
    norm1_grad, first_gain_term = norm_backward(rows, first_scale, first_gain, normed_grad)
    input_gradient = hidden_grad + norm1_grad
    gains = all_sum(jnp.stack([first_gain_term, second_gain_term]))
    pair_sum = jnp.concatenate(
        [pair_sums[i * pair_rows : (i + 1) * pair_rows] for i in range(strips)], axis=1
    )
    return (
        layer,
        input_gradient,
        gains[0],
        early_sums[:, :width],
        early_sums[:, width : width + features],
        pair_sum[:, :width],
        pair_sum[:, width:],
        early_sums[:, width + features : 2 * width + features].T,
        gains[1],
        late_sums[:, :hidden_units],
        late_sums[:, units : units + hidden_units],
        late_sums[:, 2 * units : 2 * units + hidden_units].T,
    )


def solution(mesh):
    rows = P(("col", "row"), None)
    placed = (
        rows, P(), P("col", "row"), P("col", "row"), P("col", "row"), P("col", "row"),
        P("row", "col"), P(), P("col", "row"), P("col", "row"), P("row", "col"), P(), rows,
    )
    given = (
        rows, rows, P(), P("col", "row"), P("col", "row"), P("col", "row"), P("col", "row"),
        P("row", "col"), P(), P("col", "row"), P("col", "row"), P("row", "col"),
    )
    return jax.shard_map(
        per_device, mesh=mesh, in_specs=placed, out_specs=given, check_vma=False
    )
```

time: 1200 us -> 574 us (0.48)
  waiting for transfers between devices: 610 us -> 280 us
  blocking collectives: 213 us -> 0 us
  matrix products: 233 us -> 56 us
  Pallas kernels: 0 us -> 91.7 us
  starting transfers between devices: 7.51 us -> 57.3 us
  other arithmetic: 76.4 us -> 34.2 us
    dot_general x78 -> x20, matrix products: 233 us -> 56 us  [dot(): lax.dot_general(left, right, (((left_dim,), (right_dim,)), ((), ())), pre...]
    all_gather x5 -> x0, blocking collectives: 172 us -> none  [the longest x1 95.8 us: forward(): lax.all_gather(weights[4], 'col', axis=1, tiled=True)]
    unnamed x27 -> x7, waiting for transfers between devices: 167 us -> 12.6 us
    all_gather x8 -> x3, waiting for transfers between devices: 169 us -> 39.8 us  [the longest x1 39.8 us: gather_prompt(): return lax.all_gather(held, 'col', axis=0, tiled=True)]
    reduce_scatter x7 -> x2, waiting for transfers between devices: 164 us -> 69.4 us  [the longest x1 69.4 us: scatter_prompt(): return lax.psum_scatter(buffer, 'col', scatter_dimension=0, tiled=True)]
    pallas_call x0 -> x2, Pallas kernels: none -> 91.7 us  [the longest x1 48.8 us: attend_back(): pl.pallas_call(functools.partial(attend_back_kernel, heads=heads, prompt_...]
    ppermute x6 -> x45, starting transfers between devices: 5.39 us -> 57 us  [the longest x40 47.4 us: exchange(): lax.ppermute(block, 'row', [(i, i ^ mask) for i in range(lax.axis_size('r...]
    ppermute x6 -> x45, waiting for transfers between devices: 110 us -> 158 us  [the longest x40 151 us: exchange(): lax.ppermute(block, 'row', [(i, i ^ mask) for i in range(lax.axis_size('r...]
  transfers between devices with their start and end apart: 27 -> 51, of which waited for: 20 -> 40; matrix products, arithmetic and copies ran while one was open for 8% -> 16% of each run, Pallas kernels for 0% -> 7%
where the time goes in v1:
time: 574 us; the launch traced here: 575 us
  waiting for transfers between devices  280 us (49%)
  Pallas kernels  91.7 us (16%)
  starting transfers between devices  57.3 us (10%)
  matrix products  56 us (10%)
  local copies, waits for them, and re-layouts  38.1 us (7%)
  other arithmetic  34.2 us (6%)
  between operations  18.2 us (3%)
    ppermute x40, waiting for transfers between devices, exchange(): lax.ppermute(block, 'row', [(i, i ^ mask) for i in range(lax.axis_size('r...  151 us
    reduce_scatter x1, waiting for transfers between devices, scatter_prompt(): return lax.psum_scatter(buffer, 'col', scatter_dimension=0, tiled=True)  69.4 us
    dot_general x20, matrix products, dot(): lax.dot_general(left, right, (((left_dim,), (right_dim,)), ((), ())), pre...  56 us
    pallas_call x1, Pallas kernels, attend_back(): pl.pallas_call(functools.partial(attend_back_kernel, heads=heads, prompt_...  48.8 us
    ppermute x40, starting transfers between devices, exchange(): lax.ppermute(block, 'row', [(i, i ^ mask) for i in range(lax.axis_size('r...  47.4 us
    pallas_call x1, Pallas kernels, attend(): pl.pallas_call(functools.partial(attend_kernel, heads=heads, prompt_tiles...  42.9 us
    all_gather x1, waiting for transfers between devices, gather_prompt(): return lax.all_gather(held, 'col', axis=0, tiled=True)  39.8 us
    unnamed x131, local copies, waits for them, and re-layouts  24.8 us
  transfers between devices with their start and end apart: 51, of which 40 were waited for; matrix products, arithmetic and copies ran while one was open for 16% of the time, Pallas kernels for 7%

profile of v1, /device:TPU:0, one launch (start us, length us, event | category | flops | bytes accessed | tf_op | source)
XLA Modules:
  0.0 575.0 jit_solution(3770052992736921353)
XLA Ops:
  17.6 6.3 %collective-permute-done.1 = bf16[128,1024]{1,0:T(8,128)(2,1)S(1)} collective-permute-done((bf16[128,1024]{1,0:T(8,128)(2,1)S(1)}, bf16[128,1024]{1,0:T(8,128)(2,1)S(1)}, u32[]{:S(2)}, u32[]{:S(2)}) %collective-permute-start.1) | collective-permute-done | bytes 262176 | tf_op jit(solution)/shard_map/ppermute | solution.py:44
  26.0 12.8 %collective-permute-done.2 = bf16[256,1024]{1,0:T(8,128)(2,1)S(1)} collective-permute-done((bf16[256,1024]{1,0:T(8,128)(2,1)S(1)}, bf16[256,1024]{1,0:T(8,128)(2,1)S(1)}, u32[]{:S(2)}, u32[]{:S(2)}) %collective-permute-start.2) | collective-permute-done | bytes 524320 | tf_op jit(solution)/shard_map/ppermute | solution.py:44
  45.1 10.8 %collective-permute-done.3 = bf16[256,1024]{1,0:T(8,128)(2,1)S(1)} collective-permute-done((bf16[256,1024]{1,0:T(8,128)(2,1)S(1)}, bf16[256,1024]{1,0:T(8,128)(2,1)S(1)}, u32[]{:S(2)}, u32[]{:S(2)}) %collective-permute-start.3) | collective-permute-done | bytes 524320 | tf_op jit(solution)/shard_map/ppermute | solution.py:44
  67.4 4.2 collective-permute-done.6
  74.5 5.1 collective-permute-done.7
  90.3 39.8 %all-gather.6.cloned.1.call-done.key_in.value_in = bf16[4096,512]{1,0:T(8,128)(2,1)} async-done(((bf16[512,512]{1,0:T(8,128)(2,1)}), bf16[4096,512]{1,0:T(8,128)(2,1)}) %all-gather.6.cloned.1.call-update) | async-done | bytes 4194320 | tf_op jit(solution)/shard_map/all_gather | solution.py:474
  130.1 42.9 %attend.1 = (f32[256,1024]{1,0:T(8,128)}, bf16[256,1024]{1,0:T(8,128)(2,1)}, f32[8,1024]{1,0:T(8,128)}) custom-call(s32[9]{0:T(128)} %pad_add_fusion.meta, bf16[256,1024]{1,0:T(8,128)(2,1)} %fusion.14.q_t, bf16[4096,512]{1,0:T(8,128)(2,1)} %all-gather.6.cloned.1.call-done.key_in.value_in, bf16[4096,512]{1,0:T(8,128)(2,1)} %all-gather.6.cloned.1.call-done.key_in.value_in, ...), custom_call_target="tpu_custom_call" | custom-call | flops 14495514624 | bytes 8388608 | tf_op jit(solution)/shard_map/attend/pallas_call | solution.py:353
  181.1 7.7 %collective-permute-done.8 = bf16[256,1024]{1,0:T(8,128)(2,1)S(1)} collective-permute-done((bf16[256,1024]{1,0:T(8,128)(2,1)S(1)}, bf16[256,1024]{1,0:T(8,128)(2,1)S(1)}, u32[]{:S(2)}, u32[]{:S(2)}) %collective-permute-start.8) | collective-permute-done | bytes 524320 | tf_op jit(solution)/shard_map/ppermute | solution.py:44
  198.9 5.6 collective-permute-done.9
  239.3 6.1 %fusion.2 = f32[1024,1536]{1,0:T(8,128)S(1)} fusion(bf16[1024,1024]{1,0:T(8,128)(2,1)} %slice_dynamic-update-slice_fusion.4, bf16[1024,2304]{0,1:T(8,128)(2,1)} %all-gather.8.cloned.1.call-done), kind=kOutput, calls=%fused_computation.10 | convolution fusion | flops 3221225472 | bytes 11534336 | tf_op jit(solution)/shard_map/dot_general | solution.py:25
  260.1 4.4 collective-permute-done.16
  266.8 6.2 %collective-permute-done.24 = bf16[256,1024]{1,0:T(8,128)(2,1)S(1)} collective-permute-done((bf16[256,1024]{1,0:T(8,128)(2,1)S(1)}, bf16[256,1024]{1,0:T(8,128)(2,1)S(1)}, u32[]{:S(2)}, u32[]{:S(2)}) %collective-permute-start.24) | collective-permute-done | bytes 524320 | tf_op jit(solution)/shard_map/ppermute | solution.py:44
  279.4 5.0 collective-permute-done.26
  287.9 7.9 %collective-permute-done.27 = bf16[128,1024]{1,0:T(8,128)(2,1)S(1)} collective-permute-done((bf16[128,1024]{1,0:T(8,128)(2,1)S(1)}, bf16[128,1024]{1,0:T(8,128)(2,1)S(1)}, u32[]{:S(2)}, u32[]{:S(2)}) %collective-permute-start.27) | collective-permute-done | bytes 262176 | tf_op jit(solution)/shard_map/ppermute | solution.py:44
  299.5 6.0 %collective-permute-done.29 = bf16[128,1024]{1,0:T(8,128)(2,1)S(1)} collective-permute-done((bf16[128,1024]{1,0:T(8,128)(2,1)S(1)}, bf16[128,1024]{1,0:T(8,128)(2,1)S(1)}, u32[]{:S(2)}, u32[]{:S(2)}) %collective-permute-start.29) | collective-permute-done | bytes 262176 | tf_op jit(solution)/shard_map/ppermute | solution.py:44
  307.6 7.2 %collective-permute-done.30 = bf16[256,1024]{1,0:T(8,128)(2,1)S(1)} collective-permute-done((bf16[256,1024]{1,0:T(8,128)(2,1)S(1)}, bf16[256,1024]{1,0:T(8,128)(2,1)S(1)}, u32[]{:S(2)}, u32[]{:S(2)}) %collective-permute-start.30) | collective-permute-done | bytes 524320 | tf_op jit(solution)/shard_map/ppermute | solution.py:44
  321.2 5.7 collective-permute-done.31
  331.1 48.8 %attend_back.1 = (bf16[256,1024]{1,0:T(8,128)(2,1)}, bf16[4096,512]{1,0:T(8,128)(2,1)}, bf16[512,512]{1,0:T(8,128)(2,1)}) custom-call(s32[9]{0:T(128)} %pad_add_fusion.meta, bf16[256,1024]{1,0:T(8,128)(2,1)} %fusion.14.q_t, bf16[256,1024]{1,0:T(8,128)(2,1)} %copy-done.10, bf16[1024,256]{1,0:T(8,128)(2,1)} %fusion.15.q, ...), custom_call_target="tpu_custom_call" | custom-call | flops 36238786560 | bytes 14680064 | tf_op jit(solution)/shard_map/attend_back/pallas_call | solution.py:395
  384.1 5.8 %convolution_convert_fusion = bf16[1024,1536]{1,0:T(8,128)(2,1)S(1)} fusion(bf16[1024,1024]{1,0:T(8,128)(2,1)} %slice_dynamic-update-slice_fusion.4, bf16[1024,768]{1,0:T(8,128)(2,1)S(1)} %copy-done.51, bf16[1024,768]{1,0:T(8,128)(2,1)S(1)} %copy-done.49), kind=kOutput, calls=%fused_computation.2 | convolution fusion | flops 3229089792 | bytes 8388608 | tf_op jit(solution)/shard_map/dot_general | solution.py:25
  403.1 69.4 %reduce-scatter.6.cloned.1.call-done = bf16[512,512]{1,0:T(8,128)(2,1)} async-done(((bf16[4096,512]{1,0:T(8,128)(2,1)}), bf16[512,512]{1,0:T(8,128)(2,1)}) %reduce-scatter.6.cloned.1.call-update) | async-done | bytes 524304 | tf_op jit(solution)/shard_map/reduce_scatter | solution.py:488
  484.7 4.3 collective-permute-done.33
  518.7 4.9 collective-permute-done.39
  537.4 6.3 %collective-permute-start.43 = (f32[2,1024]{1,0:T(2,128)S(1)}, f32[2,1024]{1,0:T(2,128)S(1)}, u32[]{:S(2)}, u32[]{:S(2)}) collective-permute-start(f32[2,1024]{1,0:T(2,128)S(1)} %add.281), channel_id=1, source_target_pairs={{0,2},{1,3},{2,0},{3,1},{4,6},{5,7},{6,4},{7,5},{8,10},{9,11},{10,... | collective-permute-start | bytes 24584 | tf_op jit(solution)/shard_map/ppermute | solution.py:141
  550.5 12.5 %reduce-scatter.10.cloned.1.call-done = bf16[128,768]{1,0:T(8,128)(2,1)} async-done(((bf16[1024,768]{1,0:T(8,128)(2,1)}), bf16[128,768]{1,0:T(8,128)(2,1)}) %reduce-scatter.10.cloned.1.call-update) | async-done | bytes 196624
  (360 shorter events, 221.2 us)
Async XLA Ops:
  7.2 50.4 %all-gather.4.cloned.1.call-start = ((), (), s32[]{:S(2)}) async-start(), calls=%async_computation.3 | async-start | bytes 1769472 | tf_op jit(solution)/shard_map/all_gather | solution.py:543
  10.6 119.5 %all-gather.6.cloned.1.call-start = ((), (), s32[]{:S(2)}) async-start(), calls=%async_computation.4 | async-start | bytes 4718592 | tf_op jit(solution)/shard_map/all_gather | solution.py:474
  23.9 14.9 %collective-permute-start.2 = (bf16[256,1024]{1,0:T(8,128)(2,1)S(1)}, bf16[256,1024]{1,0:T(8,128)(2,1)S(1)}, u32[]{:S(2)}, u32[]{:S(2)}) collective-permute-start(bf16[256,1024]{1,0:T(8,128)(2,1)S(1)} %pad_maximum_fusion.12), channel_id=1, source_target_pairs={{0,8},{8,0},{16,24},{24,16},{1,9},{9,1},{17,25},{25,17},{2,10},{10... | collective-permute-start | bytes 1572872 | tf_op jit(solution)/shard_map/ppermute | solution.py:44
  25.7 17.0 %collective-permute-start = (bf16[128,1024]{1,0:T(8,128)(2,1)S(1)}, bf16[128,1024]{1,0:T(8,128)(2,1)S(1)}, u32[]{:S(2)}, u32[]{:S(2)}) collective-permute-start(bf16[128,1024]{1,0:T(8,128)(2,1)S(1)} %get-tuple-element.145), channel_id=1, source_target_pairs={{0,8},{8,0},{16,24},{24,16},{1,9},{9,1},{17,25},{25,17},{2,10},{10... | collective-permute-start | bytes 786440 | tf_op jit(solution)/shard_map/ppermute | solution.py:44
  43.6 12.2 %collective-permute-start.3 = (bf16[256,1024]{1,0:T(8,128)(2,1)S(1)}, bf16[256,1024]{1,0:T(8,128)(2,1)S(1)}, u32[]{:S(2)}, u32[]{:S(2)}) collective-permute-start(bf16[256,1024]{1,0:T(8,128)(2,1)S(1)} %get-tuple-element.163), channel_id=1, source_target_pairs={{0,16},{8,24},{16,0},{24,8},{1,17},{9,25},{17,1},{25,9},{2,18},{10... | collective-permute-start | bytes 1572872 | tf_op jit(solution)/shard_map/ppermute | solution.py:44
  81.9 157.3 %all-gather.8.cloned.1.call-start = ((), (), s32[]{:S(2)}) async-start(), calls=%async_computation.5 | async-start | bytes 5308416 | tf_op jit(solution)/shard_map/all_gather | solution.py:576
  83.1 389.4 %reduce-scatter.6.cloned.1.call-start = ((), (), s32[]{:S(2)}) async-start(), calls=%async_computation.6 | async-start | bytes 4718592 | tf_op jit(solution)/shard_map/reduce_scatter | solution.py:488
  175.1 13.6 %collective-permute-start.8 = (bf16[256,1024]{1,0:T(8,128)(2,1)S(1)}, bf16[256,1024]{1,0:T(8,128)(2,1)S(1)}, u32[]{:S(2)}, u32[]{:S(2)}) collective-permute-start(bf16[256,1024]{1,0:T(8,128)(2,1)S(1)} %pad_maximum_fusion.16), channel_id=1, source_target_pairs={{0,16},{8,24},{16,0},{24,8},{1,17},{9,25},{17,1},{25,9},{2,18},{10... | collective-permute-start | bytes 1572872 | tf_op jit(solution)/shard_map/ppermute | solution.py:44
  177.4 14.2 %collective-permute-start.21 = (bf16[128,1024]{1,0:T(8,128)(2,1)S(1)}, bf16[128,1024]{1,0:T(8,128)(2,1)S(1)}, u32[]{:S(2)}, u32[]{:S(2)}) collective-permute-start(bf16[128,1024]{1,0:T(8,128)(2,1)S(1)} %get-tuple-element.137), channel_id=1, source_target_pairs={{0,16},{8,24},{16,0},{24,8},{1,17},{9,25},{17,1},{25,9},{2,18},{10... | collective-permute-start | bytes 786440 | tf_op jit(solution)/shard_map/ppermute | solution.py:44
  178.2 16.5 %collective-permute-start.20 = (bf16[128,1024]{1,0:T(8,128)(2,1)}, bf16[128,1024]{1,0:T(8,128)(2,1)}, u32[]{:S(2)}, u32[]{:S(2)}) collective-permute-start(bf16[128,1024]{1,0:T(8,128)(2,1)} %get-tuple-element.138), channel_id=1, source_target_pairs={{0,8},{8,0},{16,24},{24,16},{1,9},{9,1},{17,25},{25,17},{2,10},{10... | collective-permute-start | bytes 786440 | tf_op jit(solution)/shard_map/ppermute | solution.py:44
  180.5 18.4 %collective-permute-start.10 = (bf16[256,1024]{1,0:T(8,128)(2,1)}, bf16[256,1024]{1,0:T(8,128)(2,1)}, u32[]{:S(2)}, u32[]{:S(2)}) collective-permute-start(bf16[256,1024]{1,0:T(8,128)(2,1)} %pad_maximum_fusion.17), channel_id=1, source_target_pairs={{0,8},{8,0},{16,24},{24,16},{1,9},{9,1},{17,25},{25,17},{2,10},{10... | collective-permute-start | bytes 1572872 | tf_op jit(solution)/shard_map/ppermute | solution.py:44
  189.6 14.9 %collective-permute-start.9 = (bf16[128,1024]{1,0:T(8,128)(2,1)}, bf16[128,1024]{1,0:T(8,128)(2,1)}, u32[]{:S(2)}, u32[]{:S(2)}) collective-permute-start(bf16[128,1024]{1,0:T(8,128)(2,1)} %add_convert_fusion.8), channel_id=1, source_target_pairs={{0,8},{8,0},{16,24},{24,16},{1,9},{9,1},{17,25},{25,17},{2,10},{10... | collective-permute-start | bytes 786440 | tf_op jit(solution)/shard_map/ppermute | solution.py:44
  192.4 19.1 %collective-permute-start.22 = (bf16[256,1024]{1,0:T(8,128)(2,1)}, bf16[256,1024]{1,0:T(8,128)(2,1)}, u32[]{:S(2)}, u32[]{:S(2)}) collective-permute-start(bf16[256,1024]{1,0:T(8,128)(2,1)} %pad_maximum_fusion.22), channel_id=1, source_target_pairs={{0,8},{8,0},{16,24},{24,16},{1,9},{9,1},{17,25},{25,17},{2,10},{10... | collective-permute-start | bytes 1572872 | tf_op jit(solution)/shard_map/ppermute | solution.py:44
  195.8 20.7 %collective-permute-start.23 = (bf16[256,1024]{1,0:T(8,128)(2,1)S(1)}, bf16[256,1024]{1,0:T(8,128)(2,1)S(1)}, u32[]{:S(2)}, u32[]{:S(2)}) collective-permute-start(bf16[256,1024]{1,0:T(8,128)(2,1)S(1)} %pad_maximum_fusion.23), channel_id=1, source_target_pairs={{0,16},{8,24},{16,0},{24,8},{1,17},{9,25},{17,1},{25,9},{2,18},{10... | collective-permute-start | bytes 1572872 | tf_op jit(solution)/shard_map/ppermute | solution.py:44
  222.6 10.7 %collective-permute-start.14 = (bf16[256,1024]{1,0:T(8,128)(2,1)S(1)}, bf16[256,1024]{1,0:T(8,128)(2,1)S(1)}, u32[]{:S(2)}, u32[]{:S(2)}) collective-permute-start(bf16[256,1024]{1,0:T(8,128)(2,1)S(1)} %pad_maximum_fusion.18), channel_id=1, source_target_pairs={{0,8},{8,0},{16,24},{24,16},{1,9},{9,1},{17,25},{25,17},{2,10},{10... | collective-permute-start | bytes 1572872 | tf_op jit(solution)/shard_map/ppermute | solution.py:44
  252.3 12.3 %collective-permute-start.16 = (bf16[256,1024]{1,0:T(8,128)(2,1)S(1)}, bf16[256,1024]{1,0:T(8,128)(2,1)S(1)}, u32[]{:S(2)}, u32[]{:S(2)}) collective-permute-start(bf16[256,1024]{1,0:T(8,128)(2,1)S(1)} %pad_maximum_fusion.20), channel_id=1, source_target_pairs={{0,16},{8,24},{16,0},{24,8},{1,17},{9,25},{17,1},{25,9},{2,18},{10... | collective-permute-start | bytes 1572872 | tf_op jit(solution)/shard_map/ppermute | solution.py:44
  257.6 15.4 %collective-permute-start.24 = (bf16[256,1024]{1,0:T(8,128)(2,1)S(1)}, bf16[256,1024]{1,0:T(8,128)(2,1)S(1)}, u32[]{:S(2)}, u32[]{:S(2)}) collective-permute-start(bf16[256,1024]{1,0:T(8,128)(2,1)S(1)} %pad_maximum_fusion.24), channel_id=1, source_target_pairs={{0,16},{8,24},{16,0},{24,8},{1,17},{9,25},{17,1},{25,9},{2,18},{10... | collective-permute-start | bytes 1572872 | tf_op jit(solution)/shard_map/ppermute | solution.py:44
  258.6 16.0 %collective-permute-start.18 = (bf16[256,1024]{1,0:T(8,128)(2,1)S(1)}, bf16[256,1024]{1,0:T(8,128)(2,1)S(1)}, u32[]{:S(2)}, u32[]{:S(2)}) collective-permute-start(bf16[256,1024]{1,0:T(8,128)(2,1)S(1)} %pad_maximum_fusion.21), channel_id=1, source_target_pairs={{0,8},{8,0},{16,24},{24,16},{1,9},{9,1},{17,25},{25,17},{2,10},{10... | collective-permute-start | bytes 1572872 | tf_op jit(solution)/shard_map/ppermute | solution.py:44
  264.6 14.1 %collective-permute-start.17 = (bf16[128,1024]{1,0:T(8,128)(2,1)S(1)}, bf16[128,1024]{1,0:T(8,128)(2,1)S(1)}, u32[]{:S(2)}, u32[]{:S(2)}) collective-permute-start(bf16[128,1024]{1,0:T(8,128)(2,1)S(1)} %add_convert_fusion.6), channel_id=1, source_target_pairs={{0,8},{8,0},{16,24},{24,16},{1,9},{9,1},{17,25},{25,17},{2,10},{10... | collective-permute-start | bytes 786440 | tf_op jit(solution)/shard_map/ppermute | solution.py:44
  266.2 18.2 %collective-permute-start.26 = (bf16[256,1024]{1,0:T(8,128)(2,1)S(1)}, bf16[256,1024]{1,0:T(8,128)(2,1)S(1)}, u32[]{:S(2)}, u32[]{:S(2)}) collective-permute-start(bf16[256,1024]{1,0:T(8,128)(2,1)S(1)} %pad_maximum_fusion.25), channel_id=1, source_target_pairs={{0,8},{8,0},{16,24},{24,16},{1,9},{9,1},{17,25},{25,17},{2,10},{10... | collective-permute-start | bytes 1572872 | tf_op jit(solution)/shard_map/ppermute | solution.py:44
  273.1 14.1 %collective-permute-start.25 = (bf16[128,1024]{1,0:T(8,128)(2,1)S(1)}, bf16[128,1024]{1,0:T(8,128)(2,1)S(1)}, u32[]{:S(2)}, u32[]{:S(2)}) collective-permute-start(bf16[128,1024]{1,0:T(8,128)(2,1)S(1)} %add_convert_fusion.4), channel_id=1, source_target_pairs={{0,8},{8,0},{16,24},{24,16},{1,9},{9,1},{17,25},{25,17},{2,10},{10... | collective-permute-start | bytes 786440 | tf_op jit(solution)/shard_map/ppermute | solution.py:44
  379.9 150.5 %reduce-scatter.8.cloned.1.call-start = ((), (), s32[]{:S(2)}) async-start(), calls=%async_computation.7 | async-start | bytes 5308416 | tf_op jit(solution)/shard_map/reduce_scatter | solution.py:604
  392.4 170.6 %reduce-scatter.10.cloned.1.call-start = ((), (), s32[]{:S(2)}) async-start(), calls=%async_computation.8 | async-start | bytes 1769472
  500.5 12.2 %collective-permute-start.38 = (bf16[256,1024]{1,0:T(8,128)(2,1)S(1)}, bf16[256,1024]{1,0:T(8,128)(2,1)}, u32[]{:S(2)}, u32[]{:S(2)}) collective-permute-start(bf16[256,1024]{1,0:T(8,128)(2,1)S(1)} %pad_maximum_fusion.28), channel_id=1, source_target_pairs={{0,8},{8,0},{16,24},{24,16},{1,9},{9,1},{17,25},{25,17},{2,10},{10... | collective-permute-start | bytes 1572872 | tf_op jit(solution)/shard_map/ppermute | solution.py:44
  (81 other events, 1002.3 us)
Sparse Core Ops, SparseCore 0:
  10.7 27.9 all-gather.3
  82.0 48.0 all-gather.5
  132.3 50.9 all-gather.7
  380.1 92.3 reduce-scatter.5
  474.6 53.3 reduce-scatter.7
  530.1 32.8 reduce-scatter.9

commit v2 on v1

--- a/solution.py
+++ b/solution.py
@@ -112,35 +112,39 @@
     )
 
 
-def gather_features(part):
-    if lax.axis_size("row") != 4:
-        return lax.all_gather(part, "row", axis=1, tiled=True)
-    count = part.shape[0]
-    whole = gather_true(part)
-    return jnp.concatenate([whole[j * count : (j + 1) * count] for j in range(4)], axis=1)
-
-
-def scatter_features(part):
+def across(block, mask):
+    return lax.ppermute(block, "col", [(i, i ^ mask) for i in range(lax.axis_size("col"))])
+
+
+def add_low(left, right):
+    return (left.astype(F32) + right.astype(F32)).astype(BF16)
+
+
+def scatter_columns(part):
     part = part.astype(BF16)
-    size = lax.axis_size("row")
-    if size != 4:
-        return lax.psum_scatter(part, "row", scatter_dimension=1, tiled=True)
-    width = part.shape[1] // size
-    stacked = jnp.concatenate([part[:, j * width : (j + 1) * width] for j in range(size)], axis=0)
-    return scatter_true(stacked).astype(BF16)
+    size = lax.axis_size("col")
+    if size != 8:
+        return lax.psum_scatter(part, "col", scatter_dimension=0, tiled=True).astype(F32)
+    count = part.shape[0] // size
+    here = lax.axis_index("col")
+
+    def pieces(order):
+        return jnp.concatenate(
+            [lax.dynamic_slice_in_dim(part, (here ^ j) * count, count, 0) for j in order], axis=0
+        )
+
+    mine = pieces((0, 2, 4, 6)).astype(F32) + across(pieces((1, 3, 5, 7)), 1).astype(F32)
+    low = mine.astype(BF16)
+    got = [across(low[j * count : (j + 1) * count], 2 * j) for j in (1, 2, 3)]
+    return (mine[:count] + got[0].astype(F32)) + (got[1].astype(F32) + got[2].astype(F32))
 
 
 def all_sum(value):
-    for axis in ("row", "col"):
-        size = lax.axis_size(axis)
-        if size & (size - 1):
-            value = lax.psum(value, axis)
-            continue
-        bit = 1
-        while bit < size:
-            value = value + lax.ppermute(value, axis, [(i, i ^ bit) for i in range(size)])
-            bit *= 2
-    return value
+    if lax.axis_size("row") == 4 and lax.axis_size("col") == 8:
+        value = (value + exchange(value, 1)) + (exchange(value, 2) + exchange(value, 3))
+        value = value + across(value, 1)
+        return (value + across(value, 2)) + (across(value, 4) + across(value, 6))
+    return lax.psum(value, ("row", "col"))
 
 
 def masked_heads(tile, heads):
@@ -156,7 +160,7 @@
 
 
 def visit_tiles(meta, step, prompt_tiles, portion, rows, body):
-    place = meta[prompt_tiles]
+    place = meta[prompt_tiles + portion // KEY_TILE]
     first_rows = portion // ROW_TILE
 
     def visit(index, carry):
@@ -198,11 +202,26 @@
     return jnp.where(key <= query + ahead, scores, masked_value)
 
 
+def load_pairs(step, near_tiles, meta, near, far, spread, latents):
+    place = meta[step]
+
+    @pl.when(place < near_tiles)
+    def _():
+        latents[...] = near[...]
+
+    @pl.when(place >= near_tiles)
+    def _():
+        latents[...] = far[...]
+
+    return dot(latents[...], spread[...], 1, 0).astype(BF16)
+
+
 def attend_kernel(
-    meta, q_t, key_in, value_in, key_own, value_own, out, out_low, lse, keys, values_t, acc, top, total,
-    *, heads, prompt_tiles, portion, rows,
+    meta, q_t, near, far, spread, out, out_low, lse, latents, keys, values_t, acc, top, total,
+    *, heads, prompt_tiles, near_tiles, portion, rows,
 ):
     step = pl.program_id(0)
+    width = heads * HEAD_DIM
 
     @pl.when(step == 0)
     def _():
@@ -210,31 +229,35 @@
         top[...] = jnp.full_like(top, masked_value)
         total[...] = jnp.zeros_like(total)
 
-    @pl.when(step < prompt_tiles)
-    def _():
-        keys[...] = key_in[...]
-        values_t[...] = value_in[...].T
-
-    @pl.when(step >= prompt_tiles)
-    def _():
-        keys[...] = key_own[...]
-        values_t[...] = value_own[...].T
+    pairs = load_pairs(step, near_tiles, meta, near, far, spread, latents)
+    keys[...] = pairs[:, :width]
+    values_t[...] = pairs[:, width:].T
 
     def body(index, ahead):
         at = pl.ds(pl.multiple_of(index * ROW_TILE, ROW_TILE), ROW_TILE)
+        before = top[:, at]
+        sums = total[:, at]
+        scores = []
         for h in range(heads):
             pair, query = one_head(q_t, h, at)
-            scores = hide(dot(keys[:, pair], query, 1, 0), ahead)
-            before = top[h : h + 1, at]
-            now = jnp.maximum(before, jnp.max(scores, axis=0, keepdims=True))
-            probs = jnp.exp(scores - now)
-            decay = jnp.exp(before - now)
-            top[h : h + 1, at] = now
-            total[h : h + 1, at] = decay * total[h : h + 1, at] + jnp.sum(
-                probs, axis=0, keepdims=True
+            scores.append(hide(dot(keys[:, pair], query, 1, 0), ahead))
+        nows = []
+        news = []
+        results = []
+        for h in range(heads):
+            mine = slice(h * HEAD_DIM, (h + 1) * HEAD_DIM)
+            now = jnp.maximum(before[h : h + 1], jnp.max(scores[h], axis=0, keepdims=True))
+            probs = jnp.exp(scores[h] - now)
+            decay = jnp.exp(before[h : h + 1] - now)
+            nows.append(now)
+            news.append(decay * sums[h : h + 1] + jnp.sum(probs, axis=0, keepdims=True))
+            results.append(
+                decay * acc[mine, at] + dot(values_t[mine, :], probs.astype(BF16), 1, 0)
             )
-            mine = slice(h * HEAD_DIM, (h + 1) * HEAD_DIM)
-            acc[mine, at] = decay * acc[mine, at] + dot(values_t[mine, :], probs.astype(BF16), 1, 0)
+        for h in range(heads):
+            top[h : h + 1, at] = nows[h]
+            total[h : h + 1, at] = news[h]
+            acc[h * HEAD_DIM : (h + 1) * HEAD_DIM, at] = results[h]
 
     visit_tiles(meta, step, prompt_tiles, portion, rows, body)
 
@@ -249,45 +272,39 @@
 
 
 def attend_back_kernel(
-    meta, q_t, grad_t, q, grad, lse, inner, key_in, value_in, key_own, value_own,
-    query_grad, prompt_grad, own_grad,
-    keys, keys_t, values, queries_apart, grads_apart, query_acc, key_acc, value_acc,
-    *, heads, prompt_tiles, portion, rows,
+    meta, q_t, grad_t, q, grad, lse, inner, near, far, spread,
+    query_grad, latent_grad, pair_grad,
+    latents, keys, keys_t, values, queries_apart, grads_apart, query_acc, key_acc, value_acc,
+    *, heads, prompt_tiles, near_tiles, portion, rows,
 ):
     step = pl.program_id(0)
-    wide = heads * ROW_TILE
+    tall = heads * ROW_TILE
+    width = heads * HEAD_DIM
 
     @pl.when(step == 0)
     def _():
         query_acc[...] = jnp.zeros_like(query_acc)
-
-        def spread(index, carry):
+        pair_grad[...] = jnp.zeros_like(pair_grad)
+
+        def apart(index, carry):
             at = pl.ds(pl.multiple_of(index * ROW_TILE, ROW_TILE), ROW_TILE)
-            far = pl.ds(pl.multiple_of(index * wide, wide), wide)
-            queries_apart[far, :] = jnp.concatenate(masked_heads(q[at, :], heads), axis=0)
-            grads_apart[far, :] = jnp.concatenate(masked_heads(grad[at, :], heads), axis=0)
+            to = pl.ds(pl.multiple_of(index * tall, tall), tall)
+            queries_apart[to, :] = jnp.concatenate(masked_heads(q[at, :], heads), axis=0)
+            grads_apart[to, :] = jnp.concatenate(masked_heads(grad[at, :], heads), axis=0)
             return carry
 
-        lax.fori_loop(0, rows // ROW_TILE, spread, 0)
+        lax.fori_loop(0, rows // ROW_TILE, apart, 0)
 
     key_acc[...] = jnp.zeros_like(key_acc)
     value_acc[...] = jnp.zeros_like(value_acc)
-
-    @pl.when(step < prompt_tiles)
-    def _():
-        keys[...] = key_in[...]
-        keys_t[...] = key_in[...].T
-        values[...] = value_in[...]
-
-    @pl.when(step >= prompt_tiles)
-    def _():
-        keys[...] = key_own[...]
-        keys_t[...] = key_own[...].T
-        values[...] = value_own[...]
+    pairs = load_pairs(step, near_tiles, meta, near, far, spread, latents)
+    keys[...] = pairs[:, :width]
+    keys_t[...] = pairs[:, :width].T
+    values[...] = pairs[:, width:]
 
     def body(index, ahead):
         at = pl.ds(pl.multiple_of(index * ROW_TILE, ROW_TILE), ROW_TILE)
-        far = pl.ds(pl.multiple_of(index * wide, wide), wide)
+        to = pl.ds(pl.multiple_of(index * tall, tall), tall)
         all_probs = []
         all_grads = []
         for h in range(heads):
@@ -301,22 +318,14 @@
             query_acc[mine, at] += dot(keys_t[mine, :], score_grad, 1, 0)
             all_probs.append(probs.astype(BF16))
             all_grads.append(score_grad)
-        value_acc[...] += dot(jnp.concatenate(all_probs, axis=1), grads_apart[far, :], 1, 0)
-        key_acc[...] += dot(jnp.concatenate(all_grads, axis=1), queries_apart[far, :], 1, 0)
+        value_acc[...] += dot(jnp.concatenate(all_probs, axis=1), grads_apart[to, :], 1, 0)
+        key_acc[...] += dot(jnp.concatenate(all_grads, axis=1), queries_apart[to, :], 1, 0)
 
     visit_tiles(meta, step, prompt_tiles, portion, rows, body)
 
-    width = heads * HEAD_DIM
-
-    @pl.when(step < prompt_tiles)
-    def _():
-        prompt_grad[:, :width] = key_acc[...].astype(BF16)
-        prompt_grad[:, width:] = value_acc[...].astype(BF16)
-
-    @pl.when(step >= prompt_tiles)
-    def _():
-        own_grad[:, :width] = key_acc[...].astype(BF16)
-        own_grad[:, width:] = value_acc[...].astype(BF16)
+    pair_low = jnp.concatenate([key_acc[...].astype(BF16), value_acc[...].astype(BF16)], axis=1)
+    latent_grad[...] = dot(pair_low, spread[...], 1, 1).astype(BF16)
+    pair_grad[...] += dot(latents[...], pair_low, 0, 0)
 
     @pl.when(step == pl.num_programs(0) - 1)
     def _():
@@ -327,43 +336,38 @@
     return pl.BlockSpec(shape, lambda step, meta: (0, 0))
 
 
-def attention_specs(width, prompt_tiles):
-    def prompt_map(column):
-        return lambda step, meta: (meta[jnp.minimum(step, prompt_tiles - 1)], column)
-
-    def own_map(column):
-        return lambda step, meta: (jnp.maximum(step - prompt_tiles, 0), column)
-
-    tile = (KEY_TILE, width)
+def latent_specs(near, far, spread):
+    near_tiles = near.shape[0] // KEY_TILE
+    tile = (KEY_TILE, near.shape[1])
     return [
-        pl.BlockSpec(tile, prompt_map(0)),
-        pl.BlockSpec(tile, prompt_map(1)),
-        pl.BlockSpec(tile, own_map(0)),
-        pl.BlockSpec(tile, own_map(1)),
+        pl.BlockSpec(tile, lambda step, meta: (jnp.minimum(meta[step], near_tiles - 1), 0)),
+        pl.BlockSpec(tile, lambda step, meta: (jnp.maximum(meta[step] - near_tiles, 0), 0)),
+        whole_spec(spread.shape),
     ]
 
 
-def attend(meta, q_t, prompt, own):
+def attend(meta, q_t, near, far, spread, portion):
     width, rows = q_t.shape
     heads = width // HEAD_DIM
-    portion = own.shape[0]
     prompt_tiles = PROMPT // KEY_TILE
     steps = prompt_tiles + portion // KEY_TILE
-    keys = (prompt.shape[0] + portion) * rows * heads * 3 // 4
+    keys = (PROMPT + portion) * rows * heads * 3 // 4
     return pl.pallas_call(
         functools.partial(
-            attend_kernel, heads=heads, prompt_tiles=prompt_tiles, portion=portion, rows=rows
+            attend_kernel, heads=heads, prompt_tiles=prompt_tiles,
+            near_tiles=near.shape[0] // KEY_TILE, portion=portion, rows=rows,
         ),
         grid_spec=pltpu.PrefetchScalarGridSpec(
             num_scalar_prefetch=1,
             grid=(steps,),
-            in_specs=[whole_spec((width, rows))] + attention_specs(width, prompt_tiles),
+            in_specs=[whole_spec((width, rows))] + latent_specs(near, far, spread),
             out_specs=[
                 whole_spec((width, rows)),
                 whole_spec((width, rows)),
                 whole_spec((8, rows)),
             ],
             scratch_shapes=[
+                pltpu.VMEM((KEY_TILE, near.shape[1]), BF16),
                 pltpu.VMEM((KEY_TILE, width), BF16),
                 pltpu.VMEM((width, KEY_TILE), BF16),
                 pltpu.VMEM((width, rows), F32),
@@ -381,20 +385,20 @@
             flops=keys * HEAD_DIM * 16, transcendentals=keys, bytes_accessed=8 << 20
         ),
         name="attend",
-    )(meta, q_t, prompt, prompt, own, own)
-
-
-def attend_back(meta, q_t, grad_t, q, grad, lse, inner, prompt, own):
+    )(meta, q_t, near, far, spread)
+
+
+def attend_back(meta, q_t, grad_t, q, grad, lse, inner, near, far, spread, portion):
     width, rows = q_t.shape
     heads = width // HEAD_DIM
-    portion = own.shape[0]
+    features = near.shape[1]
     prompt_tiles = PROMPT // KEY_TILE
     steps = prompt_tiles + portion // KEY_TILE
-    keys = (prompt.shape[0] + portion) * rows * heads * 3 // 4
-    tall = heads * rows
+    keys = (PROMPT + portion) * rows * heads * 3 // 4
     return pl.pallas_call(
         functools.partial(
-            attend_back_kernel, heads=heads, prompt_tiles=prompt_tiles, portion=portion, rows=rows
+            attend_back_kernel, heads=heads, prompt_tiles=prompt_tiles,
+            near_tiles=near.shape[0] // KEY_TILE, portion=portion, rows=rows,
         ),
         grid_spec=pltpu.PrefetchScalarGridSpec(
             num_scalar_prefetch=1,
@@ -407,24 +411,19 @@
                 whole_spec((8, rows)),
                 whole_spec((8, rows)),
             ]
-            + attention_specs(width, prompt_tiles),
+            + latent_specs(near, far, spread),
             out_specs=[
                 whole_spec((width, rows)),
-                pl.BlockSpec(
-                    (KEY_TILE, 2 * width),
-                    lambda step, meta: (meta[jnp.minimum(step, prompt_tiles - 1)], 0),
-                ),
-                pl.BlockSpec(
-                    (KEY_TILE, 2 * width),
-                    lambda step, meta: (jnp.maximum(step - prompt_tiles, 0), 0),
-                ),
+                pl.BlockSpec((KEY_TILE, features), lambda step, meta: (meta[step], 0)),
+                whole_spec((features, 2 * width)),
             ],
             scratch_shapes=[
+                pltpu.VMEM((KEY_TILE, features), BF16),
                 pltpu.VMEM((KEY_TILE, width), BF16),
                 pltpu.VMEM((width, KEY_TILE), BF16),
                 pltpu.VMEM((KEY_TILE, width), BF16),
-                pltpu.VMEM((tall, width), BF16),
-                pltpu.VMEM((tall, width), BF16),
+                pltpu.VMEM((heads * rows, width), BF16),
+                pltpu.VMEM((heads * rows, width), BF16),
                 pltpu.VMEM((width, rows), F32),
                 pltpu.VMEM((KEY_TILE, width), F32),
                 pltpu.VMEM((KEY_TILE, width), F32),
@@ -432,15 +431,21 @@
         ),
         out_shape=[
             jax.ShapeDtypeStruct((width, rows), BF16),
-            jax.ShapeDtypeStruct((PROMPT, 2 * width), BF16),
-            jax.ShapeDtypeStruct((portion, 2 * width), BF16),
+            jax.ShapeDtypeStruct((PROMPT + portion, features), BF16),
+            jax.ShapeDtypeStruct((features, 2 * width), F32),
         ],
         compiler_params=pltpu.CompilerParams(dimension_semantics=("arbitrary",)),
         cost_estimate=pl.CostEstimate(
             flops=keys * HEAD_DIM * 40, transcendentals=keys, bytes_accessed=14 << 20
         ),
         name="attend_back",
-    )(meta, q_t, grad_t, q, grad, lse, inner, prompt, prompt, own, own)
+    )(meta, q_t, grad_t, q, grad, lse, inner, near, far, spread)
+
+
+def paired_columns(portion):
+    return (
+        lax.axis_size("row") == 4 and lax.axis_size("col") == 8 and PROMPT // portion == 8
+    )
 
 
 def key_layout(block_order, portion):
@@ -454,8 +459,15 @@
     parts = group * portions + jnp.arange(portions, dtype=jnp.int32)
     sources = jnp.sum(jnp.where(block_order[None, :] == parts[:, None], slots[None, :], 0), axis=1)
     split = portion // KEY_TILE
-    tiles = (sources - base)[:, None] * split + jnp.arange(split, dtype=jnp.int32)[None, :]
-    return jnp.concatenate([tiles.reshape(-1), place[None]]).astype(jnp.int32)
+    prompt_tiles = portions * split
+    if paired_columns(portion):
+        apart = sources ^ column
+        tiles = jnp.where(apart % 2 == 0, apart // 2, 5 + apart // 2)
+        own = jnp.full((1,), 4, jnp.int32)
+    else:
+        tiles = (sources - base)[:, None] * split + jnp.arange(split, dtype=jnp.int32)[None, :]
+        own = prompt_tiles + jnp.arange(split, dtype=jnp.int32)
+    return jnp.concatenate([tiles.reshape(-1), own, place[None]]).astype(jnp.int32)
 
 
 def bit_of(value, bit):
@@ -497,17 +509,51 @@
     return buffer
 
 
+def gather_latents(part):
+    portion = part.shape[0] // 2
+    if not paired_columns(portion):
+        whole = lax.all_gather(part, "row", axis=1, tiled=True)
+        return gather_prompt(whole[:portion]), whole[portion:]
+    held = part[:portion]
+    held = jnp.concatenate([held, across(held, 2)], axis=0)
+    held = jnp.concatenate([held, across(held, 4), part[portion:]], axis=0)
+    near = jnp.concatenate(
+        [jnp.concatenate(piece, axis=0) for piece in gather_pieces(held)], axis=1
+    )
+    return near, across(near[: 4 * portion], 1)
+
+
+def scatter_latents(grad, portion):
+    if not paired_columns(portion):
+        prompt = scatter_prompt(grad[:PROMPT], portion)
+        whole = jnp.concatenate([prompt, grad[PROMPT:]], axis=0)
+        return lax.psum_scatter(whole, "row", scatter_dimension=1, tiled=True)
+    here = 4 * portion
+    near = grad[: here + portion]
+    got = across(grad[here + portion :], 1)
+    near = jnp.concatenate([add_low(near[:here], got), near[here:]], axis=0)
+    width = near.shape[1] // 4
+    mine = scatter_pieces([near[:, j * width : (j + 1) * width] for j in range(4)])
+    low = mine[:here].astype(BF16)
+    blocks = [low[j * portion : (j + 1) * portion] for j in range(4)]
+    got = across(jnp.concatenate([blocks[1], blocks[3]], axis=0), 2)
+    other = across(add_low(blocks[2], got[portion:]), 4)
+    prompt = mine[:portion] + got[:portion].astype(F32) + other.astype(F32)
+    return jnp.concatenate([prompt.astype(BF16), mine[here:].astype(BF16)], axis=0)
+
+
+def near_features(table, portion):
+    if not paired_columns(portion):
+        return table
+    here = lax.axis_index("row")
+    count = table.shape[0] // 4
+    return jnp.concatenate(
+        [lax.dynamic_slice_in_dim(table, (here ^ j) * count, count, 0) for j in range(4)], axis=0
+    )
+
+
 def padded(block, width):
     return jnp.pad(block, ((0, 0), (0, width - block.shape[1])))
-
-
-def to_strips(block, rows):
-    count = block.shape[0]
-    strips = [block[:, i : i + 128] for i in range(0, block.shape[1], 128)]
-    tall = jnp.concatenate(strips, axis=0)
-    return jnp.concatenate(
-        [tall[i : i + rows] for i in range(0, tall.shape[0], rows)], axis=1
-    ) if tall.shape[0] != rows else tall
 
 
 def head_mask(width):
@@ -563,21 +609,20 @@
     portion = block // 2
     mask = head_mask(width)
     spread = jnp.where(mask, jnp.concatenate([pair_full] * LATENT_HEADS, axis=0), jnp.zeros((), BF16))
+    spread = near_features(spread, portion)
     latent_part = dot(normed_block, latent_full, 1, 0).astype(BF16)
-    latent_all = gather_features(latent_part)
-    pairs = dot(latent_all, spread, 1, 0).astype(BF16)
-    own = pairs[portion:]
-    prompt = gather_prompt(pairs[:portion])
+    cotangent_later, latent_part = lax.optimization_barrier((cotangent, latent_part))
+    cot_block = gather_near(cotangent_later)
+    near, far = gather_latents(latent_part)
     scale = HEAD_DIM**-0.5
     queries_t = (dot(query_full, normed_block, 0, 1).astype(BF16) * scale).astype(BF16)
     queries = (dot(normed_block, query_full, 1, 0).astype(BF16) * scale).astype(BF16)
     meta = key_layout(block_order, portion)
-    late, prompt_first = lax.optimization_barrier((late, prompt[:8]))
+    late, near, far, cot_block = lax.optimization_barrier((late, near, far, cot_block))
     late_all = lax.all_gather(late, "col", axis=0, tiled=True)
     wide_full = late_all[:, : 2 * units]
     down_full = late_all[:, 2 * units :]
-    cot_block = gather_near(cotangent)
-    result_t, attended_t, lse = attend(meta, queries_t, prompt, own)
+    result_t, attended_t, lse = attend(meta, queries_t, near, far, spread, portion)
     branch = dot(attended_t, output_full, 0, 1)
     hidden = rows + scatter_true(branch)
 
@@ -593,7 +638,6 @@
     up_grad = (act_grad * gate * sigma).astype(BF16)
     both_grad = jnp.concatenate([gate_grad, up_grad], axis=1)
     normed2_grad = scatter_near(dot(both_grad, wide_full, 1, 1))
-    layer = hidden + scatter_near(dot(act, down_full, 1, 1))
     late_terms = jnp.concatenate(
         [
             dot(normed2_block, both_grad, 0, 0).astype(BF16),
@@ -606,29 +650,27 @@
     hidden_grad = cotangent.astype(F32) + norm2_grad
 
     branch_block = gather_true(hidden_grad.astype(BF16))
+    act, branch_block = lax.optimization_barrier((act, branch_block))
+    layer = hidden + scatter_near(dot(act, down_full, 1, 1))
     attended_grad = dot(branch_block, output_full, 1, 0).astype(BF16)
     attended_grad_t = dot(output_full, branch_block, 0, 1).astype(BF16)
     inner = jnp.sum(
         (attended_grad_t.astype(F32) * result_t).reshape(-1, HEAD_DIM, block), axis=1
     )
     inner = jnp.pad(inner, ((0, 8 - inner.shape[0]), (0, 0)))
-    query_grad_t, prompt_grad, own_grad = attend_back(
-        meta, queries_t, attended_grad_t, queries, attended_grad, lse, inner, prompt, own
-    )
+    query_grad_t, latent_terms, pair_big = attend_back(
+        meta, queries_t, attended_grad_t, queries, attended_grad, lse, inner, near, far, spread,
+        portion,
+    )
+    latent_grad = scatter_latents(latent_terms, portion)
     output_term = dot(branch_block, attended_t, 0, 1).astype(BF16)
     query_term = dot(normed_block, query_grad_t, 0, 1).astype(BF16)
-    pair_grad = jnp.concatenate([scatter_prompt(prompt_grad, portion), own_grad], axis=0)
-    latent_grad = scatter_features(dot(pair_grad, spread, 1, 1))
-    pair_big = dot(latent_all, pair_grad, 0, 0)
+    pair_big = near_features(pair_big, portion)
     pair_term = jnp.where(mask[:LATENT], pair_big[:LATENT], pair_big[LATENT:]).astype(BF16)
-    normed_grad = scatter_true(
-        dot(query_grad_t, query_full, 0, 1) + dot(latent_grad, latent_full, 1, 1)
-    )
-    latent_term = dot(normed_block, latent_grad, 0, 0).astype(BF16)
     pair_terms = pair_term.reshape(columns, pair_rows, strips, 128)
     pair_terms = jnp.concatenate([pair_terms[:, :, i] for i in range(strips)], axis=1)
     pair_terms = pair_terms.reshape(columns * strips * pair_rows, 128)
-    early_terms = jnp.concatenate([query_term, latent_term, output_term], axis=1)
+    early_terms = jnp.concatenate([query_term, output_term], axis=1)
     if pair_flat.shape[0] == share:
         early_sums = lax.psum_scatter(
             jnp.concatenate([early_terms, pair_terms], axis=1),
@@ -642,6 +684,10 @@
         pair_sums = lax.psum_scatter(
             pair_terms, "col", scatter_dimension=0, tiled=True
         ).astype(F32)
+    latent_sums = scatter_columns(dot(normed_block, latent_grad, 0, 0))
+    normed_grad = scatter_true(
+        dot(query_grad_t, query_full, 0, 1) + dot(latent_grad, latent_full, 1, 1)
+    )
     norm1_grad, first_gain_term = norm_backward(rows, first_scale, first_gain, normed_grad)
     input_gradient = hidden_grad + norm1_grad
     gains = all_sum(jnp.stack([first_gain_term, second_gain_term]))
@@ -653,10 +699,10 @@
         input_gradient,
         gains[0],
         early_sums[:, :width],
-        early_sums[:, width : width + features],
+        latent_sums,
         pair_sum[:, :width],
         pair_sum[:, width:],
-        early_sums[:, width + features : 2 * width + features].T,
+        early_sums[:, width : 2 * width].T,
         gains[1],
         late_sums[:, :hidden_units],
         late_sums[:, units : units + hidden_units],

time: 574 us -> 565 us (0.984)
  waiting for transfers between devices: 280 us -> 239 us
  starting transfers between devices: 57.3 us -> 86.1 us
  other arithmetic: 34.2 us -> 49.8 us
  matrix products: 56 us -> 47.9 us
    reduce_scatter x1 -> x0, waiting for transfers between devices: 69.4 us -> none  [scatter_prompt(): return lax.psum_scatter(buffer, 'col', scatter_dimension=0, tiled=True)]
    ppermute x40 -> x43, waiting for transfers between devices: 151 us -> 207 us  [exchange(): lax.ppermute(block, 'row', [(i, i ^ mask) for i in range(lax.axis_size('r...]
    all_gather x1 -> x0, waiting for transfers between devices: 39.8 us -> none  [gather_prompt(): return lax.all_gather(held, 'col', axis=0, tiled=True)]
    ppermute x5 -> x14, waiting for transfers between devices: 6.92 us -> 31.9 us  [across(): lax.ppermute(block, 'col', [(i, i ^ mask) for i in range(lax.axis_size('c...]
    ppermute x5 -> x14, starting transfers between devices: 9.65 us -> 32.8 us  [across(): lax.ppermute(block, 'col', [(i, i ^ mask) for i in range(lax.axis_size('c...]
    unnamed x7 -> x5, waiting for transfers between devices: 12.6 us -> 0.07 us
    pallas_call x1, Pallas kernels: 42.9 us -> 30.6 us  [attend(): pl.pallas_call(functools.partial(attend_kernel, heads=heads, prompt_tiles...]
    pallas_call x1, Pallas kernels: 48.8 us -> 59 us  [attend_back(): pl.pallas_call(functools.partial(attend_back_kernel, heads=heads, prompt_...]
  transfers between devices with their start and end apart: 51 -> 61, of which waited for: 40 -> 42; matrix products, arithmetic and copies ran while one was open for 16% -> 15% of each run, Pallas kernels for 7% -> 5%
where the time goes in v2:
time: 565 us; the launch traced here: 563 us
  waiting for transfers between devices  239 us (42%)
  Pallas kernels  89.6 us (16%)
  starting transfers between devices  86.1 us (15%)
  other arithmetic  49.8 us (9%)
  matrix products  47.9 us (8%)
  local copies, waits for them, and re-layouts  32.4 us (6%)
  between operations  17.8 us (3%)
    ppermute x43, waiting for transfers between devices, exchange(): lax.ppermute(block, 'row', [(i, i ^ mask) for i in range(lax.axis_size('r...  207 us
    pallas_call x1, Pallas kernels, attend_back(): pl.pallas_call(functools.partial(attend_back_kernel, heads=heads, prompt_...  59 us
    ppermute x43, starting transfers between devices, exchange(): lax.ppermute(block, 'row', [(i, i ^ mask) for i in range(lax.axis_size('r...  52.9 us
    dot_general x17, matrix products, dot(): lax.dot_general(left, right, (((left_dim,), (right_dim,)), ((), ())), pre...  47.9 us
    ppermute x14, starting transfers between devices, across(): lax.ppermute(block, 'col', [(i, i ^ mask) for i in range(lax.axis_size('c...  32.8 us
    ppermute x14, waiting for transfers between devices, across(): lax.ppermute(block, 'col', [(i, i ^ mask) for i in range(lax.axis_size('c...  31.9 us
    pallas_call x1, Pallas kernels, attend(): pl.pallas_call(functools.partial(attend_kernel, heads=heads, prompt_tiles...  30.6 us
    unnamed x108, local copies, waits for them, and re-layouts  16.2 us
  transfers between devices with their start and end apart: 61, of which 42 were waited for; matrix products, arithmetic and copies ran while one was open for 15% of the time, Pallas kernels for 5%

profile of v2, /device:TPU:0, one launch (start us, length us, event | category | flops | bytes accessed | tf_op | source)
XLA Modules:
  0.0 562.9 jit_solution(9058442647438033989)
XLA Ops:
  16.6 6.3 %collective-permute-done.1 = bf16[128,1024]{1,0:T(8,128)(2,1)S(1)} collective-permute-done((bf16[128,1024]{1,0:T(8,128)(2,1)S(1)}, bf16[128,1024]{1,0:T(8,128)(2,1)S(1)}, u32[]{:S(2)}, u32[]{:S(2)}) %collective-permute-start.1) | collective-permute-done | bytes 262176 | tf_op jit(solution)/shard_map/ppermute | solution.py:44
  25.1 12.8 %collective-permute-done.2 = bf16[256,1024]{1,0:T(8,128)(2,1)S(1)} collective-permute-done((bf16[256,1024]{1,0:T(8,128)(2,1)S(1)}, bf16[256,1024]{1,0:T(8,128)(2,1)S(1)}, u32[]{:S(2)}, u32[]{:S(2)}) %collective-permute-start.2) | collective-permute-done | bytes 524320 | tf_op jit(solution)/shard_map/ppermute | solution.py:44
  44.2 10.8 %collective-permute-done.3 = bf16[256,1024]{1,0:T(8,128)(2,1)S(1)} collective-permute-done((bf16[256,1024]{1,0:T(8,128)(2,1)S(1)}, bf16[256,1024]{1,0:T(8,128)(2,1)S(1)}, u32[]{:S(2)}, u32[]{:S(2)}) %collective-permute-start.3) | collective-permute-done | bytes 524320 | tf_op jit(solution)/shard_map/ppermute | solution.py:44
  67.6 7.6 %collective-permute-done.5 = bf16[1024,128]{1,0:T(8,128)(2,1)S(1)} collective-permute-done((bf16[1024,128]{1,0:T(8,128)(2,1)S(1)}, bf16[1024,128]{1,0:T(8,128)(2,1)S(1)}, u32[]{:S(2)}, u32[]{:S(2)}) %collective-permute-start.5) | collective-permute-done | bytes 262176 | tf_op jit(solution)/shard_map/ppermute | solution.py:116
  89.5 11.1 %collective-permute-done.9 = bf16[2560,128]{1,0:T(8,128)(2,1)S(1)} collective-permute-done((bf16[2560,128]{1,0:T(8,128)(2,1)S(1)}, bf16[2560,128]{1,0:T(8,128)(2,1)S(1)}, u32[]{:S(2)}, u32[]{:S(2)}) %collective-permute-start.9) | collective-permute-done | bytes 655392 | tf_op jit(solution)/shard_map/ppermute | solution.py:44
  100.7 6.0 %maximum_maximum_fusion.near = bf16[2560,512]{1,0:T(8,128)(2,1)S(1)} fusion(bf16[1280,128]{1,0:T(8,128)(2,1)S(1)} %get-tuple-element.140, bf16[1280,128]{1,0:T(8,128)(2,1)S(1)} %get-tuple-element.142, bf16[1280,128]{1,0:T(8,128)(2,1)S(1)} %collective-permute-done.7, bf16[1280,128]{1,0:T(8,128)(2,1)S(1)} %get-tuple-element.141, ...), kind=kLoop, calls=%fused_computation.13 | loop fusion | flops 20971520 | bytes 5242880 | tf_op jit(solution)/shard_map/concatenate | solution.py:520
  116.0 6.1 %collective-permute-done.11 = bf16[128,1024]{1,0:T(8,128)(2,1)S(1)} collective-permute-done((bf16[128,1024]{1,0:T(8,128)(2,1)S(1)}, bf16[128,1024]{1,0:T(8,128)(2,1)S(1)}, u32[]{:S(2)}, u32[]{:S(2)}) %collective-permute-start.11) | collective-permute-done | bytes 262176 | tf_op jit(solution)/shard_map/ppermute | solution.py:44
  124.5 8.3 %collective-permute-done.13 = bf16[256,1024]{1,0:T(8,128)(2,1)S(1)} collective-permute-done((bf16[256,1024]{1,0:T(8,128)(2,1)}, bf16[256,1024]{1,0:T(8,128)(2,1)S(1)}, u32[]{:S(2)}, u32[]{:S(2)}) %collective-permute-start.13) | collective-permute-done | bytes 524320 | tf_op jit(solution)/shard_map/ppermute | solution.py:44
  142.2 30.6 %attend.1 = (f32[256,1024]{1,0:T(8,128)}, bf16[256,1024]{1,0:T(8,128)(2,1)}, f32[8,1024]{1,0:T(8,128)}) custom-call(s32[10]{0:T(128)} %pad_add_fusion.meta, bf16[256,1024]{1,0:T(8,128)(2,1)} %fusion.15.q_t, bf16[2560,512]{1,0:T(8,128)(2,1)} %copy-done.2, bf16[2048,512]{1,0:T(8,128)(2,1)} %collective-permute-done.10.far, ...), custom_call_target="tpu_custom_call" | custom-call | flops 14495514624 | bytes 8388608 | tf_op jit(solution)/shard_map/attend/pallas_call | solution.py:355
  177.1 7.2 %collective-permute-done.15 = bf16[256,1024]{1,0:T(8,128)(2,1)S(1)} collective-permute-done((bf16[256,1024]{1,0:T(8,128)(2,1)S(1)}, bf16[256,1024]{1,0:T(8,128)(2,1)S(1)}, u32[]{:S(2)}, u32[]{:S(2)}) %collective-permute-start.15) | collective-permute-done | bytes 524320 | tf_op jit(solution)/shard_map/ppermute | solution.py:44
  185.7 7.6 %collective-permute-done.16 = bf16[128,1024]{1,0:T(8,128)(2,1)S(1)} collective-permute-done((bf16[128,1024]{1,0:T(8,128)(2,1)S(1)}, bf16[128,1024]{1,0:T(8,128)(2,1)S(1)}, u32[]{:S(2)}, u32[]{:S(2)}) %collective-permute-start.16) | collective-permute-done | bytes 262176 | tf_op jit(solution)/shard_map/ppermute | solution.py:44
  212.9 10.4 %collective-permute-done.21 = bf16[256,1024]{1,0:T(8,128)(2,1)S(1)} collective-permute-done((bf16[256,1024]{1,0:T(8,128)(2,1)S(1)}, bf16[256,1024]{1,0:T(8,128)(2,1)S(1)}, u32[]{:S(2)}, u32[]{:S(2)}) %collective-permute-start.21) | collective-permute-done | bytes 524320 | tf_op jit(solution)/shard_map/ppermute | solution.py:44
  227.0 6.1 %fusion.2 = f32[1024,1536]{1,0:T(8,128)S(1)} fusion(bf16[1024,1024]{1,0:T(8,128)(2,1)} %slice_dynamic-update-slice_fusion, bf16[1024,2304]{0,1:T(8,128)(2,1)} %all-gather.5.cloned.1.call-done), kind=kOutput, calls=%fused_computation.11 | convolution fusion | flops 3221225472 | bytes 11534336 | tf_op jit(solution)/shard_map/dot_general | solution.py:25
  244.7 11.1 %collective-permute-done.23 = bf16[256,1024]{1,0:T(8,128)(2,1)S(1)} collective-permute-done((bf16[256,1024]{1,0:T(8,128)(2,1)S(1)}, bf16[256,1024]{1,0:T(8,128)(2,1)S(1)}, u32[]{:S(2)}, u32[]{:S(2)}) %collective-permute-start.23) | collective-permute-done | bytes 524320 | tf_op jit(solution)/shard_map/ppermute | solution.py:44
  258.5 6.3 %collective-permute-done.24 = bf16[128,1024]{1,0:T(8,128)(2,1)S(1)} collective-permute-done((bf16[128,1024]{1,0:T(8,128)(2,1)S(1)}, bf16[128,1024]{1,0:T(8,128)(2,1)S(1)}, u32[]{:S(2)}, u32[]{:S(2)}) %collective-permute-start.24) | collective-permute-done | bytes 262176 | tf_op jit(solution)/shard_map/ppermute | solution.py:44
  267.1 6.3 %collective-permute-done.26 = bf16[128,1024]{1,0:T(8,128)(2,1)S(1)} collective-permute-done((bf16[128,1024]{1,0:T(8,128)(2,1)S(1)}, bf16[128,1024]{1,0:T(8,128)(2,1)S(1)}, u32[]{:S(2)}, u32[]{:S(2)}) %collective-permute-start.26) | collective-permute-done | bytes 262176 | tf_op jit(solution)/shard_map/ppermute | solution.py:44
  277.0 6.1 %collective-permute-done.28 = bf16[128,1024]{1,0:T(8,128)(2,1)S(1)} collective-permute-done((bf16[128,1024]{1,0:T(8,128)(2,1)S(1)}, bf16[128,1024]{1,0:T(8,128)(2,1)S(1)}, u32[]{:S(2)}, u32[]{:S(2)}) %collective-permute-start.28) | collective-permute-done | bytes 262176 | tf_op jit(solution)/shard_map/ppermute | solution.py:44
  285.3 12.8 %collective-permute-done.29 = bf16[256,1024]{1,0:T(8,128)(2,1)S(1)} collective-permute-done((bf16[256,1024]{1,0:T(8,128)(2,1)S(1)}, bf16[256,1024]{1,0:T(8,128)(2,1)S(1)}, u32[]{:S(2)}, u32[]{:S(2)}) %collective-permute-start.29) | collective-permute-done | bytes 524320 | tf_op jit(solution)/shard_map/ppermute | solution.py:44
  304.5 8.1 %collective-permute-done.30 = bf16[256,1024]{1,0:T(8,128)(2,1)S(1)} collective-permute-done((bf16[256,1024]{1,0:T(8,128)(2,1)S(1)}, bf16[256,1024]{1,0:T(8,128)(2,1)S(1)}, u32[]{:S(2)}, u32[]{:S(2)}) %collective-permute-start.30) | collective-permute-done | bytes 524320 | tf_op jit(solution)/shard_map/ppermute | solution.py:44
  317.9 59.0 %attend_back.1 = (bf16[256,1024]{1,0:T(8,128)(2,1)}, bf16[4608,512]{1,0:T(8,128)(2,1)}, f32[512,512]{1,0:T(8,128)}) custom-call(s32[10]{0:T(128)} %pad_add_fusion.meta, bf16[256,1024]{1,0:T(8,128)(2,1)} %fusion.15.q_t, bf16[256,1024]{1,0:T(8,128)(2,1)} %copy-done.24, bf16[1024,256]{1,0:T(8,128)(2,1)} %fusion.16.q, ...), custom_call_target="tpu_custom_call" | custom-call | flops 36238786560 | bytes 14680064 | tf_op jit(solution)/shard_map/attend_back/pallas_call | solution.py:398
  391.0 18.8 %collective-permute-start.35 = (bf16[2048,512]{1,0:T(8,128)(2,1)S(1)}, bf16[2048,512]{1,0:T(8,128)(2,1)}, u32[]{:S(2)}, u32[]{:S(2)}) collective-permute-start(bf16[2048,512]{1,0:T(8,128)(2,1)S(1)} %slice.573), channel_id=1, source_target_pairs={{0,1},{1,0},{2,3},{3,2},{4,5},{5,4},{6,7},{7,6},{8,9},{9,8},{10,11... | collective-permute-start | bytes 6291464 | tf_op jit(solution)/shard_map/ppermute | solution.py:116
  432.7 7.3 %collective-permute-done.31 = bf16[256,1024]{1,0:T(8,128)(2,1)S(1)} collective-permute-done((bf16[256,1024]{1,0:T(8,128)(2,1)S(1)}, bf16[256,1024]{1,0:T(8,128)(2,1)S(1)}, u32[]{:S(2)}, u32[]{:S(2)}) %collective-permute-start.31) | collective-permute-done | bytes 524320 | tf_op jit(solution)/shard_map/ppermute | solution.py:44
  441.6 16.6 %collective-permute-done.32 = bf16[128,1024]{1,0:T(8,128)(2,1)} collective-permute-done((bf16[128,1024]{1,0:T(8,128)(2,1)S(1)}, bf16[128,1024]{1,0:T(8,128)(2,1)}, u32[]{:S(2)}, u32[]{:S(2)}) %collective-permute-start.32) | collective-permute-done | bytes 262176 | tf_op jit(solution)/shard_map/ppermute | solution.py:44
  480.1 13.0 %collective-permute-done.40 = bf16[1024,128]{1,0:T(8,128)(2,1)S(1)} collective-permute-done((bf16[1024,128]{1,0:T(8,128)(2,1)S(1)}, bf16[1024,128]{1,0:T(8,128)(2,1)S(1)}, u32[]{:S(2)}, u32[]{:S(2)}) %collective-permute-start.40) | collective-permute-done | bytes 262176 | tf_op jit(solution)/shard_map/ppermute | solution.py:116
  (363 shorter events, 248.8 us)
Async XLA Ops:
  7.2 49.4 %all-gather.3.cloned.1.call-start = ((), (), s32[]{:S(2)}) async-start(), calls=%async_computation.2 | async-start | bytes 1769472 | tf_op jit(solution)/shard_map/all_gather | solution.py:589
  10.6 216.4 %all-gather.5.cloned.1.call-start = ((), (), s32[]{:S(2)}) async-start(), calls=%async_computation.3 | async-start | bytes 5308416 | tf_op jit(solution)/shard_map/all_gather | solution.py:622
  23.0 14.9 %collective-permute-start.2 = (bf16[256,1024]{1,0:T(8,128)(2,1)S(1)}, bf16[256,1024]{1,0:T(8,128)(2,1)S(1)}, u32[]{:S(2)}, u32[]{:S(2)}) collective-permute-start(bf16[256,1024]{1,0:T(8,128)(2,1)S(1)} %pad_maximum_fusion.14), channel_id=1, source_target_pairs={{0,8},{8,0},{16,24},{24,16},{1,9},{9,1},{17,25},{25,17},{2,10},{10... | collective-permute-start | bytes 1572872 | tf_op jit(solution)/shard_map/ppermute | solution.py:44
  24.8 17.0 %collective-permute-start = (bf16[128,1024]{1,0:T(8,128)(2,1)S(1)}, bf16[128,1024]{1,0:T(8,128)(2,1)S(1)}, u32[]{:S(2)}, u32[]{:S(2)}) collective-permute-start(bf16[128,1024]{1,0:T(8,128)(2,1)S(1)} %get-tuple-element.163), channel_id=1, source_target_pairs={{0,8},{8,0},{16,24},{24,16},{1,9},{9,1},{17,25},{25,17},{2,10},{10... | collective-permute-start | bytes 786440 | tf_op jit(solution)/shard_map/ppermute | solution.py:44
  83.0 17.5 %collective-permute-start.9 = (bf16[2560,128]{1,0:T(8,128)(2,1)S(1)}, bf16[2560,128]{1,0:T(8,128)(2,1)S(1)}, u32[]{:S(2)}, u32[]{:S(2)}) collective-permute-start(bf16[2560,128]{1,0:T(8,128)(2,1)S(1)} %pad_maximum_fusion.11), channel_id=1, source_target_pairs={{0,16},{8,24},{16,0},{24,8},{1,17},{9,25},{17,1},{25,9},{2,18},{10... | collective-permute-start | bytes 1966088 | tf_op jit(solution)/shard_map/ppermute | solution.py:44
  85.5 15.1 %collective-permute-start.8 = (bf16[2560,128]{1,0:T(8,128)(2,1)S(1)}, bf16[2560,128]{1,0:T(8,128)(2,1)S(1)}, u32[]{:S(2)}, u32[]{:S(2)}) collective-permute-start(bf16[2560,128]{1,0:T(8,128)(2,1)S(1)} %pad_maximum_fusion.10), channel_id=1, source_target_pairs={{0,8},{8,0},{16,24},{24,16},{1,9},{9,1},{17,25},{25,17},{2,10},{10... | collective-permute-start | bytes 1966088 | tf_op jit(solution)/shard_map/ppermute | solution.py:44
  87.1 26.8 %collective-permute-start.12 = (bf16[128,1024]{1,0:T(8,128)(2,1)S(1)}, bf16[128,1024]{1,0:T(8,128)(2,1)S(1)}, u32[]{:S(2)}, u32[]{:S(2)}) collective-permute-start(bf16[128,1024]{1,0:T(8,128)(2,1)S(1)} %get-tuple-element.157), channel_id=1, source_target_pairs={{0,16},{8,24},{16,0},{24,8},{1,17},{9,25},{17,1},{25,9},{2,18},{10... | collective-permute-start | bytes 786440 | tf_op jit(solution)/shard_map/ppermute | solution.py:44
  108.8 28.9 %collective-permute-start.10 = (bf16[2048,512]{1,0:T(8,128)(2,1)}, bf16[2048,512]{1,0:T(8,128)(2,1)}, u32[]{:S(2)}, u32[]{:S(2)}) collective-permute-start(bf16[2048,512]{1,0:T(8,128)(2,1)} %slice.638), channel_id=1, source_target_pairs={{0,1},{1,0},{2,3},{3,2},{4,5},{5,4},{6,7},{7,6},{8,9},{9,8},{10,11... | collective-permute-start | bytes 6291464 | tf_op jit(solution)/shard_map/ppermute | solution.py:116
  114.7 18.2 %collective-permute-start.13 = (bf16[256,1024]{1,0:T(8,128)(2,1)}, bf16[256,1024]{1,0:T(8,128)(2,1)S(1)}, u32[]{:S(2)}, u32[]{:S(2)}) collective-permute-start(bf16[256,1024]{1,0:T(8,128)(2,1)} %pad_maximum_fusion.18), channel_id=1, source_target_pairs={{0,8},{8,0},{16,24},{24,16},{1,9},{9,1},{17,25},{25,17},{2,10},{10... | collective-permute-start | bytes 1572872 | tf_op jit(solution)/shard_map/ppermute | solution.py:44
  137.7 341.3 %reduce-scatter.7.cloned.1.call-start = ((), (), s32[]{:S(2)}) async-start(), calls=%async_computation.5 | async-start | bytes 1474560
  242.1 13.7 %collective-permute-start.23 = (bf16[256,1024]{1,0:T(8,128)(2,1)S(1)}, bf16[256,1024]{1,0:T(8,128)(2,1)S(1)}, u32[]{:S(2)}, u32[]{:S(2)}) collective-permute-start(bf16[256,1024]{1,0:T(8,128)(2,1)S(1)} %pad_maximum_fusion.25), channel_id=1, source_target_pairs={{0,16},{8,24},{16,0},{24,8},{1,17},{9,25},{17,1},{25,9},{2,18},{10... | collective-permute-start | bytes 1572872 | tf_op jit(solution)/shard_map/ppermute | solution.py:44
  243.9 14.6 %collective-permute-start.25 = (bf16[256,1024]{1,0:T(8,128)(2,1)S(1)}, bf16[256,1024]{1,0:T(8,128)(2,1)S(1)}, u32[]{:S(2)}, u32[]{:S(2)}) collective-permute-start(bf16[256,1024]{1,0:T(8,128)(2,1)S(1)} %pad_maximum_fusion.26), channel_id=1, source_target_pairs={{0,8},{8,0},{16,24},{24,16},{1,9},{9,1},{17,25},{25,17},{2,10},{10... | collective-permute-start | bytes 1572872 | tf_op jit(solution)/shard_map/ppermute | solution.py:44
  283.2 14.9 %collective-permute-start.29 = (bf16[256,1024]{1,0:T(8,128)(2,1)S(1)}, bf16[256,1024]{1,0:T(8,128)(2,1)S(1)}, u32[]{:S(2)}, u32[]{:S(2)}) collective-permute-start(bf16[256,1024]{1,0:T(8,128)(2,1)S(1)} %pad_maximum_fusion.16), channel_id=1, source_target_pairs={{0,8},{8,0},{16,24},{24,16},{1,9},{9,1},{17,25},{25,17},{2,10},{10... | collective-permute-start | bytes 1572872 | tf_op jit(solution)/shard_map/ppermute | solution.py:44
  284.5 16.6 %collective-permute-start.27 = (bf16[128,1024]{1,0:T(8,128)(2,1)S(1)}, bf16[128,1024]{1,0:T(8,128)(2,1)S(1)}, u32[]{:S(2)}, u32[]{:S(2)}) collective-permute-start(bf16[128,1024]{1,0:T(8,128)(2,1)S(1)} %get-tuple-element.149), channel_id=1, source_target_pairs={{0,8},{8,0},{16,24},{24,16},{1,9},{9,1},{17,25},{25,17},{2,10},{10... | collective-permute-start | bytes 786440 | tf_op jit(solution)/shard_map/ppermute | solution.py:44
  384.9 167.2 %reduce-scatter.5.cloned.1.call-start = ((), (), s32[]{:S(2)}) async-start(), calls=%async_computation.4 | async-start | bytes 5308416 | tf_op jit(solution)/shard_map/reduce_scatter | solution.py:648
  391.0 35.2 %collective-permute-start.35 = (bf16[2048,512]{1,0:T(8,128)(2,1)S(1)}, bf16[2048,512]{1,0:T(8,128)(2,1)}, u32[]{:S(2)}, u32[]{:S(2)}) collective-permute-start(bf16[2048,512]{1,0:T(8,128)(2,1)S(1)} %slice.573), channel_id=1, source_target_pairs={{0,1},{1,0},{2,3},{3,2},{4,5},{5,4},{6,7},{7,6},{8,9},{9,8},{10,11... | collective-permute-start | bytes 6291464 | tf_op jit(solution)/shard_map/ppermute | solution.py:116
  423.9 17.8 %collective-permute-start.33 = (bf16[256,1024]{1,0:T(8,128)(2,1)}, bf16[256,1024]{1,0:T(8,128)(2,1)}, u32[]{:S(2)}, u32[]{:S(2)}) collective-permute-start(bf16[256,1024]{1,0:T(8,128)(2,1)} %pad_maximum_fusion.29), channel_id=1, source_target_pairs={{0,8},{8,0},{16,24},{24,16},{1,9},{9,1},{17,25},{25,17},{2,10},{10... | collective-permute-start | bytes 1572872 | tf_op jit(solution)/shard_map/ppermute | solution.py:44
  425.2 14.9 %collective-permute-start.31 = (bf16[256,1024]{1,0:T(8,128)(2,1)S(1)}, bf16[256,1024]{1,0:T(8,128)(2,1)S(1)}, u32[]{:S(2)}, u32[]{:S(2)}) collective-permute-start(bf16[256,1024]{1,0:T(8,128)(2,1)S(1)} %pad_maximum_fusion.28), channel_id=1, source_target_pairs={{0,16},{8,24},{16,0},{24,8},{1,17},{9,25},{17,1},{25,9},{2,18},{10... | collective-permute-start | bytes 1572872 | tf_op jit(solution)/shard_map/ppermute | solution.py:44
  430.0 30.6 %collective-permute-start.38 = (bf16[2560,128]{1,0:T(8,128)(2,1)}, bf16[2560,128]{1,0:T(8,128)(2,1)}, u32[]{:S(2)}, u32[]{:S(2)}) collective-permute-start(bf16[2560,128]{1,0:T(8,128)(2,1)} %fusion.31), channel_id=1, source_target_pairs={{0,8},{8,0},{16,24},{24,16},{1,9},{9,1},{17,25},{25,17},{2,10},{10... | collective-permute-start | bytes 1966088 | tf_op jit(solution)/shard_map/ppermute | solution.py:44
  431.5 29.1 %collective-permute-start.36 = (bf16[2560,128]{1,0:T(8,128)(2,1)}, bf16[2560,128]{1,0:T(8,128)(2,1)}, u32[]{:S(2)}, u32[]{:S(2)}) collective-permute-start(bf16[2560,128]{1,0:T(8,128)(2,1)} %pad_maximum_fusion.12), channel_id=1, source_target_pairs={{0,16},{8,24},{16,0},{24,8},{1,17},{9,25},{17,1},{25,9},{2,18},{10... | collective-permute-start | bytes 1966088 | tf_op jit(solution)/shard_map/ppermute | solution.py:44
  440.9 17.4 %collective-permute-start.32 = (bf16[128,1024]{1,0:T(8,128)(2,1)S(1)}, bf16[128,1024]{1,0:T(8,128)(2,1)}, u32[]{:S(2)}, u32[]{:S(2)}) collective-permute-start(bf16[128,1024]{1,0:T(8,128)(2,1)S(1)} %add_convert_fusion.8), channel_id=1, source_target_pairs={{0,8},{8,0},{16,24},{24,16},{1,9},{9,1},{17,25},{25,17},{2,10},{10... | collective-permute-start | bytes 786440 | tf_op jit(solution)/shard_map/ppermute | solution.py:44
  477.8 15.3 %collective-permute-start.40 = (bf16[1024,128]{1,0:T(8,128)(2,1)S(1)}, bf16[1024,128]{1,0:T(8,128)(2,1)S(1)}, u32[]{:S(2)}, u32[]{:S(2)}) collective-permute-start(bf16[1024,128]{1,0:T(8,128)(2,1)S(1)} %pad_maximum_fusion.37), channel_id=1, source_target_pairs={{0,2},{1,3},{2,0},{3,1},{4,6},{5,7},{6,4},{7,5},{8,10},{9,11},{10,... | collective-permute-start | bytes 786440 | tf_op jit(solution)/shard_map/ppermute | solution.py:116
  505.0 13.5 %collective-permute-start.42 = (bf16[256,1024]{1,0:T(8,128)(2,1)}, bf16[256,1024]{1,0:T(8,128)(2,1)}, u32[]{:S(2)}, u32[]{:S(2)}) collective-permute-start(bf16[256,1024]{1,0:T(8,128)(2,1)} %pad_maximum_fusion.30), channel_id=1, source_target_pairs={{0,16},{8,24},{16,0},{24,8},{1,17},{9,25},{17,1},{25,9},{2,18},{10... | collective-permute-start | bytes 1572872 | tf_op jit(solution)/shard_map/ppermute | solution.py:44
  511.0 14.9 %collective-permute-start.44 = (bf16[256,1024]{1,0:T(8,128)(2,1)S(1)}, bf16[256,1024]{1,0:T(8,128)(2,1)S(1)}, u32[]{:S(2)}, u32[]{:S(2)}) collective-permute-start(bf16[256,1024]{1,0:T(8,128)(2,1)S(1)} %pad_maximum_fusion.31), channel_id=1, source_target_pairs={{0,8},{8,0},{16,24},{24,16},{1,9},{9,1},{17,25},{25,17},{2,10},{10... | collective-permute-start | bytes 1572872 | tf_op jit(solution)/shard_map/ppermute | solution.py:44
  (81 other events, 745.7 us)
Sparse Core Ops, SparseCore 0:
  10.7 27.9 all-gather.2
  137.9 51.4 all-gather.4
  385.1 49.2 reduce-scatter.6
  436.6 58.7 reduce-scatter.4

commit v3 on v2

--- a/solution.py
+++ b/solution.py
@@ -44,25 +44,45 @@
     return lax.ppermute(block, "row", [(i, i ^ mask) for i in range(lax.axis_size("row"))])
 
 
-def gather_pieces(rows):
+def together(*values):
+    return lax.optimization_barrier(values)
+
+
+def gather_first(rows):
     half = rows.shape[0] // 2
-    low, high = rows[:half], rows[half:]
-    low_x = exchange(low, 1)
-    high_y = exchange(high, 2)
-    low_y = exchange(jnp.concatenate([low, low_x], axis=0), 2)
-    high_x = exchange(jnp.concatenate([high, high_y], axis=0), 1)
+    return exchange(rows[:half], 1), exchange(rows[half:], 2)
+
+
+def gather_second(rows, low_x, high_y):
+    half = rows.shape[0] // 2
+    low_y = exchange(jnp.concatenate([rows[:half], low_x], axis=0), 2)
+    high_x = exchange(jnp.concatenate([rows[half:], high_y], axis=0), 1)
+    return low_y, high_x
+
+
+def gather_order(rows, low_x, high_y, low_y, high_x):
+    half = rows.shape[0] // 2
     return [
-        (low, high),
+        (rows[:half], rows[half:]),
         (low_x, high_x[:half]),
         (low_y[:half], high_y),
         (low_y[half:], high_x[half:]),
     ]
 
 
+def gather_pieces(rows):
+    first = together(*gather_first(rows))
+    return gather_order(rows, *first, *together(*gather_second(rows, *first)))
+
+
+def join(pieces):
+    return jnp.concatenate([part for piece in pieces for part in piece], axis=0)
+
+
 def gather_near(rows):
     if lax.axis_size("row") != 4:
         return lax.all_gather(rows, "row", axis=0, tiled=True)
-    return jnp.concatenate([part for piece in gather_pieces(rows) for part in piece], axis=0)
+    return join(gather_pieces(rows))
 
 
 def gather_true(rows):
@@ -78,19 +98,36 @@
     return whole
 
 
+def scatter_first(pieces):
+    half = pieces[0].shape[0] // 2
+    return (
+        exchange(jnp.concatenate([pieces[2][:half], pieces[3][:half]], axis=0), 2),
+        exchange(jnp.concatenate([pieces[1][half:], pieces[3][half:]], axis=0), 1),
+    )
+
+
+def scatter_second(pieces, low_in, high_in):
+    half = pieces[0].shape[0] // 2
+    return (
+        exchange(add_low(pieces[1][:half], low_in[half:]), 1),
+        exchange(add_low(pieces[2][half:], high_in[half:]), 2),
+    )
+
+
+def scatter_last(pieces, low_in, high_in, low_last, high_last):
+    half = pieces[0].shape[0] // 2
+    low = pieces[0][:half].astype(F32) + low_in[:half].astype(F32) + low_last.astype(F32)
+    high = pieces[0][half:].astype(F32) + high_in[:half].astype(F32) + high_last.astype(F32)
+    return jnp.concatenate([low, high], axis=0)
+
+
 def scatter_pieces(pieces):
-    half = pieces[0].shape[0] // 2
-    low = [piece[:half] for piece in pieces]
-    high = [piece[half:] for piece in pieces]
-    low_in = exchange(jnp.concatenate([low[2], low[3]], axis=0), 2)
-    high_in = exchange(jnp.concatenate([high[1], high[3]], axis=0), 1)
-    low_on = (low[1].astype(F32) + low_in[half:].astype(F32)).astype(BF16)
-    high_on = (high[2].astype(F32) + high_in[half:].astype(F32)).astype(BF16)
-    low_last = exchange(low_on, 1)
-    high_last = exchange(high_on, 2)
-    low_sum = low[0].astype(F32) + low_in[:half].astype(F32) + low_last.astype(F32)
-    high_sum = high[0].astype(F32) + high_in[:half].astype(F32) + high_last.astype(F32)
-    return jnp.concatenate([low_sum, high_sum], axis=0)
+    first = together(*scatter_first(pieces))
+    return scatter_last(pieces, *first, *together(*scatter_second(pieces, *first)))
+
+
+def add_low(left, right):
+    return (left.astype(F32) + right.astype(F32)).astype(BF16)
 
 
 def scatter_near(part):
@@ -101,30 +138,25 @@
     return scatter_pieces([part[j * count : (j + 1) * count] for j in range(4)])
 
 
+def true_pieces(part):
+    count = part.shape[0] // 4
+    here = lax.axis_index("row")
+    return [lax.dynamic_slice_in_dim(part, (here ^ j) * count, count, 0) for j in range(4)]
+
+
 def scatter_true(part):
     part = part.astype(BF16)
     if lax.axis_size("row") != 4:
         return lax.psum_scatter(part, "row", scatter_dimension=0, tiled=True).astype(F32)
-    count = part.shape[0] // 4
-    here = lax.axis_index("row")
-    return scatter_pieces(
-        [lax.dynamic_slice_in_dim(part, (here ^ j) * count, count, 0) for j in range(4)]
-    )
+    return scatter_pieces(true_pieces(part))
 
 
 def across(block, mask):
     return lax.ppermute(block, "col", [(i, i ^ mask) for i in range(lax.axis_size("col"))])
 
 
-def add_low(left, right):
-    return (left.astype(F32) + right.astype(F32)).astype(BF16)
-
-
-def scatter_columns(part):
-    part = part.astype(BF16)
+def column_first(part):
     size = lax.axis_size("col")
-    if size != 8:
-        return lax.psum_scatter(part, "col", scatter_dimension=0, tiled=True).astype(F32)
     count = part.shape[0] // size
     here = lax.axis_index("col")
 
@@ -133,10 +165,18 @@
             [lax.dynamic_slice_in_dim(part, (here ^ j) * count, count, 0) for j in order], axis=0
         )
 
-    mine = pieces((0, 2, 4, 6)).astype(F32) + across(pieces((1, 3, 5, 7)), 1).astype(F32)
+    return pieces((0, 2, 4, 6)), across(pieces((1, 3, 5, 7)), 1)
+
+
+def column_second(mine, got):
+    count = mine.shape[0] // 4
+    mine = mine.astype(F32) + got.astype(F32)
     low = mine.astype(BF16)
-    got = [across(low[j * count : (j + 1) * count], 2 * j) for j in (1, 2, 3)]
-    return (mine[:count] + got[0].astype(F32)) + (got[1].astype(F32) + got[2].astype(F32))
+    return mine[:count], [across(low[j * count : (j + 1) * count], 2 * j) for j in (1, 2, 3)]
+
+
+def column_last(mine, got):
+    return (mine + got[0].astype(F32)) + (got[1].astype(F32) + got[2].astype(F32))
 
 
 def all_sum(value):
@@ -207,11 +247,11 @@
 
     @pl.when(place < near_tiles)
     def _():
-        latents[...] = near[...]
+        latents[...] = jnp.concatenate([near[j] for j in range(near.shape[0])], axis=1)
 
     @pl.when(place >= near_tiles)
     def _():
-        latents[...] = far[...]
+        latents[...] = jnp.concatenate([far[j] for j in range(far.shape[0])], axis=1)
 
     return dot(latents[...], spread[...], 1, 0).astype(BF16)
 
@@ -324,7 +364,9 @@
     visit_tiles(meta, step, prompt_tiles, portion, rows, body)
 
     pair_low = jnp.concatenate([key_acc[...].astype(BF16), value_acc[...].astype(BF16)], axis=1)
-    latent_grad[...] = dot(pair_low, spread[...], 1, 1).astype(BF16)
+    grads = dot(pair_low, spread[...], 1, 1).astype(BF16)
+    for j in range(latent_grad.shape[0]):
+        latent_grad[j] = grads[:, j * 128 : (j + 1) * 128]
     pair_grad[...] += dot(latents[...], pair_low, 0, 0)
 
     @pl.when(step == pl.num_programs(0) - 1)
@@ -337,11 +379,11 @@
 
 
 def latent_specs(near, far, spread):
-    near_tiles = near.shape[0] // KEY_TILE
-    tile = (KEY_TILE, near.shape[1])
+    near_tiles = near.shape[1] // KEY_TILE
+    tile = (near.shape[0], KEY_TILE, 128)
     return [
-        pl.BlockSpec(tile, lambda step, meta: (jnp.minimum(meta[step], near_tiles - 1), 0)),
-        pl.BlockSpec(tile, lambda step, meta: (jnp.maximum(meta[step] - near_tiles, 0), 0)),
+        pl.BlockSpec(tile, lambda step, meta: (0, jnp.minimum(meta[step], near_tiles - 1), 0)),
+        pl.BlockSpec(tile, lambda step, meta: (0, jnp.maximum(meta[step] - near_tiles, 0), 0)),
         whole_spec(spread.shape),
     ]
 
@@ -355,7 +397,7 @@
     return pl.pallas_call(
         functools.partial(
             attend_kernel, heads=heads, prompt_tiles=prompt_tiles,
-            near_tiles=near.shape[0] // KEY_TILE, portion=portion, rows=rows,
+            near_tiles=near.shape[1] // KEY_TILE, portion=portion, rows=rows,
         ),
         grid_spec=pltpu.PrefetchScalarGridSpec(
             num_scalar_prefetch=1,
@@ -367,7 +409,7 @@
                 whole_spec((8, rows)),
             ],
             scratch_shapes=[
-                pltpu.VMEM((KEY_TILE, near.shape[1]), BF16),
+                pltpu.VMEM((KEY_TILE, spread.shape[0]), BF16),
                 pltpu.VMEM((KEY_TILE, width), BF16),
                 pltpu.VMEM((width, KEY_TILE), BF16),
                 pltpu.VMEM((width, rows), F32),
@@ -391,14 +433,15 @@
 def attend_back(meta, q_t, grad_t, q, grad, lse, inner, near, far, spread, portion):
     width, rows = q_t.shape
     heads = width // HEAD_DIM
-    features = near.shape[1]
+    planes = near.shape[0]
+    features = spread.shape[0]
     prompt_tiles = PROMPT // KEY_TILE
     steps = prompt_tiles + portion // KEY_TILE
     keys = (PROMPT + portion) * rows * heads * 3 // 4
     return pl.pallas_call(
         functools.partial(
             attend_back_kernel, heads=heads, prompt_tiles=prompt_tiles,
-            near_tiles=near.shape[0] // KEY_TILE, portion=portion, rows=rows,
+            near_tiles=near.shape[1] // KEY_TILE, portion=portion, rows=rows,
         ),
         grid_spec=pltpu.PrefetchScalarGridSpec(
             num_scalar_prefetch=1,
@@ -414,7 +457,7 @@
             + latent_specs(near, far, spread),
             out_specs=[
                 whole_spec((width, rows)),
-                pl.BlockSpec((KEY_TILE, features), lambda step, meta: (meta[step], 0)),
+                pl.BlockSpec((planes, KEY_TILE, 128), lambda step, meta: (0, meta[step], 0)),
                 whole_spec((features, 2 * width)),
             ],
             scratch_shapes=[
@@ -431,7 +474,7 @@
         ),
         out_shape=[
             jax.ShapeDtypeStruct((width, rows), BF16),
-            jax.ShapeDtypeStruct((PROMPT + portion, features), BF16),
+            jax.ShapeDtypeStruct((planes, PROMPT + portion, 128), BF16),
             jax.ShapeDtypeStruct((features, 2 * width), F32),
         ],
         compiler_params=pltpu.CompilerParams(dimension_semantics=("arbitrary",)),
@@ -509,37 +552,56 @@
     return buffer
 
 
-def gather_latents(part):
+def planes_of(whole):
+    return jnp.stack([whole[:, j : j + 128] for j in range(0, whole.shape[1], 128)], axis=0)
+
+
+def gather_latents(part, beside):
     portion = part.shape[0] // 2
     if not paired_columns(portion):
         whole = lax.all_gather(part, "row", axis=1, tiled=True)
-        return gather_prompt(whole[:portion]), whole[portion:]
+        near = planes_of(gather_prompt(whole[:portion]))
+        return near, planes_of(whole[portion:]), near[:, :8], gather_near(beside)
     held = part[:portion]
-    held = jnp.concatenate([held, across(held, 2)], axis=0)
-    held = jnp.concatenate([held, across(held, 4), part[portion:]], axis=0)
-    near = jnp.concatenate(
-        [jnp.concatenate(piece, axis=0) for piece in gather_pieces(held)], axis=1
-    )
-    return near, across(near[: 4 * portion], 1)
-
-
-def scatter_latents(grad, portion):
+    beside, held = together(beside, held)
+    got, *first = together(across(held, 2), *gather_first(beside))
+    held = jnp.concatenate([held, got], axis=0)
+    got, *second = together(across(held, 4), *gather_second(beside, *first))
+    beside = join(gather_order(beside, *first, *second))
+    held = jnp.concatenate([held, got, part[portion:]], axis=0)
+    near = jnp.stack([jnp.concatenate(piece, axis=0) for piece in gather_pieces(held)], axis=0)
+    return near, across(near[:, : 4 * portion], 1), got, beside
+
+
+def scatter_latents(grad, portion, column_terms):
     if not paired_columns(portion):
-        prompt = scatter_prompt(grad[:PROMPT], portion)
-        whole = jnp.concatenate([prompt, grad[PROMPT:]], axis=0)
-        return lax.psum_scatter(whole, "row", scatter_dimension=1, tiled=True)
+        whole = jnp.concatenate([grad[j] for j in range(grad.shape[0])], axis=1)
+        prompt = scatter_prompt(whole[:PROMPT], portion)
+        whole = jnp.concatenate([prompt, whole[PROMPT:]], axis=0)
+        sums = lax.psum_scatter(
+            column_terms(), "col", scatter_dimension=0, tiled=True
+        ).astype(F32)
+        return lax.psum_scatter(whole, "row", scatter_dimension=1, tiled=True), sums
     here = 4 * portion
-    near = grad[: here + portion]
-    got = across(grad[here + portion :], 1)
-    near = jnp.concatenate([add_low(near[:here], got), near[here:]], axis=0)
-    width = near.shape[1] // 4
-    mine = scatter_pieces([near[:, j * width : (j + 1) * width] for j in range(4)])
+    got = across(grad[:, here + portion :], 1)
+    pieces = [
+        jnp.concatenate(
+            [add_low(grad[j, :here], got[j]), grad[j, here : here + portion]], axis=0
+        )
+        for j in range(4)
+    ]
+    terms, terms_got = column_first(column_terms())
+    terms_got, *first = together(terms_got, *scatter_first(pieces))
+    terms, terms_on = column_second(terms, terms_got)
+    *terms_on, low_last, high_last = together(*terms_on, *scatter_second(pieces, *first))
+    mine = scatter_last(pieces, *first, low_last, high_last)
     low = mine[:here].astype(BF16)
     blocks = [low[j * portion : (j + 1) * portion] for j in range(4)]
     got = across(jnp.concatenate([blocks[1], blocks[3]], axis=0), 2)
     other = across(add_low(blocks[2], got[portion:]), 4)
     prompt = mine[:portion] + got[:portion].astype(F32) + other.astype(F32)
-    return jnp.concatenate([prompt.astype(BF16), mine[here:].astype(BF16)], axis=0)
+    sums = column_last(terms, terms_on)
+    return jnp.concatenate([prompt.astype(BF16), mine[here:].astype(BF16)], axis=0), sums
 
 
 def near_features(table, portion):
@@ -611,14 +673,13 @@
     spread = jnp.where(mask, jnp.concatenate([pair_full] * LATENT_HEADS, axis=0), jnp.zeros((), BF16))
     spread = near_features(spread, portion)
     latent_part = dot(normed_block, latent_full, 1, 0).astype(BF16)
-    cotangent_later, latent_part = lax.optimization_barrier((cotangent, latent_part))
-    cot_block = gather_near(cotangent_later)
-    near, far = gather_latents(latent_part)
+    near, far, prompt_there, cot_block = gather_latents(latent_part, cotangent)
     scale = HEAD_DIM**-0.5
     queries_t = (dot(query_full, normed_block, 0, 1).astype(BF16) * scale).astype(BF16)
     queries = (dot(normed_block, query_full, 1, 0).astype(BF16) * scale).astype(BF16)
     meta = key_layout(block_order, portion)
-    late, near, far, cot_block = lax.optimization_barrier((late, near, far, cot_block))
+    late, _ = together(late, prompt_there)
+    queries_t, queries, cot_block = together(queries_t, queries, cot_block)
     late_all = lax.all_gather(late, "col", axis=0, tiled=True)
     wide_full = late_all[:, : 2 * units]
     down_full = late_all[:, 2 * units :]
@@ -645,6 +706,7 @@
         ],
         axis=1,
     )
+    late_terms, normed2_grad = together(late_terms, normed2_grad)
     late_sums = lax.psum_scatter(late_terms, "col", scatter_dimension=0, tiled=True).astype(F32)
     norm2_grad, second_gain_term = norm_backward(hidden, second_scale, second_gain, normed2_grad)
     hidden_grad = cotangent.astype(F32) + norm2_grad
@@ -662,32 +724,37 @@
         meta, queries_t, attended_grad_t, queries, attended_grad, lse, inner, near, far, spread,
         portion,
     )
-    latent_grad = scatter_latents(latent_terms, portion)
-    output_term = dot(branch_block, attended_t, 0, 1).astype(BF16)
-    query_term = dot(normed_block, query_grad_t, 0, 1).astype(BF16)
-    pair_big = near_features(pair_big, portion)
-    pair_term = jnp.where(mask[:LATENT], pair_big[:LATENT], pair_big[LATENT:]).astype(BF16)
-    pair_terms = pair_term.reshape(columns, pair_rows, strips, 128)
-    pair_terms = jnp.concatenate([pair_terms[:, :, i] for i in range(strips)], axis=1)
-    pair_terms = pair_terms.reshape(columns * strips * pair_rows, 128)
-    early_terms = jnp.concatenate([query_term, output_term], axis=1)
-    if pair_flat.shape[0] == share:
-        early_sums = lax.psum_scatter(
-            jnp.concatenate([early_terms, pair_terms], axis=1),
-            "col", scatter_dimension=0, tiled=True,
+    def column_terms():
+        output_term = dot(branch_block, attended_t, 0, 1).astype(BF16)
+        query_term = dot(normed_block, query_grad_t, 0, 1).astype(BF16)
+        pair_table = near_features(pair_big, portion)
+        pair_term = jnp.where(mask[:LATENT], pair_table[:LATENT], pair_table[LATENT:])
+        pair_terms = pair_term.astype(BF16).reshape(columns, pair_rows, strips, 128)
+        pair_terms = jnp.concatenate([pair_terms[:, :, i] for i in range(strips)], axis=1)
+        pair_terms = jnp.pad(pair_terms, ((0, 0), (0, share - strips * pair_rows), (0, 0)))
+        return jnp.concatenate(
+            [query_term, output_term, pair_terms.reshape(columns * share, 128)], axis=1
+        )
+
+    latent_grad, early_sums = scatter_latents(latent_terms, portion, column_terms)
+    pair_sums = early_sums[:, 2 * width :]
+    latent_term = dot(normed_block, latent_grad, 0, 0).astype(BF16)
+    norm_part = (
+        dot(query_grad_t, query_full, 0, 1) + dot(latent_grad, latent_full, 1, 1)
+    ).astype(BF16)
+    if paired_columns(portion):
+        mine, got = column_first(latent_term)
+        pieces = true_pieces(norm_part)
+        got, *first = together(got, *scatter_first(pieces))
+        mine, got = column_second(mine, got)
+        *got, low_last, high_last = together(*got, *scatter_second(pieces, *first))
+        latent_sums = column_last(mine, got)
+        normed_grad = scatter_last(pieces, *first, low_last, high_last)
+    else:
+        latent_sums = lax.psum_scatter(
+            latent_term, "col", scatter_dimension=0, tiled=True
         ).astype(F32)
-        pair_sums = early_sums[:, early_terms.shape[1] :]
-    else:
-        early_sums = lax.psum_scatter(
-            early_terms, "col", scatter_dimension=0, tiled=True
-        ).astype(F32)
-        pair_sums = lax.psum_scatter(
-            pair_terms, "col", scatter_dimension=0, tiled=True
-        ).astype(F32)
-    latent_sums = scatter_columns(dot(normed_block, latent_grad, 0, 0))
-    normed_grad = scatter_true(
-        dot(query_grad_t, query_full, 0, 1) + dot(latent_grad, latent_full, 1, 1)
-    )
+        normed_grad = scatter_true(norm_part)
     norm1_grad, first_gain_term = norm_backward(rows, first_scale, first_gain, normed_grad)
     input_gradient = hidden_grad + norm1_grad
     gains = all_sum(jnp.stack([first_gain_term, second_gain_term]))

time: 565 us -> 525 us (0.929); the launches traced: 563 us -> 517 us
  waiting for transfers between devices: 239 us -> 169 us
  other arithmetic: 49.8 us -> 63.7 us
  Pallas kernels: 89.6 us -> 101 us
  local copies, waits for them, and re-layouts: 32.4 us -> 40.9 us
  starting transfers between devices: 86.1 us -> 78.1 us
    ppermute x43, waiting for transfers between devices: 207 us -> 121 us  [exchange(): lax.ppermute(block, 'row', [(i, i ^ mask) for i in range(lax.axis_size('r...]
    ppermute x14 -> x18, waiting for transfers between devices: 31.9 us -> 48.4 us  [across(): lax.ppermute(block, 'col', [(i, i ^ mask) for i in range(lax.axis_size('c...]
    ppermute x43, starting transfers between devices: 52.9 us -> 43.2 us  [exchange(): lax.ppermute(block, 'row', [(i, i ^ mask) for i in range(lax.axis_size('r...]
    convert_element_type x2 -> x8, other arithmetic: 2.9 us -> 10.9 us  [add_low(): return (left.astype(F32) + right.astype(F32)).astype(BF16)]
    pallas_call x1, Pallas kernels: 59 us -> 66.7 us  [attend_back(): pl.pallas_call(functools.partial(attend_back_kernel, heads=heads, prompt_...]
    ppermute x14 -> x18, starting transfers between devices: 32.8 us -> 34.8 us  [across(): lax.ppermute(block, 'col', [(i, i ^ mask) for i in range(lax.axis_size('c...]
    concatenate x25 -> x23, other arithmetic: 12.9 us -> 11.1 us  [the longest x5 2.81 us: scatter_first(): jnp.concatenate([pieces[1][half:], pieces[3][half:]], axis=0)]
    unnamed x108 -> x132, local copies, waits for them, and re-layouts: 16.2 us -> 17.3 us
  transfers between devices with their start and end apart: 61 -> 64, of which waited for: 42 -> 42; matrix products, arithmetic and copies ran while one was open for 15% -> 19% of each run, Pallas kernels for 5% -> 7%
where the time goes in v3:
time: 525 us; the launch traced here: 517 us
  waiting for transfers between devices  169 us (32%)
  Pallas kernels  101 us (19%)
  starting transfers between devices  78.1 us (15%)
  other arithmetic  63.7 us (12%)
  matrix products  45.6 us (9%)
  local copies, waits for them, and re-layouts  40.9 us (8%)
  between operations  17.7 us (3%)
    ppermute x43, waiting for transfers between devices, exchange(): lax.ppermute(block, 'row', [(i, i ^ mask) for i in range(lax.axis_size('r...  121 us
    pallas_call x1, Pallas kernels, attend_back(): pl.pallas_call(functools.partial(attend_back_kernel, heads=heads, prompt_...  66.7 us
    ppermute x18, waiting for transfers between devices, across(): lax.ppermute(block, 'col', [(i, i ^ mask) for i in range(lax.axis_size('c...  48.4 us
    dot_general x17, matrix products, dot(): lax.dot_general(left, right, (((left_dim,), (right_dim,)), ((), ())), pre...  45.6 us
    ppermute x43, starting transfers between devices, exchange(): lax.ppermute(block, 'row', [(i, i ^ mask) for i in range(lax.axis_size('r...  43.2 us
    ppermute x18, starting transfers between devices, across(): lax.ppermute(block, 'col', [(i, i ^ mask) for i in range(lax.axis_size('c...  34.8 us
    pallas_call x1, Pallas kernels, attend(): pl.pallas_call(functools.partial(attend_kernel, heads=heads, prompt_tiles...  34.7 us
    unnamed x132, local copies, waits for them, and re-layouts  17.3 us
  transfers between devices with their start and end apart: 64, of which 42 were waited for; matrix products, arithmetic and copies ran while one was open for 19% of the time, Pallas kernels for 7%

profile of v3, /device:TPU:0, one launch (start us, length us, event | category | flops | bytes accessed | tf_op | source)
XLA Modules:
  0.0 516.7 jit_solution(11418705320510553262)
XLA Ops:
  18.3 4.8 collective-permute-done
  26.8 10.4 %collective-permute-done.3 = bf16[256,1024]{1,0:T(8,128)(2,1)S(1)} collective-permute-done((bf16[256,1024]{1,0:T(8,128)(2,1)S(1)}, bf16[256,1024]{1,0:T(8,128)(2,1)S(1)}, u32[]{:S(2)}, u32[]{:S(2)}) %collective-permute-start.3) | collective-permute-done | bytes 524320 | tf_op jit(solution)/shard_map/ppermute | solution.py:44
  61.1 8.0 %collective-permute-done.7 = bf16[1024,128]{1,0:T(8,128)(2,1)S(1)} collective-permute-done((bf16[1024,128]{1,0:T(8,128)(2,1)S(1)}, bf16[1024,128]{1,0:T(8,128)(2,1)S(1)}, u32[]{:S(2)}, u32[]{:S(2)}) %collective-permute-start.7) | collective-permute-done | bytes 262176 | tf_op jit(solution)/shard_map/ppermute | solution.py:155
  87.0 6.8 %collective-permute-done.12 = bf16[2560,128]{1,0:T(8,128)(2,1)S(1)} collective-permute-done((bf16[2560,128]{1,0:T(8,128)(2,1)S(1)}, bf16[2560,128]{1,0:T(8,128)(2,1)S(1)}, u32[]{:S(2)}, u32[]{:S(2)}) %collective-permute-start.12) | collective-permute-done | bytes 655392 | tf_op jit(solution)/shard_map/ppermute | solution.py:44
  109.4 34.7 %attend.1 = (f32[256,1024]{1,0:T(8,128)}, bf16[256,1024]{1,0:T(8,128)(2,1)}, f32[8,1024]{1,0:T(8,128)}) custom-call(s32[10]{0:T(128)} %pad_add_fusion.meta, bf16[256,1024]{1,0:T(8,128)(2,1)} %fusion.15.q_t, bf16[4,2560,128]{2,1,0:T(8,128)(2,1)} %copy-done.1, bf16[4,2048,128]{2,1,0:T(8,128)(2,1)} %collective-permute-done.14.far, ...), custom_call_target="tpu_custom_call" | custom-call | flops 14495514624 | bytes 8388608 | tf_op jit(solution)/shard_map/attend/pallas_call | solution.py:397
  147.8 8.3 %collective-permute-done.16 = bf16[256,1024]{1,0:T(8,128)(2,1)S(1)} collective-permute-done((bf16[256,1024]{1,0:T(8,128)(2,1)S(1)}, bf16[256,1024]{1,0:T(8,128)(2,1)S(1)}, u32[]{:S(2)}, u32[]{:S(2)}) %collective-permute-start.16) | collective-permute-done | bytes 524320 | tf_op jit(solution)/shard_map/ppermute | solution.py:44
  160.1 4.8 collective-permute-done.17
  169.8 6.1 %collective-permute-done.19 = bf16[128,1024]{1,0:T(8,128)(2,1)S(1)} collective-permute-done((bf16[128,1024]{1,0:T(8,128)(2,1)S(1)}, bf16[128,1024]{1,0:T(8,128)(2,1)S(1)}, u32[]{:S(2)}, u32[]{:S(2)}) %collective-permute-start.19) | collective-permute-done | bytes 262176 | tf_op jit(solution)/shard_map/ppermute | solution.py:44
  179.3 10.7 %collective-permute-done.22 = bf16[256,1024]{1,0:T(8,128)(2,1)S(1)} collective-permute-done((bf16[256,1024]{1,0:T(8,128)(2,1)S(1)}, bf16[256,1024]{1,0:T(8,128)(2,1)S(1)}, u32[]{:S(2)}, u32[]{:S(2)}) %collective-permute-start.22) | collective-permute-done | bytes 524320 | tf_op jit(solution)/shard_map/ppermute | solution.py:44
  196.4 6.1 %fusion.2 = f32[1024,1536]{1,0:T(8,128)S(1)} fusion(bf16[1024,1024]{1,0:T(8,128)(2,1)} %slice_dynamic-update-slice_fusion, bf16[1024,2304]{0,1:T(8,128)(2,1)} %all-gather.5.cloned.1.call-done), kind=kOutput, calls=%fused_computation.10 | convolution fusion | flops 3221225472 | bytes 11534336 | tf_op jit(solution)/shard_map/dot_general | solution.py:25
  210.3 6.0 %convolution_convert_fusion = bf16[1024,1536]{1,0:T(8,128)(2,1)S(1)} fusion(bf16[1024,1024]{1,0:T(8,128)(2,1)} %slice_dynamic-update-slice_fusion, bf16[1024,768]{1,0:T(8,128)(2,1)S(1)} %get-tuple-element.207, bf16[1024,768]{1,0:T(8,128)(2,1)S(1)} %get-tuple-element.206), kind=kOutput, calls=%fused_computation.2 | convolution fusion | flops 3229089792 | bytes 8388608 | tf_op jit(solution)/shard_map/dot_general | solution.py:25
  218.3 6.0 %collective-permute-done.24 = bf16[256,1024]{1,0:T(8,128)(2,1)S(1)} collective-permute-done((bf16[256,1024]{1,0:T(8,128)(2,1)S(1)}, bf16[256,1024]{1,0:T(8,128)(2,1)S(1)}, u32[]{:S(2)}, u32[]{:S(2)}) %collective-permute-start.24) | collective-permute-done | bytes 524320 | tf_op jit(solution)/shard_map/ppermute | solution.py:44
  240.9 5.2 %collective-permute-done.27 = bf16[128,1024]{1,0:T(8,128)(2,1)S(1)} collective-permute-done((bf16[128,1024]{1,0:T(8,128)(2,1)S(1)}, bf16[128,1024]{1,0:T(8,128)(2,1)S(1)}, u32[]{:S(2)}, u32[]{:S(2)}) %collective-permute-start.27) | collective-permute-done | bytes 262176 | tf_op jit(solution)/shard_map/ppermute | solution.py:44
  252.1 7.4 %collective-permute-done.30 = bf16[256,1024]{1,0:T(8,128)(2,1)} collective-permute-done((bf16[256,1024]{1,0:T(8,128)(2,1)}, bf16[256,1024]{1,0:T(8,128)(2,1)}, u32[]{:S(2)}, u32[]{:S(2)}) %collective-permute-start.30) | collective-permute-done | bytes 524320 | tf_op jit(solution)/shard_map/ppermute | solution.py:44
  272.4 66.7 %attend_back.1 = (bf16[256,1024]{1,0:T(8,128)(2,1)}, bf16[4,4608,128]{2,1,0:T(8,128)(2,1)}, f32[512,512]{1,0:T(8,128)}) custom-call(s32[10]{0:T(128)} %pad_add_fusion.meta, bf16[256,1024]{1,0:T(8,128)(2,1)} %fusion.15.q_t, bf16[256,1024]{1,0:T(8,128)(2,1)} %copy-done.29, bf16[1024,256]{1,0:T(8,128)(2,1)} %fusion.16.q, ...), custom_call_target="tpu_custom_call" | custom-call | flops 36238786560 | bytes 14680064 | tf_op jit(solution)/shard_map/attend_back/pallas_call | solution.py:441
  342.3 6.7 %collective-permute-start.35 = (bf16[4,2048,128]{2,1,0:T(8,128)(2,1)}, bf16[4,2048,128]{2,1,0:T(8,128)(2,1)}, u32[]{:S(2)}, u32[]{:S(2)}) collective-permute-start(bf16[4,2048,128]{2,1,0:T(8,128)(2,1)} %slice.624), channel_id=1, source_target_pairs={{0,1},{1,0},{2,3},{3,2},{4,5},{5,4},{6,7},{7,6},{8,9},{9,8},{10,11... | collective-permute-start | bytes 6291464 | tf_op jit(solution)/shard_map/ppermute | solution.py:155
  374.1 4.6 collective-permute-done.32
  384.2 8.6 %collective-permute-done.38 = bf16[2560,128]{1,0:T(8,128)(2,1)} collective-permute-done((bf16[2560,128]{1,0:T(8,128)(2,1)}, bf16[2560,128]{1,0:T(8,128)(2,1)}, u32[]{:S(2)}, u32[]{:S(2)}) %collective-permute-start.38) | collective-permute-done | bytes 655392 | tf_op jit(solution)/shard_map/ppermute | solution.py:44
  400.9 6.6 %collective-permute-start.40 = (bf16[128,640]{0,1:T(8,128)(2,1)S(1)}, bf16[128,640]{0,1:T(8,128)(2,1)S(1)}, u32[]{:S(2)}, u32[]{:S(2)}) collective-permute-start(bf16[128,640]{0,1:T(8,128)(2,1)S(1)} %get-tuple-element.266), channel_id=1, source_target_pairs={{0,4},{1,5},{2,6},{3,7},{4,0},{5,1},{6,2},{7,3},{8,12},{9,13},{10,... | collective-permute-start | bytes 491528 | tf_op jit(solution)/shard_map/ppermute | solution.py:155
  408.9 6.7 %collective-permute-done.39 = bf16[128,640]{0,1:T(8,128)(2,1)S(1)} collective-permute-done((bf16[128,640]{0,1:T(8,128)(2,1)S(1)}, bf16[128,640]{0,1:T(8,128)(2,1)S(1)}, u32[]{:S(2)}, u32[]{:S(2)}) %collective-permute-start.39) | collective-permute-done | bytes 163872 | tf_op jit(solution)/shard_map/ppermute | solution.py:155
  418.4 11.9 %collective-permute-done.41 = bf16[128,640]{0,1:T(8,128)(2,1)S(1)} collective-permute-done((bf16[128,640]{0,1:T(8,128)(2,1)S(1)}, bf16[128,640]{0,1:T(8,128)(2,1)S(1)}, u32[]{:S(2)}, u32[]{:S(2)}) %collective-permute-start.41) | collective-permute-done | bytes 163872 | tf_op jit(solution)/shard_map/ppermute | solution.py:155
  432.6 4.8 collective-permute-start.44
  439.9 6.6 %collective-permute-done.44 = bf16[1024,128]{1,0:T(8,128)(2,1)S(1)} collective-permute-done((bf16[1024,128]{1,0:T(8,128)(2,1)S(1)}, bf16[1024,128]{1,0:T(8,128)(2,1)S(1)}, u32[]{:S(2)}, u32[]{:S(2)}) %collective-permute-start.44) | collective-permute-done | bytes 262176 | tf_op jit(solution)/shard_map/ppermute | solution.py:155
  465.1 4.7 collective-permute-done.48
  (398 shorter events, 245.8 us)
Async XLA Ops:
  7.2 34.1 %all-gather.3.cloned.1.call-start = ((), (), s32[]{:S(2)}) async-start(), calls=%async_computation.1 | async-start | bytes 1769472 | tf_op jit(solution)/shard_map/all_gather | solution.py:651
  10.6 185.8 %all-gather.5.cloned.1.call-start = ((), (), s32[]{:S(2)}) async-start(), calls=%async_computation.2 | async-start | bytes 5308416 | tf_op jit(solution)/shard_map/all_gather | solution.py:683
  25.0 12.7 %collective-permute-start.2 = (bf16[256,1024]{1,0:T(8,128)(2,1)S(1)}, bf16[256,1024]{1,0:T(8,128)(2,1)}, u32[]{:S(2)}, u32[]{:S(2)}) collective-permute-start(bf16[256,1024]{1,0:T(8,128)(2,1)S(1)} %pad_maximum_fusion.21), channel_id=1, source_target_pairs={{0,16},{8,24},{16,0},{24,8},{1,17},{9,25},{17,1},{25,9},{2,18},{10... | collective-permute-start | bytes 1572872 | tf_op jit(solution)/shard_map/ppermute | solution.py:44
  99.9 406.0 %reduce-scatter.2.cloned.1.call-start = ((), (), s32[]{:S(2)}) async-start(), calls=%async_computation.3 | async-start | bytes 5308416 | tf_op jit(solution)/shard_map/reduce_scatter | solution.py:710
  176.4 13.6 %collective-permute-start.22 = (bf16[256,1024]{1,0:T(8,128)(2,1)S(1)}, bf16[256,1024]{1,0:T(8,128)(2,1)S(1)}, u32[]{:S(2)}, u32[]{:S(2)}) collective-permute-start(bf16[256,1024]{1,0:T(8,128)(2,1)S(1)} %pad_maximum_fusion.28), channel_id=1, source_target_pairs={{0,8},{8,0},{16,24},{24,16},{1,9},{9,1},{17,25},{25,17},{2,10},{10... | collective-permute-start | bytes 1572872 | tf_op jit(solution)/shard_map/ppermute | solution.py:44
  178.4 14.4 %collective-permute-start.21 = (bf16[256,1024]{1,0:T(8,128)(2,1)S(1)}, bf16[256,1024]{1,0:T(8,128)(2,1)S(1)}, u32[]{:S(2)}, u32[]{:S(2)}) collective-permute-start(bf16[256,1024]{1,0:T(8,128)(2,1)S(1)} %pad_maximum_fusion.27), channel_id=1, source_target_pairs={{0,16},{8,24},{16,0},{24,8},{1,17},{9,25},{17,1},{25,9},{2,18},{10... | collective-permute-start | bytes 1572872 | tf_op jit(solution)/shard_map/ppermute | solution.py:44
  210.1 14.2 %collective-permute-start.24 = (bf16[256,1024]{1,0:T(8,128)(2,1)S(1)}, bf16[256,1024]{1,0:T(8,128)(2,1)S(1)}, u32[]{:S(2)}, u32[]{:S(2)}) collective-permute-start(bf16[256,1024]{1,0:T(8,128)(2,1)S(1)} %pad_maximum_fusion.30), channel_id=1, source_target_pairs={{0,8},{8,0},{16,24},{24,16},{1,9},{9,1},{17,25},{25,17},{2,10},{10... | collective-permute-start | bytes 1572872 | tf_op jit(solution)/shard_map/ppermute | solution.py:44
  210.2 14.2 %collective-permute-start.23 = (bf16[256,1024]{1,0:T(8,128)(2,1)S(1)}, bf16[256,1024]{1,0:T(8,128)(2,1)S(1)}, u32[]{:S(2)}, u32[]{:S(2)}) collective-permute-start(bf16[256,1024]{1,0:T(8,128)(2,1)S(1)} %pad_maximum_fusion.29), channel_id=1, source_target_pairs={{0,16},{8,24},{16,0},{24,8},{1,17},{9,25},{17,1},{25,9},{2,18},{10... | collective-permute-start | bytes 1572872 | tf_op jit(solution)/shard_map/ppermute | solution.py:44
  342.3 25.3 %collective-permute-start.35 = (bf16[4,2048,128]{2,1,0:T(8,128)(2,1)}, bf16[4,2048,128]{2,1,0:T(8,128)(2,1)}, u32[]{:S(2)}, u32[]{:S(2)}) collective-permute-start(bf16[4,2048,128]{2,1,0:T(8,128)(2,1)} %slice.624), channel_id=1, source_target_pairs={{0,1},{1,0},{2,3},{3,2},{4,5},{5,4},{6,7},{7,6},{8,9},{9,8},{10,11... | collective-permute-start | bytes 6291464 | tf_op jit(solution)/shard_map/ppermute | solution.py:155
  358.8 25.4 %collective-permute-start.36 = (bf16[512,640]{0,1:T(8,128)(2,1)}, bf16[512,640]{0,1:T(8,128)(2,1)}, u32[]{:S(2)}, u32[]{:S(2)}) collective-permute-start(bf16[512,640]{0,1:T(8,128)(2,1)} %pad_maximum_fusion.15), channel_id=1, source_target_pairs={{0,1},{1,0},{2,3},{3,2},{4,5},{5,4},{6,7},{7,6},{8,9},{9,8},{10,11... | collective-permute-start | bytes 1966088 | tf_op jit(solution)/shard_map/ppermute | solution.py:155
  363.6 15.1 %collective-permute-start.32 = (bf16[256,1024]{1,0:T(8,128)(2,1)}, bf16[256,1024]{1,0:T(8,128)(2,1)}, u32[]{:S(2)}, u32[]{:S(2)}) collective-permute-start(bf16[256,1024]{1,0:T(8,128)(2,1)} %pad_maximum_fusion.33), channel_id=1, source_target_pairs={{0,8},{8,0},{16,24},{24,16},{1,9},{9,1},{17,25},{25,17},{2,10},{10... | collective-permute-start | bytes 1572872 | tf_op jit(solution)/shard_map/ppermute | solution.py:44
  365.6 15.1 %collective-permute-start.31 = (bf16[256,1024]{1,0:T(8,128)(2,1)}, bf16[256,1024]{1,0:T(8,128)(2,1)}, u32[]{:S(2)}, u32[]{:S(2)}) collective-permute-start(bf16[256,1024]{1,0:T(8,128)(2,1)} %pad_maximum_fusion.32), channel_id=1, source_target_pairs={{0,16},{8,24},{16,0},{24,8},{1,17},{9,25},{17,1},{25,9},{2,18},{10... | collective-permute-start | bytes 1572872 | tf_op jit(solution)/shard_map/ppermute | solution.py:44
  371.4 21.3 %collective-permute-start.38 = (bf16[2560,128]{1,0:T(8,128)(2,1)}, bf16[2560,128]{1,0:T(8,128)(2,1)}, u32[]{:S(2)}, u32[]{:S(2)}) collective-permute-start(bf16[2560,128]{1,0:T(8,128)(2,1)} %fusion.33), channel_id=1, source_target_pairs={{0,8},{8,0},{16,24},{24,16},{1,9},{9,1},{17,25},{25,17},{2,10},{10... | collective-permute-start | bytes 1966088 | tf_op jit(solution)/shard_map/ppermute | solution.py:44
  373.2 21.7 %collective-permute-start.37 = (bf16[2560,128]{1,0:T(8,128)(2,1)}, bf16[2560,128]{1,0:T(8,128)(2,1)}, u32[]{:S(2)}, u32[]{:S(2)}) collective-permute-start(bf16[2560,128]{1,0:T(8,128)(2,1)} %pad_maximum_fusion.16), channel_id=1, source_target_pairs={{0,16},{8,24},{16,0},{24,8},{1,17},{9,25},{17,1},{25,9},{2,18},{10... | collective-permute-start | bytes 1966088 | tf_op jit(solution)/shard_map/ppermute | solution.py:44
  382.1 18.7 %collective-permute-start.33 = (bf16[128,1024]{1,0:T(8,128)(2,1)S(1)}, bf16[128,1024]{1,0:T(8,128)(2,1)S(1)}, u32[]{:S(2)}, u32[]{:S(2)}) collective-permute-start(bf16[128,1024]{1,0:T(8,128)(2,1)S(1)} %get-tuple-element.228), channel_id=1, source_target_pairs={{0,8},{8,0},{16,24},{24,16},{1,9},{9,1},{17,25},{25,17},{2,10},{10... | collective-permute-start | bytes 786440 | tf_op jit(solution)/shard_map/ppermute | solution.py:44
  383.1 24.4 %collective-permute-start.34 = (bf16[128,1024]{1,0:T(8,128)(2,1)S(1)}, bf16[128,1024]{1,0:T(8,128)(2,1)S(1)}, u32[]{:S(2)}, u32[]{:S(2)}) collective-permute-start(bf16[128,1024]{1,0:T(8,128)(2,1)S(1)} %get-tuple-element.227), channel_id=1, source_target_pairs={{0,16},{8,24},{16,0},{24,8},{1,17},{9,25},{17,1},{25,9},{2,18},{10... | collective-permute-start | bytes 786440 | tf_op jit(solution)/shard_map/ppermute | solution.py:44
  396.0 34.3 %collective-permute-start.43 = (bf16[1280,128]{1,0:T(8,128)(2,1)S(1)}, bf16[1280,128]{1,0:T(8,128)(2,1)S(1)}, u32[]{:S(2)}, u32[]{:S(2)}) collective-permute-start(bf16[1280,128]{1,0:T(8,128)(2,1)S(1)} %add_convert_fusion.6), channel_id=1, source_target_pairs={{0,16},{8,24},{16,0},{24,8},{1,17},{9,25},{17,1},{25,9},{2,18},{10... | collective-permute-start | bytes 983048 | tf_op jit(solution)/shard_map/ppermute | solution.py:44
  398.4 31.9 %collective-permute-start.42 = (bf16[1280,128]{1,0:T(8,128)(2,1)S(1)}, bf16[1280,128]{1,0:T(8,128)(2,1)S(1)}, u32[]{:S(2)}, u32[]{:S(2)}) collective-permute-start(bf16[1280,128]{1,0:T(8,128)(2,1)S(1)} %fusion.34), channel_id=1, source_target_pairs={{0,8},{8,0},{16,24},{24,16},{1,9},{9,1},{17,25},{25,17},{2,10},{10... | collective-permute-start | bytes 983048 | tf_op jit(solution)/shard_map/ppermute | solution.py:44
  400.8 14.9 %collective-permute-start.39 = (bf16[128,640]{0,1:T(8,128)(2,1)S(1)}, bf16[128,640]{0,1:T(8,128)(2,1)S(1)}, u32[]{:S(2)}, u32[]{:S(2)}) collective-permute-start(bf16[128,640]{0,1:T(8,128)(2,1)S(1)} %get-tuple-element.267), channel_id=1, source_target_pairs={{0,2},{1,3},{2,0},{3,1},{4,6},{5,7},{6,4},{7,5},{8,10},{9,11},{10,... | collective-permute-start | bytes 491528 | tf_op jit(solution)/shard_map/ppermute | solution.py:155
  400.9 17.5 %collective-permute-start.40 = (bf16[128,640]{0,1:T(8,128)(2,1)S(1)}, bf16[128,640]{0,1:T(8,128)(2,1)S(1)}, u32[]{:S(2)}, u32[]{:S(2)}) collective-permute-start(bf16[128,640]{0,1:T(8,128)(2,1)S(1)} %get-tuple-element.266), channel_id=1, source_target_pairs={{0,4},{1,5},{2,6},{3,7},{4,0},{5,1},{6,2},{7,3},{8,12},{9,13},{10,... | collective-permute-start | bytes 491528 | tf_op jit(solution)/shard_map/ppermute | solution.py:155
  407.5 22.8 %collective-permute-start.41 = (bf16[128,640]{0,1:T(8,128)(2,1)S(1)}, bf16[128,640]{0,1:T(8,128)(2,1)S(1)}, u32[]{:S(2)}, u32[]{:S(2)}) collective-permute-start(bf16[128,640]{0,1:T(8,128)(2,1)S(1)} %get-tuple-element.265), channel_id=1, source_target_pairs={{0,6},{1,7},{2,4},{3,5},{4,2},{5,3},{6,0},{7,1},{8,14},{9,15},{10,... | collective-permute-start | bytes 491528 | tf_op jit(solution)/shard_map/ppermute | solution.py:155
  432.6 13.9 %collective-permute-start.44 = (bf16[1024,128]{1,0:T(8,128)(2,1)S(1)}, bf16[1024,128]{1,0:T(8,128)(2,1)S(1)}, u32[]{:S(2)}, u32[]{:S(2)}) collective-permute-start(bf16[1024,128]{1,0:T(8,128)(2,1)S(1)} %pad_maximum_fusion.43), channel_id=1, source_target_pairs={{0,2},{1,3},{2,0},{3,1},{4,6},{5,7},{6,4},{7,5},{8,10},{9,11},{10,... | collective-permute-start | bytes 786440 | tf_op jit(solution)/shard_map/ppermute | solution.py:155
  456.5 13.3 %collective-permute-start.48 = (bf16[256,1024]{1,0:T(8,128)(2,1)}, bf16[256,1024]{1,0:T(8,128)(2,1)}, u32[]{:S(2)}, u32[]{:S(2)}) collective-permute-start(bf16[256,1024]{1,0:T(8,128)(2,1)} %pad_maximum_fusion.35), channel_id=1, source_target_pairs={{0,8},{8,0},{16,24},{24,16},{1,9},{9,1},{17,25},{25,17},{2,10},{10... | collective-permute-start | bytes 1572872 | tf_op jit(solution)/shard_map/ppermute | solution.py:44
  458.8 12.8 %collective-permute-start.47 = (bf16[256,1024]{1,0:T(8,128)(2,1)}, bf16[256,1024]{1,0:T(8,128)(2,1)}, u32[]{:S(2)}, u32[]{:S(2)}) collective-permute-start(bf16[256,1024]{1,0:T(8,128)(2,1)} %pad_maximum_fusion.34), channel_id=1, source_target_pairs={{0,16},{8,24},{16,0},{24,8},{1,17},{9,25},{17,1},{25,9},{2,18},{10... | collective-permute-start | bytes 1572872 | tf_op jit(solution)/shard_map/ppermute | solution.py:44
  (97 other events, 847.5 us)
Sparse Core Ops, SparseCore 0:
  10.7 27.9 all-gather.2
  100.0 50.7 all-gather.4
  374.2 71.0 reduce-scatter.1

commit v4 on v3

--- a/solution.py
+++ b/solution.py
@@ -14,6 +14,8 @@
 CONT = 512
 KEY_TILE = 512
 ROW_TILE = 256
+TALL = HEAD_DIM + 16
+LOG2E = 1.4426950408889634
 
 epsilon = 1e-05
 masked_value = -1e30
@@ -223,11 +225,15 @@
 
         @pl.when(full)
         def _():
-            body(index, None)
-
-        @pl.when(partly)
+            body(index, None, KEY_TILE)
+
+        @pl.when(partly & (ahead < ROW_TILE))
         def _():
-            body(index, ahead)
+            body(index, ahead, ROW_TILE)
+
+        @pl.when(partly & (ahead >= ROW_TILE))
+        def _():
+            body(index, ahead, KEY_TILE)
 
         return carry
 
@@ -268,32 +274,36 @@
         acc[...] = jnp.zeros_like(acc)
         top[...] = jnp.full_like(top, masked_value)
         total[...] = jnp.zeros_like(total)
+        values_t[...] = jnp.ones_like(values_t)
 
     pairs = load_pairs(step, near_tiles, meta, near, far, spread, latents)
     keys[...] = pairs[:, :width]
-    values_t[...] = pairs[:, width:].T
-
-    def body(index, ahead):
+    turned = pairs[:, width:].T
+    for h in range(heads):
+        values_t[h * TALL : h * TALL + HEAD_DIM, :] = turned[h * HEAD_DIM : (h + 1) * HEAD_DIM]
+
+    def body(index, ahead, count):
         at = pl.ds(pl.multiple_of(index * ROW_TILE, ROW_TILE), ROW_TILE)
         before = top[:, at]
         sums = total[:, at]
-        scores = []
-        for h in range(heads):
-            pair, query = one_head(q_t, h, at)
-            scores.append(hide(dot(keys[:, pair], query, 1, 0), ahead))
         nows = []
         news = []
         results = []
-        for h in range(heads):
-            mine = slice(h * HEAD_DIM, (h + 1) * HEAD_DIM)
-            now = jnp.maximum(before[h : h + 1], jnp.max(scores[h], axis=0, keepdims=True))
-            probs = jnp.exp(scores[h] - now)
-            decay = jnp.exp(before[h : h + 1] - now)
-            nows.append(now)
-            news.append(decay * sums[h : h + 1] + jnp.sum(probs, axis=0, keepdims=True))
-            results.append(
-                decay * acc[mine, at] + dot(values_t[mine, :], probs.astype(BF16), 1, 0)
-            )
+        for first in range(0, heads, 2):
+            scores = []
+            for h in (first, first + 1):
+                pair, query = one_head(q_t, h, at)
+                scores.append(hide(dot(keys[:count, pair], query, 1, 0), ahead))
+            for h in (first, first + 1):
+                score = scores[h - first]
+                now = jnp.maximum(before[h : h + 1], jnp.max(score, axis=0, keepdims=True))
+                probs = jnp.exp2(score - now).astype(BF16)
+                decay = jnp.exp2(before[h : h + 1] - now)
+                got = dot(values_t[h * TALL : (h + 1) * TALL, :count], probs, 1, 0)
+                nows.append(now)
+                news.append(decay * sums[h : h + 1] + got[HEAD_DIM : HEAD_DIM + 1])
+                mine = slice(h * HEAD_DIM, (h + 1) * HEAD_DIM)
+                results.append(decay * acc[mine, at] + got[:HEAD_DIM])
         for h in range(heads):
             top[h : h + 1, at] = nows[h]
             total[h : h + 1, at] = news[h]
@@ -303,7 +313,7 @@
 
     @pl.when(step == pl.num_programs(0) - 1)
     def _():
-        lse[...] = top[...] + jnp.log(jnp.maximum(total[...], 1e-37))
+        lse[...] = top[...] + jnp.log2(jnp.maximum(total[...], 1e-37))
         for h in range(heads):
             mine = slice(h * HEAD_DIM, (h + 1) * HEAD_DIM)
             result = acc[mine, :] / total[h : h + 1, :]
@@ -342,7 +352,7 @@
     keys_t[...] = pairs[:, :width].T
     values[...] = pairs[:, width:]
 
-    def body(index, ahead):
+    def body(index, ahead, count):
         at = pl.ds(pl.multiple_of(index * ROW_TILE, ROW_TILE), ROW_TILE)
         to = pl.ds(pl.multiple_of(index * tall, tall), tall)
         all_probs = []
@@ -350,16 +360,16 @@
         for h in range(heads):
             pair, query = one_head(q_t, h, at)
             _, out_grad = one_head(grad_t, h, at)
-            scores = hide(dot(keys[:, pair], query, 1, 0), ahead)
-            probs = jnp.exp(scores - lse[h : h + 1, at])
-            dprobs = dot(values[:, pair], out_grad, 1, 0)
+            scores = hide(dot(keys[:count, pair], query, 1, 0), ahead)
+            probs = jnp.exp2(scores - lse[h : h + 1, at])
+            dprobs = dot(values[:count, pair], out_grad, 1, 0)
             score_grad = (probs * (dprobs - inner[h : h + 1, at])).astype(BF16)
             mine = slice(h * HEAD_DIM, (h + 1) * HEAD_DIM)
-            query_acc[mine, at] += dot(keys_t[mine, :], score_grad, 1, 0)
+            query_acc[mine, at] += dot(keys_t[mine, :count], score_grad, 1, 0)
             all_probs.append(probs.astype(BF16))
             all_grads.append(score_grad)
-        value_acc[...] += dot(jnp.concatenate(all_probs, axis=1), grads_apart[to, :], 1, 0)
-        key_acc[...] += dot(jnp.concatenate(all_grads, axis=1), queries_apart[to, :], 1, 0)
+        value_acc[:count] += dot(jnp.concatenate(all_probs, axis=1), grads_apart[to, :], 1, 0)
+        key_acc[:count] += dot(jnp.concatenate(all_grads, axis=1), queries_apart[to, :], 1, 0)
 
     visit_tiles(meta, step, prompt_tiles, portion, rows, body)
 
@@ -411,7 +421,7 @@
             scratch_shapes=[
                 pltpu.VMEM((KEY_TILE, spread.shape[0]), BF16),
                 pltpu.VMEM((KEY_TILE, width), BF16),
-                pltpu.VMEM((width, KEY_TILE), BF16),
+                pltpu.VMEM((heads * TALL, KEY_TILE), BF16),
                 pltpu.VMEM((width, rows), F32),
                 pltpu.VMEM((8, rows), F32),
                 pltpu.VMEM((8, rows), F32),
@@ -564,24 +574,23 @@
         return near, planes_of(whole[portion:]), near[:, :8], gather_near(beside)
     held = part[:portion]
     beside, held = together(beside, held)
-    got, *first = together(across(held, 2), *gather_first(beside))
-    held = jnp.concatenate([held, got], axis=0)
-    got, *second = together(across(held, 4), *gather_second(beside, *first))
-    beside = join(gather_order(beside, *first, *second))
-    held = jnp.concatenate([held, got, part[portion:]], axis=0)
+    first = gather_first(beside)
+    got = together(*[across(held, mask) for mask in (2, 4, 6)], *first)
+    *got, low_x, high_y = got
+    held = jnp.concatenate([held, *got, part[portion:]], axis=0)
+    beside = join(
+        gather_order(beside, low_x, high_y, *together(*gather_second(beside, low_x, high_y)))
+    )
     near = jnp.stack([jnp.concatenate(piece, axis=0) for piece in gather_pieces(held)], axis=0)
-    return near, across(near[:, : 4 * portion], 1), got, beside
-
-
-def scatter_latents(grad, portion, column_terms):
+    return near, across(near[:, : 4 * portion], 1), got[0], beside
+
+
+def scatter_latents(grad, portion):
     if not paired_columns(portion):
         whole = jnp.concatenate([grad[j] for j in range(grad.shape[0])], axis=1)
         prompt = scatter_prompt(whole[:PROMPT], portion)
         whole = jnp.concatenate([prompt, whole[PROMPT:]], axis=0)
-        sums = lax.psum_scatter(
-            column_terms(), "col", scatter_dimension=0, tiled=True
-        ).astype(F32)
-        return lax.psum_scatter(whole, "row", scatter_dimension=1, tiled=True), sums
+        return lax.psum_scatter(whole, "row", scatter_dimension=1, tiled=True)
     here = 4 * portion
     got = across(grad[:, here + portion :], 1)
     pieces = [
@@ -590,18 +599,13 @@
         )
         for j in range(4)
     ]
-    terms, terms_got = column_first(column_terms())
-    terms_got, *first = together(terms_got, *scatter_first(pieces))
-    terms, terms_on = column_second(terms, terms_got)
-    *terms_on, low_last, high_last = together(*terms_on, *scatter_second(pieces, *first))
-    mine = scatter_last(pieces, *first, low_last, high_last)
+    mine = scatter_pieces(pieces)
     low = mine[:here].astype(BF16)
-    blocks = [low[j * portion : (j + 1) * portion] for j in range(4)]
-    got = across(jnp.concatenate([blocks[1], blocks[3]], axis=0), 2)
-    other = across(add_low(blocks[2], got[portion:]), 4)
-    prompt = mine[:portion] + got[:portion].astype(F32) + other.astype(F32)
-    sums = column_last(terms, terms_on)
-    return jnp.concatenate([prompt.astype(BF16), mine[here:].astype(BF16)], axis=0), sums
+    got = together(
+        *[across(low[j * portion : (j + 1) * portion], 2 * j) for j in (1, 2, 3)]
+    )
+    prompt = (mine[:portion] + got[0].astype(F32)) + (got[1].astype(F32) + got[2].astype(F32))
+    return jnp.concatenate([prompt.astype(BF16), mine[here:].astype(BF16)], axis=0)
 
 
 def near_features(table, portion):
@@ -675,7 +679,7 @@
     latent_part = dot(normed_block, latent_full, 1, 0).astype(BF16)
     near, far, prompt_there, cot_block = gather_latents(latent_part, cotangent)
     scale = HEAD_DIM**-0.5
-    queries_t = (dot(query_full, normed_block, 0, 1).astype(BF16) * scale).astype(BF16)
+    queries_t = (dot(query_full, normed_block, 0, 1) * (scale * LOG2E)).astype(BF16)
     queries = (dot(normed_block, query_full, 1, 0).astype(BF16) * scale).astype(BF16)
     meta = key_layout(block_order, portion)
     late, _ = together(late, prompt_there)
@@ -724,24 +728,24 @@
         meta, queries_t, attended_grad_t, queries, attended_grad, lse, inner, near, far, spread,
         portion,
     )
-    def column_terms():
-        output_term = dot(branch_block, attended_t, 0, 1).astype(BF16)
-        query_term = dot(normed_block, query_grad_t, 0, 1).astype(BF16)
-        pair_table = near_features(pair_big, portion)
-        pair_term = jnp.where(mask[:LATENT], pair_table[:LATENT], pair_table[LATENT:])
-        pair_terms = pair_term.astype(BF16).reshape(columns, pair_rows, strips, 128)
-        pair_terms = jnp.concatenate([pair_terms[:, :, i] for i in range(strips)], axis=1)
-        pair_terms = jnp.pad(pair_terms, ((0, 0), (0, share - strips * pair_rows), (0, 0)))
-        return jnp.concatenate(
-            [query_term, output_term, pair_terms.reshape(columns * share, 128)], axis=1
-        )
-
-    latent_grad, early_sums = scatter_latents(latent_terms, portion, column_terms)
+    latent_grad = scatter_latents(latent_terms, portion)
+    output_term = dot(branch_block, attended_t, 0, 1).astype(BF16)
+    query_term = dot(normed_block, query_grad_t, 0, 1).astype(BF16)
+    pair_table = near_features(pair_big, portion)
+    pair_term = jnp.where(mask[:LATENT], pair_table[:LATENT], pair_table[LATENT:])
+    pair_terms = pair_term.astype(BF16).reshape(columns, pair_rows, strips, 128)
+    pair_terms = jnp.concatenate([pair_terms[:, :, i] for i in range(strips)], axis=1)
+    pair_terms = jnp.pad(pair_terms, ((0, 0), (0, share - strips * pair_rows), (0, 0)))
+    early_terms = jnp.concatenate(
+        [query_term, output_term, pair_terms.reshape(columns * share, 128)], axis=1
+    )
+    early_sums = lax.psum_scatter(early_terms, "col", scatter_dimension=0, tiled=True).astype(F32)
     pair_sums = early_sums[:, 2 * width :]
     latent_term = dot(normed_block, latent_grad, 0, 0).astype(BF16)
-    norm_part = (
-        dot(query_grad_t, query_full, 0, 1) + dot(latent_grad, latent_full, 1, 1)
-    ).astype(BF16)
+    norm_part = dot(query_grad_t, query_full, 0, 1) + dot(latent_grad, latent_full, 1, 1)
+    first_gain_term = jnp.sum(norm_part * normed_block.astype(F32), axis=0) / first_gain
+    norm_part = norm_part.astype(BF16)
+    gains = jnp.stack([first_gain_term, second_gain_term])
     if paired_columns(portion):
         mine, got = column_first(latent_term)
         pieces = true_pieces(norm_part)
@@ -755,9 +759,9 @@
             latent_term, "col", scatter_dimension=0, tiled=True
         ).astype(F32)
         normed_grad = scatter_true(norm_part)
-    norm1_grad, first_gain_term = norm_backward(rows, first_scale, first_gain, normed_grad)
+    gains = all_sum(gains)
+    norm1_grad = norm_backward(rows, first_scale, first_gain, normed_grad)[0]
     input_gradient = hidden_grad + norm1_grad
-    gains = all_sum(jnp.stack([first_gain_term, second_gain_term]))
     pair_sum = jnp.concatenate(
         [pair_sums[i * pair_rows : (i + 1) * pair_rows] for i in range(strips)], axis=1
     )

time: 525 us -> 507 us (0.966)
  waiting for transfers between devices: 169 us -> 142 us
  starting transfers between devices: 78.1 us -> 89.9 us
  other arithmetic: 63.7 us -> 57.7 us
  local copies, waits for them, and re-layouts: 40.9 us -> 46.9 us
    ppermute x18 -> x16, waiting for transfers between devices: 48.4 us -> 24.8 us  [across(): lax.ppermute(block, 'col', [(i, i ^ mask) for i in range(lax.axis_size('c...]
    ppermute x43, starting transfers between devices: 43.2 us -> 49.1 us  [exchange(): lax.ppermute(block, 'row', [(i, i ^ mask) for i in range(lax.axis_size('r...]
    ppermute x18 -> x16, starting transfers between devices: 34.8 us -> 40.5 us  [across(): lax.ppermute(block, 'col', [(i, i ^ mask) for i in range(lax.axis_size('c...]
    dynamic_update_slice x8, other arithmetic: 6.42 us -> 0.78 us  [gather_true(): lax.dynamic_update_slice_in_dim(whole, jnp.concatenate(piece, axis=0), (h...]
    unnamed x132 -> x122, local copies, waits for them, and re-layouts: 17.3 us -> 21.1 us
    convert_element_type x8 -> x7, other arithmetic: 10.9 us -> 12.7 us  [add_low(): return (left.astype(F32) + right.astype(F32)).astype(BF16)]
  transfers between devices with their start and end apart: 64 -> 63, of which waited for: 42 -> 41; matrix products, arithmetic and copies ran while one was open for 19% -> 19% of each run, Pallas kernels for 7% -> 8%
where the time goes in v4:
time: 507 us; the launch traced here: 500 us
  waiting for transfers between devices  142 us (28%)
  Pallas kernels  104 us (21%)
  starting transfers between devices  89.9 us (18%)
  other arithmetic  57.7 us (11%)
  local copies, waits for them, and re-layouts  46.9 us (9%)
  matrix products  41.5 us (8%)
  between operations  17.8 us (4%)
    ppermute x43, waiting for transfers between devices, exchange(): lax.ppermute(block, 'row', [(i, i ^ mask) for i in range(lax.axis_size('r...  117 us
    pallas_call x1, Pallas kernels, attend_back(): pl.pallas_call(functools.partial(attend_back_kernel, heads=heads, prompt_...  66.1 us
    ppermute x43, starting transfers between devices, exchange(): lax.ppermute(block, 'row', [(i, i ^ mask) for i in range(lax.axis_size('r...  49.1 us
    dot_general x17, matrix products, dot(): lax.dot_general(left, right, (((left_dim,), (right_dim,)), ((), ())), pre...  41.5 us
    ppermute x16, starting transfers between devices, across(): lax.ppermute(block, 'col', [(i, i ^ mask) for i in range(lax.axis_size('c...  40.5 us
    pallas_call x1, Pallas kernels, attend(): pl.pallas_call(functools.partial(attend_kernel, heads=heads, prompt_tiles...  38 us
    ppermute x16, waiting for transfers between devices, across(): lax.ppermute(block, 'col', [(i, i ^ mask) for i in range(lax.axis_size('c...  24.8 us
    unnamed x122, local copies, waits for them, and re-layouts  21.1 us
  transfers between devices with their start and end apart: 63, of which 41 were waited for; matrix products, arithmetic and copies ran while one was open for 19% of the time, Pallas kernels for 8%

profile of v4, /device:TPU:0, one launch (start us, length us, event | category | flops | bytes accessed | tf_op | source)
XLA Modules:
  0.0 499.9 jit_solution(2947953425570029740)
XLA Ops:
  31.0 7.8 %collective-permute-done.3 = bf16[256,1024]{1,0:T(8,128)(2,1)} collective-permute-done((bf16[256,1024]{1,0:T(8,128)(2,1)}, bf16[256,1024]{1,0:T(8,128)(2,1)}, u32[]{:S(2)}, u32[]{:S(2)}) %collective-permute-start.3) | collective-permute-done | bytes 524320 | tf_op jit(solution)/shard_map/ppermute | solution.py:46
  53.6 6.4 %collective-permute-done.5 = bf16[512,128]{1,0:T(8,128)(2,1)} collective-permute-done((bf16[512,128]{1,0:T(8,128)(2,1)}, bf16[512,128]{1,0:T(8,128)(2,1)}, u32[]{:S(2)}, u32[]{:S(2)}) %collective-permute-start.5) | collective-permute-done | bytes 131104 | tf_op jit(solution)/shard_map/ppermute | solution.py:157
  63.8 7.0 %collective-permute-done.11 = bf16[1280,128]{1,0:T(8,128)(2,1)S(1)} collective-permute-done((bf16[1280,128]{1,0:T(8,128)(2,1)S(1)}, bf16[1280,128]{1,0:T(8,128)(2,1)S(1)}, u32[]{:S(2)}, u32[]{:S(2)}) %collective-permute-start.11) | collective-permute-done | bytes 327712 | tf_op jit(solution)/shard_map/ppermute | solution.py:46
  76.5 6.5 %collective-permute-done.13 = bf16[2560,128]{1,0:T(8,128)(2,1)S(1)} collective-permute-done((bf16[2560,128]{1,0:T(8,128)(2,1)S(1)}, bf16[2560,128]{1,0:T(8,128)(2,1)S(1)}, u32[]{:S(2)}, u32[]{:S(2)}) %collective-permute-start.13) | collective-permute-done | bytes 655392 | tf_op jit(solution)/shard_map/ppermute | solution.py:46
  97.7 5.7 %collective-permute-done.10 = bf16[256,1024]{1,0:T(8,128)(2,1)S(1)} collective-permute-done((bf16[256,1024]{1,0:T(8,128)(2,1)S(1)}, bf16[256,1024]{1,0:T(8,128)(2,1)S(1)}, u32[]{:S(2)}, u32[]{:S(2)}) %collective-permute-start.10) | collective-permute-done | bytes 524320 | tf_op jit(solution)/shard_map/ppermute | solution.py:46
  109.6 38.0 %attend.1 = (f32[256,1024]{1,0:T(8,128)}, bf16[256,1024]{1,0:T(8,128)(2,1)}, f32[8,1024]{1,0:T(8,128)}) custom-call(s32[10]{0:T(128)} %pad_add_fusion.meta, bf16[256,1024]{1,0:T(8,128)(2,1)} %fusion.14.q_t, bf16[4,2560,128]{2,1,0:T(8,128)(2,1)} %copy-done.1, bf16[4,2048,128]{2,1,0:T(8,128)(2,1)} %collective-permute-done.15.far, ...), custom_call_target="tpu_custom_call" | custom-call | flops 14495514624 | bytes 8388608 | tf_op jit(solution)/shard_map/attend/pallas_call | solution.py:407
  153.3 8.3 %collective-permute-done.17 = bf16[256,1024]{1,0:T(8,128)(2,1)} collective-permute-done((bf16[256,1024]{1,0:T(8,128)(2,1)}, bf16[256,1024]{1,0:T(8,128)(2,1)}, u32[]{:S(2)}, u32[]{:S(2)}) %collective-permute-start.17) | collective-permute-done | bytes 524320 | tf_op jit(solution)/shard_map/ppermute | solution.py:46
  167.7 3.6 collective-permute-done.18
  177.6 7.4 %collective-permute-done.20 = bf16[128,1024]{1,0:T(8,128)(2,1)S(1)} collective-permute-done((bf16[128,1024]{1,0:T(8,128)(2,1)S(1)}, bf16[128,1024]{1,0:T(8,128)(2,1)S(1)}, u32[]{:S(2)}, u32[]{:S(2)}) %collective-permute-start.20) | collective-permute-done | bytes 262176 | tf_op jit(solution)/shard_map/ppermute | solution.py:46
  189.2 5.4 %collective-permute-done.23 = bf16[256,1024]{1,0:T(8,128)(2,1)S(1)} collective-permute-done((bf16[256,1024]{1,0:T(8,128)(2,1)S(1)}, bf16[256,1024]{1,0:T(8,128)(2,1)S(1)}, u32[]{:S(2)}, u32[]{:S(2)}) %collective-permute-start.23) | collective-permute-done | bytes 524320 | tf_op jit(solution)/shard_map/ppermute | solution.py:46
  200.0 6.1 %fusion.2 = f32[1024,1536]{1,0:T(8,128)S(1)} fusion(bf16[1024,1024]{1,0:T(8,128)(2,1)} %slice_dynamic-update-slice_fusion, bf16[1024,2304]{0,1:T(8,128)(2,1)} %all-gather.5.cloned.1.call-done), kind=kOutput, calls=%fused_computation.10 | convolution fusion | flops 3221225472 | bytes 11534336 | tf_op jit(solution)/shard_map/dot_general | solution.py:27
  206.2 3.8 multiply_convert_fusion.1
  210.0 3.6 fusion.4
  215.7 5.8 %convolution_convert_fusion = bf16[1024,1536]{1,0:T(8,128)(2,1)S(1)} fusion(bf16[1024,1024]{1,0:T(8,128)(2,1)} %slice_dynamic-update-slice_fusion, bf16[1024,768]{1,0:T(8,128)(2,1)S(1)} %get-tuple-element.205, bf16[1024,768]{1,0:T(8,128)(2,1)S(1)} %get-tuple-element.204), kind=kOutput, calls=%fused_computation.2 | convolution fusion | flops 3229089792 | bytes 8388608 | tf_op jit(solution)/shard_map/dot_general | solution.py:27
  241.2 5.7 %collective-permute-done.28 = bf16[128,1024]{1,0:T(8,128)(2,1)S(1)} collective-permute-done((bf16[128,1024]{1,0:T(8,128)(2,1)S(1)}, bf16[128,1024]{1,0:T(8,128)(2,1)S(1)}, u32[]{:S(2)}, u32[]{:S(2)}) %collective-permute-start.28) | collective-permute-done | bytes 262176 | tf_op jit(solution)/shard_map/ppermute | solution.py:46
  249.5 7.9 %collective-permute-done.31 = bf16[256,1024]{1,0:T(8,128)(2,1)S(1)} collective-permute-done((bf16[256,1024]{1,0:T(8,128)(2,1)S(1)}, bf16[256,1024]{1,0:T(8,128)(2,1)S(1)}, u32[]{:S(2)}, u32[]{:S(2)}) %collective-permute-start.31) | collective-permute-done | bytes 524320 | tf_op jit(solution)/shard_map/ppermute | solution.py:46
  264.3 66.1 %attend_back.1 = (bf16[256,1024]{1,0:T(8,128)(2,1)}, bf16[4,4608,128]{2,1,0:T(8,128)(2,1)}, f32[512,512]{1,0:T(8,128)}) custom-call(s32[10]{0:T(128)} %pad_add_fusion.meta, bf16[256,1024]{1,0:T(8,128)(2,1)} %fusion.14.q_t, bf16[256,1024]{1,0:T(8,128)(2,1)} %copy-done.22, bf16[1024,256]{1,0:T(8,128)(2,1)} %fusion.15.q, ...), custom_call_target="tpu_custom_call" | custom-call | flops 36238786560 | bytes 14680064 | tf_op jit(solution)/shard_map/attend_back/pallas_call | solution.py:451
  354.2 10.3 %collective-permute-done.33 = bf16[256,1024]{1,0:T(8,128)(2,1)} collective-permute-done((bf16[256,1024]{1,0:T(8,128)(2,1)}, bf16[256,1024]{1,0:T(8,128)(2,1)}, u32[]{:S(2)}, u32[]{:S(2)}) %collective-permute-start.33) | collective-permute-done | bytes 524320 | tf_op jit(solution)/shard_map/ppermute | solution.py:46
  366.5 3.5 add_convert_fusion.3
  378.1 14.8 %collective-permute-done.34 = bf16[128,1024]{1,0:T(8,128)(2,1)} collective-permute-done((bf16[128,1024]{1,0:T(8,128)(2,1)}, bf16[128,1024]{1,0:T(8,128)(2,1)}, u32[]{:S(2)}, u32[]{:S(2)}) %collective-permute-start.34) | collective-permute-done | bytes 262176 | tf_op jit(solution)/shard_map/ppermute | solution.py:46
  414.0 18.7 %collective-permute-start.41 = (bf16[512,128]{1,0:T(8,128)(2,1)}, bf16[512,128]{1,0:T(8,128)(2,1)}, u32[]{:S(2)}, u32[]{:S(2)}) collective-permute-start(bf16[512,128]{1,0:T(8,128)(2,1)} %get-tuple-element.284), channel_id=1, source_target_pairs={{0,2},{1,3},{2,0},{3,1},{4,6},{5,7},{6,4},{7,5},{8,10},{9,11},{10,... | collective-permute-start | bytes 393224 | tf_op jit(solution)/shard_map/ppermute | solution.py:157
  441.3 9.0 %collective-permute-done.42 = bf16[512,128]{1,0:T(8,128)(2,1)} collective-permute-done((bf16[512,128]{1,0:T(8,128)(2,1)}, bf16[512,128]{1,0:T(8,128)(2,1)}, u32[]{:S(2)}, u32[]{:S(2)}) %collective-permute-start.42) | collective-permute-done | bytes 131104 | tf_op jit(solution)/shard_map/ppermute | solution.py:157
  463.5 5.7 %collective-permute-start.56 = (f32[2,1024]{1,0:T(2,128)S(1)}, f32[2,1024]{1,0:T(2,128)S(1)}, u32[]{:S(2)}, u32[]{:S(2)}) collective-permute-start(f32[2,1024]{1,0:T(2,128)S(1)} %add.374), channel_id=1, source_target_pairs={{0,2},{1,3},{2,0},{3,1},{4,6},{5,7},{6,4},{7,5},{8,10},{9,11},{10,... | collective-permute-start | bytes 24584 | tf_op jit(solution)/shard_map/ppermute | solution.py:157
  476.0 4.3 collective-permute-start.47
  (380 shorter events, 221.0 us)
Async XLA Ops:
  7.2 34.2 %all-gather.3.cloned.1.call-start = ((), (), s32[]{:S(2)}) async-start(), calls=%async_computation.2 | async-start | bytes 1769472 | tf_op jit(solution)/shard_map/all_gather | solution.py:655
  10.6 189.5 %all-gather.5.cloned.1.call-start = ((), (), s32[]{:S(2)}) async-start(), calls=%async_computation.3 | async-start | bytes 5308416 | tf_op jit(solution)/shard_map/all_gather | solution.py:687
  25.9 12.8 %collective-permute-start.3 = (bf16[256,1024]{1,0:T(8,128)(2,1)}, bf16[256,1024]{1,0:T(8,128)(2,1)}, u32[]{:S(2)}, u32[]{:S(2)}) collective-permute-start(bf16[256,1024]{1,0:T(8,128)(2,1)} %pad_maximum_fusion.16), channel_id=1, source_target_pairs={{0,8},{8,0},{16,24},{24,16},{1,9},{9,1},{17,25},{25,17},{2,10},{10... | collective-permute-start | bytes 1572872 | tf_op jit(solution)/shard_map/ppermute | solution.py:46
  27.1 12.8 %collective-permute-start.2 = (bf16[256,1024]{1,0:T(8,128)(2,1)}, bf16[256,1024]{1,0:T(8,128)(2,1)}, u32[]{:S(2)}, u32[]{:S(2)}) collective-permute-start(bf16[256,1024]{1,0:T(8,128)(2,1)} %pad_maximum_fusion.19), channel_id=1, source_target_pairs={{0,16},{8,24},{16,0},{24,8},{1,17},{9,25},{17,1},{25,9},{2,18},{10... | collective-permute-start | bytes 1572872 | tf_op jit(solution)/shard_map/ppermute | solution.py:46
  45.0 15.0 %collective-permute-start.7 = (bf16[128,1024]{1,0:T(8,128)(2,1)}, bf16[128,1024]{1,0:T(8,128)(2,1)}, u32[]{:S(2)}, u32[]{:S(2)}) collective-permute-start(bf16[128,1024]{1,0:T(8,128)(2,1)} %get-tuple-element.274), channel_id=1, source_target_pairs={{0,8},{8,0},{16,24},{24,16},{1,9},{9,1},{17,25},{25,17},{2,10},{10... | collective-permute-start | bytes 786440 | tf_op jit(solution)/shard_map/ppermute | solution.py:46
  46.4 13.6 %collective-permute-start.8 = (bf16[128,1024]{1,0:T(8,128)(2,1)}, bf16[128,1024]{1,0:T(8,128)(2,1)S(1)}, u32[]{:S(2)}, u32[]{:S(2)}) collective-permute-start(bf16[128,1024]{1,0:T(8,128)(2,1)} %get-tuple-element.273), channel_id=1, source_target_pairs={{0,16},{8,24},{16,0},{24,8},{1,17},{9,25},{17,1},{25,9},{2,18},{10... | collective-permute-start | bytes 786440 | tf_op jit(solution)/shard_map/ppermute | solution.py:46
  86.3 23.4 %collective-permute-start.15 = (bf16[4,2048,128]{2,1,0:T(8,128)(2,1)}, bf16[4,2048,128]{2,1,0:T(8,128)(2,1)}, u32[]{:S(2)}, u32[]{:S(2)}) collective-permute-start(bf16[4,2048,128]{2,1,0:T(8,128)(2,1)} %slice.675), channel_id=1, source_target_pairs={{0,1},{1,0},{2,3},{3,2},{4,5},{5,4},{6,7},{7,6},{8,9},{9,8},{10,11... | collective-permute-start | bytes 6291464 | tf_op jit(solution)/shard_map/ppermute | solution.py:157
  88.2 308.5 %reduce-scatter.7.cloned.1.call-start = ((), (), s32[]{:S(2)}) async-start(), calls=%async_computation.5 | async-start | bytes 1474560
  89.4 14.0 %collective-permute-start.10 = (bf16[256,1024]{1,0:T(8,128)(2,1)S(1)}, bf16[256,1024]{1,0:T(8,128)(2,1)S(1)}, u32[]{:S(2)}, u32[]{:S(2)}) collective-permute-start(bf16[256,1024]{1,0:T(8,128)(2,1)S(1)} %pad_maximum_fusion.21), channel_id=1, source_target_pairs={{0,8},{8,0},{16,24},{24,16},{1,9},{9,1},{17,25},{25,17},{2,10},{10... | collective-permute-start | bytes 1572872 | tf_op jit(solution)/shard_map/ppermute | solution.py:46
  92.2 13.7 %collective-permute-start.9 = (bf16[256,1024]{1,0:T(8,128)(2,1)S(1)}, bf16[256,1024]{1,0:T(8,128)(2,1)S(1)}, u32[]{:S(2)}, u32[]{:S(2)}) collective-permute-start(bf16[256,1024]{1,0:T(8,128)(2,1)S(1)} %pad_maximum_fusion.20), channel_id=1, source_target_pairs={{0,16},{8,24},{16,0},{24,8},{1,17},{9,25},{17,1},{25,9},{2,18},{10... | collective-permute-start | bytes 1572872 | tf_op jit(solution)/shard_map/ppermute | solution.py:46
  213.8 12.1 %collective-permute-start.25 = (bf16[256,1024]{1,0:T(8,128)(2,1)S(1)}, bf16[256,1024]{1,0:T(8,128)(2,1)S(1)}, u32[]{:S(2)}, u32[]{:S(2)}) collective-permute-start(bf16[256,1024]{1,0:T(8,128)(2,1)S(1)} %pad_maximum_fusion.28), channel_id=1, source_target_pairs={{0,8},{8,0},{16,24},{24,16},{1,9},{9,1},{17,25},{25,17},{2,10},{10... | collective-permute-start | bytes 1572872 | tf_op jit(solution)/shard_map/ppermute | solution.py:46
  342.1 147.1 %reduce-scatter.5.cloned.1.call-start = ((), (), s32[]{:S(2)}) async-start(), calls=%async_computation.4 | async-start | bytes 5308416 | tf_op jit(solution)/shard_map/reduce_scatter | solution.py:714
  345.5 20.9 %collective-permute-start.36 = (bf16[4,2048,128]{2,1,0:T(8,128)(2,1)}, bf16[4,2048,128]{2,1,0:T(8,128)(2,1)}, u32[]{:S(2)}, u32[]{:S(2)}) collective-permute-start(bf16[4,2048,128]{2,1,0:T(8,128)(2,1)} %slice.606), channel_id=1, source_target_pairs={{0,1},{1,0},{2,3},{3,2},{4,5},{5,4},{6,7},{7,6},{8,9},{9,8},{10,11... | collective-permute-start | bytes 6291464 | tf_op jit(solution)/shard_map/ppermute | solution.py:157
  349.8 14.7 %collective-permute-start.33 = (bf16[256,1024]{1,0:T(8,128)(2,1)}, bf16[256,1024]{1,0:T(8,128)(2,1)}, u32[]{:S(2)}, u32[]{:S(2)}) collective-permute-start(bf16[256,1024]{1,0:T(8,128)(2,1)} %pad_maximum_fusion.31), channel_id=1, source_target_pairs={{0,8},{8,0},{16,24},{24,16},{1,9},{9,1},{17,25},{25,17},{2,10},{10... | collective-permute-start | bytes 1572872 | tf_op jit(solution)/shard_map/ppermute | solution.py:46
  352.1 14.4 %collective-permute-start.32 = (bf16[256,1024]{1,0:T(8,128)(2,1)}, bf16[256,1024]{1,0:T(8,128)(2,1)}, u32[]{:S(2)}, u32[]{:S(2)}) collective-permute-start(bf16[256,1024]{1,0:T(8,128)(2,1)} %pad_maximum_fusion.30), channel_id=1, source_target_pairs={{0,16},{8,24},{16,0},{24,8},{1,17},{9,25},{17,1},{25,9},{2,18},{10... | collective-permute-start | bytes 1572872 | tf_op jit(solution)/shard_map/ppermute | solution.py:46
  371.0 26.8 %collective-permute-start.38 = (bf16[2560,128]{1,0:T(8,128)(2,1)}, bf16[2560,128]{1,0:T(8,128)(2,1)}, u32[]{:S(2)}, u32[]{:S(2)}) collective-permute-start(bf16[2560,128]{1,0:T(8,128)(2,1)} %fusion.31), channel_id=1, source_target_pairs={{0,8},{8,0},{16,24},{24,16},{1,9},{9,1},{17,25},{25,17},{2,10},{10... | collective-permute-start | bytes 1966088 | tf_op jit(solution)/shard_map/ppermute | solution.py:46
  372.5 25.4 %collective-permute-start.37 = (bf16[2560,128]{1,0:T(8,128)(2,1)}, bf16[2560,128]{1,0:T(8,128)(2,1)}, u32[]{:S(2)}, u32[]{:S(2)}) collective-permute-start(bf16[2560,128]{1,0:T(8,128)(2,1)} %pad_maximum_fusion.14), channel_id=1, source_target_pairs={{0,16},{8,24},{16,0},{24,8},{1,17},{9,25},{17,1},{25,9},{2,18},{10... | collective-permute-start | bytes 1966088 | tf_op jit(solution)/shard_map/ppermute | solution.py:46
  374.9 18.0 %collective-permute-start.34 = (bf16[128,1024]{1,0:T(8,128)(2,1)}, bf16[128,1024]{1,0:T(8,128)(2,1)}, u32[]{:S(2)}, u32[]{:S(2)}) collective-permute-start(bf16[128,1024]{1,0:T(8,128)(2,1)} %get-tuple-element.228), channel_id=1, source_target_pairs={{0,8},{8,0},{16,24},{24,16},{1,9},{9,1},{17,25},{25,17},{2,10},{10... | collective-permute-start | bytes 786440 | tf_op jit(solution)/shard_map/ppermute | solution.py:46
  376.4 17.7 %collective-permute-start.35 = (bf16[128,1024]{1,0:T(8,128)(2,1)}, bf16[128,1024]{1,0:T(8,128)(2,1)}, u32[]{:S(2)}, u32[]{:S(2)}) collective-permute-start(bf16[128,1024]{1,0:T(8,128)(2,1)} %get-tuple-element.227), channel_id=1, source_target_pairs={{0,16},{8,24},{16,0},{24,8},{1,17},{9,25},{17,1},{25,9},{2,18},{10... | collective-permute-start | bytes 786440 | tf_op jit(solution)/shard_map/ppermute | solution.py:46
  414.0 27.3 %collective-permute-start.41 = (bf16[512,128]{1,0:T(8,128)(2,1)}, bf16[512,128]{1,0:T(8,128)(2,1)}, u32[]{:S(2)}, u32[]{:S(2)}) collective-permute-start(bf16[512,128]{1,0:T(8,128)(2,1)} %get-tuple-element.284), channel_id=1, source_target_pairs={{0,2},{1,3},{2,0},{3,1},{4,6},{5,7},{6,4},{7,5},{8,10},{9,11},{10,... | collective-permute-start | bytes 393224 | tf_op jit(solution)/shard_map/ppermute | solution.py:157
  432.7 17.6 %collective-permute-start.42 = (bf16[512,128]{1,0:T(8,128)(2,1)}, bf16[512,128]{1,0:T(8,128)(2,1)}, u32[]{:S(2)}, u32[]{:S(2)}) collective-permute-start(bf16[512,128]{1,0:T(8,128)(2,1)} %get-tuple-element.283), channel_id=1, source_target_pairs={{0,4},{1,5},{2,6},{3,7},{4,0},{5,1},{6,2},{7,3},{8,12},{9,13},{10,... | collective-permute-start | bytes 393224 | tf_op jit(solution)/shard_map/ppermute | solution.py:157
  432.7 17.6 %collective-permute-start.43 = (bf16[512,128]{1,0:T(8,128)(2,1)}, bf16[512,128]{1,0:T(8,128)(2,1)}, u32[]{:S(2)}, u32[]{:S(2)}) collective-permute-start(bf16[512,128]{1,0:T(8,128)(2,1)} %get-tuple-element.281), channel_id=1, source_target_pairs={{0,6},{1,7},{2,4},{3,5},{4,2},{5,3},{6,0},{7,1},{8,14},{9,15},{10,... | collective-permute-start | bytes 393224 | tf_op jit(solution)/shard_map/ppermute | solution.py:157
  458.4 16.3 %collective-permute-start.46 = (bf16[256,1024]{1,0:T(8,128)(2,1)S(1)}, bf16[256,1024]{1,0:T(8,128)(2,1)S(1)}, u32[]{:S(2)}, u32[]{:S(2)}) collective-permute-start(bf16[256,1024]{1,0:T(8,128)(2,1)S(1)} %pad_maximum_fusion.33), channel_id=1, source_target_pairs={{0,8},{8,0},{16,24},{24,16},{1,9},{9,1},{17,25},{25,17},{2,10},{10... | collective-permute-start | bytes 1572872 | tf_op jit(solution)/shard_map/ppermute | solution.py:46
  460.6 14.1 %collective-permute-start.45 = (bf16[256,1024]{1,0:T(8,128)(2,1)S(1)}, bf16[256,1024]{1,0:T(8,128)(2,1)S(1)}, u32[]{:S(2)}, u32[]{:S(2)}) collective-permute-start(bf16[256,1024]{1,0:T(8,128)(2,1)S(1)} %pad_maximum_fusion.32), channel_id=1, source_target_pairs={{0,16},{8,24},{16,0},{24,8},{1,17},{9,25},{17,1},{25,9},{2,18},{10... | collective-permute-start | bytes 1572872 | tf_op jit(solution)/shard_map/ppermute | solution.py:46
  (90 other events, 704.3 us)
Sparse Core Ops, SparseCore 0:
  10.7 28.0 all-gather.2
  88.3 52.5 all-gather.4
  342.2 48.3 reduce-scatter.6
  392.8 61.7 reduce-scatter.4
